TPU v7x, 256 devices: a whole 4x4x8 slice. The times are simulated.
256 devices in a mesh: pair: 8 (over y, core), vv: 32 (over x, z).
Axes of the slice: x: 4, y: 4, z: 8, core: 2. Of those that a mesh axis runs over, the one named last changes fastest.
Arguments:
- amplitudes: bfloat16 [1024, 196608], P('pair', 'vv'), may hold values from -6 to 6
- integrals: bfloat16 [96, 32, 24, 128, 128], P('pair', 'vv'), may hold values from -0.01953125 to 0.01953125
- cd_tiles: int32 [96, 32, 24], P('pair', 'vv'), may hold values from 0 to 47
Outputs:
- residual: float32 [1024, 12288], P('vv', 'pair')
Inputs may be any that keep to these rules, and one draw needn't show every extreme that they name: cd_tiles counts tiles within the 48 tiles of one index of vv; a tile may appear in several slots of one row tile.
All inputs are finite; a program needn't handle non-finite values.
Results may differ from a plain program's by a relative error of at most 0.0003.
Values may be sent and summed in bfloat16 or wider, within the bound.
No kernel may reach another device: no remote copies, remote signals or barrier semaphores. Data moves between devices by JAX's collectives and lax.ppermute only.
A program may use at most 192 MiB of HBM per device.

v0:
```python
import jax
import jax.numpy as jnp
from jax import lax
from jax.sharding import PartitionSpec as P


def contract(block_rows, integrals, cd_tiles):
    height = block_rows.shape[0]
    ab_count = integrals.shape[0]
    slot_count = integrals.shape[2]
    tile_width = integrals.shape[3]
    tiled = block_rows.reshape(height, -1, tile_width)
    picked = jnp.take(tiled, cd_tiles.reshape(-1), axis=1)
    picked = picked.reshape(height, ab_count, slot_count, tile_width)
    weights = integrals.reshape(ab_count, slot_count, tile_width, tile_width)
    summed = jnp.einsum("nakc,akdc->nad", picked, weights, preferred_element_type=jnp.float32)
    return summed.reshape(height, ab_count * tile_width)


def per_device(amplitudes, integrals, cd_tiles):
    partial_sum = contract(
        lax.all_gather(amplitudes, "pair", axis=0, tiled=True), integrals, cd_tiles
    )
    return lax.psum_scatter(partial_sum, "vv", scatter_dimension=0, tiled=True)


def solution(mesh):
    return jax.shard_map(
        per_device,
        mesh=mesh,
        in_specs=(P("pair", "vv"), P("pair", "vv", None, None, None), P("pair", "vv", None)),
        out_specs=P("vv", "pair"),
        check_vma=False,
    )
```

profile of v0, /device:TPU:8, one launch (start us, length us, event | category | flops | bytes accessed | tf_op | source)
XLA Modules:
  0.0 407.3 jit_solution(2435041436776009870)
XLA Ops:
  6.5 0.0 all-gather.2.cloned.1.call-start
  6.5 2.6 copy.7
  9.1 0.0 all-gather.2.cloned.1.call-update
  9.2 0.0 reduce-scatter.2.cloned.1.call-start
  9.2 0.7 reduce
  9.9 0.1 reshape.54
  10.1 0.7 compare_and_fusion
  10.8 76.1 %all-gather.2.cloned.1.call-done = bf16[1024,6144]{0,1:T(8,128)(2,1)} async-done(((bf16[128,6144]{0,1:T(8,128)(2,1)}), bf16[1024,6144]{0,1:T(8,128)(2,1)}) %all-gather.2.cloned.1.call-update) | async-done | bytes 12582928 | tf_op jit(solution)/shard_map/all_gather | solution.py:22
  86.9 16.5 %copy.8 = bf16[1024,48,128]{2,0,1:T(8,128)(2,1)} copy(bf16[1024,48,128]{0,2,1:T(8,128)(2,1)} %bitcast.17) | data formatting | bytes 25165824 | tf_op jit(solution)/shard_map/reshape | solution.py:12
  103.4 30.6 %gather_fusion = bf16[288,1024,128]{2,1,0:T(8,128)(2,1)} fusion(bf16[1024,48,128]{2,0,1:T(8,128)(2,1)} %copy.8, s32[1024]{0:T(1024)S(1)} %pad_clamp_fusion), kind=kCustom, calls=%fused_computation | custom fusion | bytes 150996096 | tf_op jit(solution)/shard_map/jit(_take)/gather | solution.py:13
  134.0 35.1 %fusion = f32[12,1024,128,1]{1,2,3,0:T(8,128)} fusion(bf16[1024,12,24,128]{3,0,2,1:T(8,128)(2,1)} %bitcast.2, pred[12,24]{1,0:T(8,128)(4,1)S(1)} %compare_and_fusion, bf16[12,1,24,128,128]{4,3,2,1,0:T(8,128)(2,1)} %param.4), kind=kOutput, calls=%fused_computation.1 | convolution fusion | flops 9701425152 | bytes 91226400 | tf_op jit(solution)/shard_map/nakc,akdc->nad/dot_general | solution.py:16
  169.1 6.6 %copy.9 = f32[1024,1536]{1,0:T(8,128)} copy(f32[1024,1536]{0,1:T(8,128)} %bitcast.18) | data formatting | bytes 12582912 | tf_op jit(solution)/shard_map/reshape | solution.py:17
  175.7 0.0 reduce-scatter.2.cloned.1.call-update
  175.7 224.8 %reduce-scatter.2.cloned.1.call-done = f32[32,1536]{1,0:T(8,128)} async-done(((f32[1024,1536]{1,0:T(8,128)}), f32[32,1536]{1,0:T(8,128)}) %reduce-scatter.2.cloned.1.call-update) | async-done | bytes 196624 | tf_op jit(solution)/shard_map/reduce_scatter | solution.py:24
  (2 shorter events, 0.0 us)
Async XLA Ops:
  6.5 80.3 %all-gather.2.cloned.1.call-start = ((), (), s32[]{:S(2)}) async-start(), calls=%async_computation.1 | async-start | bytes 14155776 | tf_op jit(solution)/shard_map/all_gather | solution.py:22
  9.2 391.3 %reduce-scatter.2.cloned.1.call-start = ((), (), s32[]{:S(2)}) async-start(), calls=%async_computation.2 | async-start | bytes 6488064 | tf_op jit(solution)/shard_map/reduce_scatter | solution.py:24
Sparse Core Ops, SparseCore 0:
  9.3 77.5 all-gather.1
  175.8 224.6 reduce-scatter.1
where the time goes:
time: 408 us; the launch traced here: 407 us
  waiting for transfers between devices  301 us (74%)
  local copies, waits for them, and re-layouts  56.4 us (14%)
  matrix products  35.1 us (9%)
  between operations  13.4 us (3%)
    reduce_scatter x1, waiting for transfers between devices, per_device(): return lax.psum_scatter(partial_sum, 'vv', scatter_dimension=0, tiled=True)  225 us
    all_gather x1, waiting for transfers between devices, per_device(): lax.all_gather(amplitudes, 'pair', axis=0, tiled=True)  76.1 us
    dot_general x1, matrix products, contract(): jnp.einsum('nakc,akdc->nad', picked, weights, preferred_element_type=jnp....  35.1 us
    gather x1, local copies, waits for them, and re-layouts, contract(): picked = jnp.take(tiled, cd_tiles.reshape(-1), axis=1)  30.6 us
    reshape x1, local copies, waits for them, and re-layouts, contract(): tiled = block_rows.reshape(height, -1, tile_width)  16.5 us
  transfers between devices with their start and end apart: 2, of which 2 were waited for; matrix products, arithmetic and copies ran while one was open for 0% of the time, Pallas kernels for 0%

commit v1 on v0

v1 whole, which is shorter than its diff:
```python
import jax
import jax.numpy as jnp
from jax import lax
from jax.experimental import pallas as pl
from jax.experimental.pallas import tpu as pltpu
from jax.sharding import Mesh, PartitionSpec as P

NY, NC, NX, NZ = 4, 2, 4, 8
TILE = 128
ROWS = 32
QW = NY
CHUNKS = ((0, 32),)
LEVELS = 32767.0


def shift(value, axis, size, step):
    return lax.ppermute(value, axis, [(i, (i + step) % size) for i in range(size)])


def encode(total):
    top = jnp.maximum(jnp.max(jnp.abs(total), axis=1, keepdims=True), 1e-30)
    code = jnp.ceil(jnp.log2(top) * 256.0) + 1.0
    scaled = total * (jnp.exp2(code * (-1.0 / 256.0)) * LEVELS)
    return jnp.round(scaled).astype(jnp.int32).astype(jnp.int16), code


def scales(codes):
    return jnp.exp2(codes.astype(jnp.int32).astype(jnp.float32) * (1.0 / 256.0)) * (1.0 / LEVELS)


def contract(pos, cd_tiles, integrals, blocks, height, partial=None):
    n_tiles, n_slots = integrals.shape[0], integrals.shape[1]
    width = n_tiles * TILE
    depth = blocks[0][0].shape[1]
    rows = sum(b[2] for b in blocks)
    step = rows if rows <= 512 else rows // 2
    arrays = []
    for b in blocks:
        if not any(b[0] is a for a in arrays):
            arrays.append(b[0])
    n_arr, n_blk = len(arrays), len(blocks)
    where = [next(i for i, a in enumerate(arrays) if a is b[0]) for b in blocks]
    n_in = 0 if partial is None else 4

    def body(*refs):
        pos_ref, cd_ref = refs[:2]
        w_hbm = refs[2]
        a_hbm = refs[3 : 3 + n_arr]
        outs = refs[3 + n_arr + n_in : 7 + n_arr + n_in]
        wv, av, ov, codes, wsem, asem, osem = refs[7 + n_arr + n_in :]
        starts = []
        at = 0
        for i, b in enumerate(blocks):
            starts.append(at)
            pltpu.make_async_copy(
                a_hbm[where[i]].at[pl.ds(b[1], b[2]), :], av.at[pl.ds(at, b[2]), :], asem.at[i]
            ).start()
            at += b[2]
        for t in range(n_tiles):
            pltpu.make_async_copy(w_hbm.at[t], wv.at[t], wsem.at[t]).start()
        for i, b in enumerate(blocks):
            pltpu.make_async_copy(
                a_hbm[where[i]].at[pl.ds(b[1], b[2]), :], av.at[pl.ds(starts[i], b[2]), :], asem.at[i]
            ).wait()
        codes[...] = jnp.zeros_like(codes)

        def one_tile(t, carry):
            pltpu.make_async_copy(w_hbm.at[t], wv.at[t], wsem.at[t]).wait()
            weights = jnp.concatenate([wv[t, k] for k in range(n_slots)], axis=1)
            for r in range(0, rows, step):
                picked = jnp.concatenate(
                    [
                        av[pl.ds(r, step), pl.ds(pl.multiple_of(cd_ref[t, k] * TILE, TILE), TILE)]
                        for k in range(n_slots)
                    ],
                    axis=1,
                )
                total = lax.dot_general(
                    picked, weights, (((1,), (1,)), ((), ())), preferred_element_type=jnp.float32
                )
                value, code = encode(total)
                ov[pl.ds(r, step), pl.ds(pl.multiple_of(t * TILE, TILE), TILE)] = value
                lane = lax.broadcasted_iota(jnp.int32, (step, TILE), 1)
                codes[pl.ds(r, step), :] = jnp.where(lane == t, code, codes[pl.ds(r, step), :])
            return carry

        lax.fori_loop(0, n_tiles, one_tile, 0)
        ov[:, width:] = codes[...].astype(jnp.int32).astype(jnp.int16)
        y, c, x = pos_ref[0], pos_ref[1], pos_ref[2]
        for i, b in enumerate(blocks):
            slot = (y + b[3] - x + NX) % NX
            first = pl.multiple_of(((c + b[4]) % NC) * (QW * height) + b[5], 8)
            for s in range(NX):

                @pl.when(slot == s)
                def _():
                    pltpu.make_async_copy(
                        ov.at[pl.ds(starts[i], b[2]), :], outs[s].at[pl.ds(first, b[2]), :], osem.at[i]
                    ).start()

        for i, b in enumerate(blocks):
            pltpu.make_async_copy(
                ov.at[pl.ds(starts[i], b[2]), :], outs[0].at[pl.ds(0, b[2]), :], osem.at[i]
            ).wait()

    any_spec = pl.BlockSpec(memory_space=pl.ANY)
    full = jax.ShapeDtypeStruct((NC * QW * height, width + TILE), jnp.int16)
    return pl.pallas_call(
        body,
        out_shape=[full] * 4,
        grid_spec=pltpu.PrefetchScalarGridSpec(
            num_scalar_prefetch=2,
            grid=(1,),
            in_specs=[any_spec] * (1 + n_arr + n_in),
            out_specs=[any_spec] * 4,
            scratch_shapes=[
                pltpu.VMEM(integrals.shape, integrals.dtype),
                pltpu.VMEM((rows, depth), blocks[0][0].dtype),
                pltpu.VMEM((rows, width + TILE), jnp.int16),
                pltpu.VMEM((rows, TILE), jnp.float32),
                pltpu.SemaphoreType.DMA((n_tiles,)),
                pltpu.SemaphoreType.DMA((n_blk,)),
                pltpu.SemaphoreType.DMA((n_blk,)),
            ],
        ),
        input_output_aliases={} if partial is None else {3 + n_arr + s: s for s in range(4)},
        compiler_params=pltpu.CompilerParams(vmem_limit_bytes=48 << 20),
        cost_estimate=pl.CostEstimate(
            flops=4 * rows * n_slots * TILE * width,
            transcendentals=0,
            bytes_accessed=integrals.size * 2 + rows * depth * 2 + rows * width * 2,
        ),
    )(pos, cd_tiles, integrals, *arrays, *(partial or ()))


def add_and_encode(parts, heights):
    wide = parts[0][0].shape[1]
    n_tiles = wide // TILE - 1
    flat = [q for four in parts for q in four]

    def body(*refs):
        out = refs[-1]
        row = 0
        for i, h in enumerate(heights):
            four = refs[4 * i : 4 * i + 4]
            scale = [scales(q[:, n_tiles * TILE :]) for q in four]
            lane = lax.broadcasted_iota(jnp.int32, (h, TILE), 1)
            codes = jnp.zeros((h, TILE), jnp.float32)
            for t in range(n_tiles):
                total = None
                for q, s in zip(four, scale):
                    term = q[:, t * TILE : (t + 1) * TILE].astype(jnp.int32).astype(jnp.float32) * s[:, t : t + 1]
                    total = term if total is None else total + term
                value, code = encode(total)
                out[0, row : row + h, t * TILE : (t + 1) * TILE] = value
                codes = jnp.where(lane == t, code, codes)
            out[0, row : row + h, n_tiles * TILE :] = codes.astype(jnp.int32).astype(jnp.int16)
            row += h

    return pl.pallas_call(
        body,
        out_shape=jax.ShapeDtypeStruct((NZ, sum(heights), wide), jnp.int16),
        grid=(NZ,),
        in_specs=[pl.BlockSpec((h, wide), lambda z: (z, 0)) for h in heights for _ in range(4)],
        out_specs=pl.BlockSpec((1, sum(heights), wide), lambda z: (z, 0, 0)),
    )(*flat)


def add_last(arrived):
    n, rows, wide = arrived.shape
    n_tiles = wide // TILE - 1

    def body(q, out):
        scale = [scales(q[i, :, n_tiles * TILE :]) for i in range(n)]
        for t in range(n_tiles):
            total = None
            for i in range(n):
                term = q[i, :, t * TILE : (t + 1) * TILE].astype(jnp.int32).astype(jnp.float32) * scale[i][:, t : t + 1]
                total = term if total is None else total + term
            out[:, t * TILE : (t + 1) * TILE] = total

    return pl.pallas_call(
        body,
        out_shape=jax.ShapeDtypeStruct((rows, n_tiles * TILE), jnp.float32),
    )(arrived)


def per_device(amplitudes, integrals, cd_tiles):
    integrals = integrals[:, 0]
    cd_tiles = cd_tiles[:, 0]
    depth = amplitudes.shape[1]
    pos = jnp.stack([lax.axis_index("y"), lax.axis_index("c"), lax.axis_index("x")]).astype(jnp.int32)
    other = shift(amplitudes, "c", NC, 1)
    arrived = []
    for first, h in CHUNKS:
        half = QW * h // 2
        if h == ROWS:
            own = amplitudes
        else:
            own = amplitudes.reshape(QW, ROWS, depth)[:, first : first + h].reshape(QW * h, depth)
        up = shift(own, "y", NY, 1)
        down = shift(own, "y", NY, -1)
        far_lo = shift(up[:half], "y", NY, 1)
        far_hi = shift(down[half:], "y", NY, -1)
        up_o, down_o = shift(up, "c", NC, 1), shift(down, "c", NC, 1)
        lo_o, hi_o = shift(far_lo, "c", NC, 1), shift(far_hi, "c", NC, 1)
        early = []
        for source, core in ((amplitudes, 0), (other, 1)):
            for q in range(QW):
                early.append((source, q * ROWS + first, h, 0, core, q * h))
        for up_b, down_b, core in ((up, down, 0), (up_o, down_o, 1)):
            early.append((up_b, 0, QW * h, -1, core, 0))
            early.append((down_b, 0, QW * h, 1, core, 0))
        late = []
        for lo_b, hi_b, core in ((far_lo, far_hi, 0), (lo_o, hi_o, 1)):
            late.append((lo_b, 0, half, 2, core, 0))
            late.append((hi_b, 0, half, 2, core, half))
        coded = contract(pos, cd_tiles, integrals, early, h)
        coded = contract(pos, cd_tiles, integrals, late, h, coded)
        arrived.append([coded[0]] + [shift(coded[s], "x", NX, s) for s in (1, 2, 3)])
    summed = add_and_encode(arrived, [h for _, h in CHUNKS])
    return add_last(lax.all_to_all(summed, "z", 0, 0, tiled=True))


def solution(mesh):
    fine = Mesh(mesh.devices.reshape(NY, NC, NX, NZ), ("y", "c", "x", "z"))
    return jax.shard_map(
        per_device,
        mesh=fine,
        in_specs=(P(("y", "c"), ("x", "z")), P(("y", "c"), ("x", "z")), P(("y", "c"), ("x", "z"))),
        out_specs=P(("x", "z"), ("y", "c")),
        check_vma=False,
    )
```

time: 408 us -> 194 us (0.48)
  waiting for transfers between devices: 301 us -> 90.7 us
  Pallas kernels: 0 us -> 53.5 us
  local copies, waits for them, and re-layouts: 56.4 us -> 6.32 us
  matrix products: 35.1 us -> 0 us
  blocking collectives: 0 us -> 33 us
  between operations: 13.4 us -> 0.08 us
  starting transfers between devices: 0.04 us -> 9.55 us
    reduce_scatter x1 -> x0, waiting for transfers between devices: 225 us -> none  [per_device(): return lax.psum_scatter(partial_sum, 'vv', scatter_dimension=0, tiled=True)]
    ppermute x0 -> x12, waiting for transfers between devices: none -> 90.7 us  [shift(): lax.ppermute(value, axis, [(i, (i + step) % size) for i in range(size)])]
    all_gather x1 -> x0, waiting for transfers between devices: 76.1 us -> none  [per_device(): lax.all_gather(amplitudes, 'pair', axis=0, tiled=True)]
    pallas_call x0 -> x4, Pallas kernels: none -> 53.5 us  [the longest x2 40.1 us: contract(): pl.pallas_call(body, out_shape=[full] * 4, grid_spec=pltpu.PrefetchScalar...]
    dot_general x1 -> x0, matrix products: 35.1 us -> none  [contract(): jnp.einsum('nakc,akdc->nad', picked, weights, preferred_element_type=jnp....]
    all_to_all x0 -> x1, blocking collectives: none -> 33 us  [per_device(): return add_last(lax.all_to_all(summed, 'z', 0, 0, tiled=True))]
    gather x1 -> x0, local copies, waits for them, and re-layouts: 30.6 us -> none  [contract(): picked = jnp.take(tiled, cd_tiles.reshape(-1), axis=1)]
    reshape x3 -> x0, local copies, waits for them, and re-layouts: 23.2 us -> none  [the longest x1 16.5 us: contract(): tiled = block_rows.reshape(height, -1, tile_width)]
  transfers between devices with their start and end apart: 2 -> 12, of which waited for: 2 -> 6; matrix products, arithmetic and copies ran while one was open for 0% -> 2% of each run, Pallas kernels for 0% -> 15%
where the time goes in v1:
time: 194 us; the launch traced here: 193 us
  waiting for transfers between devices  90.7 us (47%)
  Pallas kernels  53.5 us (28%)
  blocking collectives  33 us (17%)
  starting transfers between devices  9.55 us (5%)
  local copies, waits for them, and re-layouts  6.32 us (3%)
    ppermute x12, waiting for transfers between devices, shift(): lax.ppermute(value, axis, [(i, (i + step) % size) for i in range(size)])  90.7 us
    pallas_call x2, Pallas kernels, contract(): pl.pallas_call(body, out_shape=[full] * 4, grid_spec=pltpu.PrefetchScalar...  40.1 us
    all_to_all x1, blocking collectives, per_device(): return add_last(lax.all_to_all(summed, 'z', 0, 0, tiled=True))  33 us
    pallas_call x1, Pallas kernels, add_and_encode(): pl.pallas_call(body, out_shape=jax.ShapeDtypeStruct((NZ, sum(heights), wi...  11.1 us
    ppermute x12, starting transfers between devices, shift(): lax.ppermute(value, axis, [(i, (i + step) % size) for i in range(size)])  9.55 us
  transfers between devices with their start and end apart: 12, of which 6 were waited for; matrix products, arithmetic and copies ran while one was open for 2% of the time, Pallas kernels for 15%

profile of v1, /device:TPU:8, one launch (start us, length us, event | category | flops | bytes accessed | tf_op | source)
XLA Modules:
  0.0 193.2 jit_solution(3977575361055681733)
XLA Ops:
  0.0 0.0 copy-start.1
  0.0 0.0 copy-start.6
  0.0 1.6 collective-permute-start
  1.6 0.6 collective-permute-start.2
  2.2 0.0 collective-permute-start.6
  2.2 34.3 %collective-permute-done.refs_5_ = bf16[128,6144]{1,0:T(8,128)(2,1)} collective-permute-done((bf16[128,6144]{1,0:T(8,128)(2,1)}, bf16[128,6144]{1,0:T(8,128)(2,1)}, u32[]{:S(2)}, u32[]{:S(2)}) %collective-permute-start) | collective-permute-done | bytes 1572896 | tf_op jit(solution)/shard_map/ppermute | solution.py:17
  36.5 0.0 collective-permute-start.7
  36.5 1.3 collective-permute-done.2.refs_6_
  37.8 0.0 collective-permute-start.8
  37.8 2.1 %slice.8 = bf16[64,6144]{1,0:T(8,128)(2,1)} slice(bf16[128,6144]{1,0:T(8,128)(2,1)} %collective-permute-done.refs_5_), slice={[0:64], [0:6144]} | slice | bytes 1572864 | tf_op jit(solution)/shard_map/slice | solution.py:203
  39.9 1.3 collective-permute-start.1
  41.2 1.2 slice.9
  42.4 0.8 collective-permute-start.3
  43.2 0.0 copy-done.6
  43.2 0.1 pad_add_fusion.refs_0_
  43.3 16.8 %collective-permute-done.1.refs_3_ = bf16[64,6144]{1,0:T(8,128)(2,1)S(1)} collective-permute-done((bf16[64,6144]{1,0:T(8,128)(2,1)}, bf16[64,6144]{1,0:T(8,128)(2,1)S(1)}, u32[]{:S(2)}, u32[]{:S(2)}) %collective-permute-start.1) | collective-permute-done | bytes 786464 | tf_op jit(solution)/shard_map/ppermute | solution.py:17
  60.0 0.0 collective-permute-start.4
  60.0 2.2 %collective-permute-done.3.refs_4_ = bf16[64,6144]{1,0:T(8,128)(2,1)} collective-permute-done((bf16[64,6144]{1,0:T(8,128)(2,1)S(1)}, bf16[64,6144]{1,0:T(8,128)(2,1)}, u32[]{:S(2)}, u32[]{:S(2)}) %collective-permute-start.3) | collective-permute-done | bytes 786464 | tf_op jit(solution)/shard_map/ppermute | solution.py:17
  62.2 0.0 collective-permute-start.5
  62.2 0.0 collective-permute-done.6.refs_4_
  62.2 0.0 collective-permute-done.7.refs_7_
  62.2 0.0 collective-permute-done.8.refs_8_
  62.2 0.0 copy-done.1
  62.2 28.6 %shard_map.37 = (s16[256,1664]{1,0:T(8,128)(2,1)S(1)}, s16[256,1664]{1,0:T(8,128)(2,1)S(1)}, s16[256,1664]{1,0:T(8,128)(2,1)S(1)}, s16[256,1664]{1,0:T(8,128)(2,1)S(1)}) custom-call(s32[3]{0:T(128)S(1)} %pad_add_fusion.refs_0_, s32[12,24]{1,0:T(8,128)S(1)} %bitcast.7, bf16[12,24,128,128]{3,2,1,0:T(8,128)(2,1)} %bitcast.9, bf16[128,6144]{1,0:T(8,128)(2,1)S(1)} %copy-done.1, ...), custom_call_target="tpu_custom_call" | custom-call | flops 14495514624 | bytes 21233664 | tf_op jit(solution)/shard_map/pallas_call | solution.py:108
  90.8 0.0 copy-start.2
  90.8 0.9 copy-done.2
  91.8 0.0 collective-permute-done.4.refs_5_
  91.8 0.0 collective-permute-done.5.refs_6_
  91.8 11.6 %shard_map.38 = (s16[256,1664]{1,0:T(8,128)(2,1)S(1)}, s16[256,1664]{1,0:T(8,128)(2,1)S(1)}, s16[256,1664]{1,0:T(8,128)(2,1)S(1)}, s16[256,1664]{1,0:T(8,128)(2,1)}) custom-call(s32[3]{0:T(128)S(1)} %pad_add_fusion.refs_0_, s32[12,24]{1,0:T(8,128)S(1)} %bitcast.8, ...), custom_call_target="tpu_custom_call", output_to_operand_aliasing={{0}: (7, {}), {1}: (8, {}), {2}: (9, {}), {3}: (10, {})} | custom-call | flops 4831838208 | bytes 13369344 | tf_op jit(solution)/shard_map/pallas_call | solution.py:108
  103.4 0.0 copy-start
  103.4 0.9 copy-done
  104.3 3.2 %collective-permute-start.10 = (s16[256,1664]{1,0:T(8,128)(2,1)S(1)}, s16[256,1664]{1,0:T(8,128)(2,1)S(1)}, u32[]{:S(2)}, u32[]{:S(2)}) collective-permute-start(s16[256,1664]{1,0:T(8,128)(2,1)S(1)} %get-tuple-element.19), channel_id=1, source_target_pairs={{0,16},{8,24},{16,0},{24,8},{1,17},{9,25},{17,1},{25,9},{2,18},{10... | collective-permute-start | bytes 2555912 | tf_op jit(solution)/shard_map/ppermute | solution.py:17
  107.5 1.2 collective-permute-start.11
  108.6 0.9 collective-permute-start.9
  109.5 18.0 %collective-permute-done.10.refs_2_ = s16[256,1664]{1,0:T(8,128)(2,1)S(1)} collective-permute-done((s16[256,1664]{1,0:T(8,128)(2,1)S(1)}, s16[256,1664]{1,0:T(8,128)(2,1)S(1)}, u32[]{:S(2)}, u32[]{:S(2)}) %collective-permute-start.10) | collective-permute-done | bytes 852000 | tf_op jit(solution)/shard_map/ppermute | solution.py:17
  127.5 0.0 copy-start.3
  127.5 18.1 %collective-permute-done.11.refs_3_ = s16[256,1664]{1,0:T(8,128)(2,1)S(1)} collective-permute-done((s16[256,1664]{1,0:T(8,128)(2,1)}, s16[256,1664]{1,0:T(8,128)(2,1)S(1)}, u32[]{:S(2)}, u32[]{:S(2)}) %collective-permute-start.11) | collective-permute-done | bytes 852000 | tf_op jit(solution)/shard_map/ppermute | solution.py:17
  145.7 0.0 copy-start.4
  145.7 0.0 collective-permute-done.9.refs_1_
  145.7 0.0 copy-start.5
  145.7 0.0 copy-done.3
  145.7 0.9 copy-done.4
  146.6 0.3 copy-done.5
  146.9 11.1 %shard_map.39 = s16[8,32,1664]{2,1,0:T(8,128)(2,1)} custom-call(s16[256,1664]{1,0:T(8,128)(2,1)} %copy-done, s16[256,1664]{1,0:T(8,128)(2,1)} %copy-done.5, s16[256,1664]{1,0:T(8,128)(2,1)} %copy-done.3, s16[256,1664]{1,0:T(8,128)(2,1)} %copy-done.4), custom_call_target="tpu_custom_call" | custom-call | tf_op jit(solution)/shard_map/pallas_call | solution.py:160
  157.9 33.0 %all_to_all.5.q = s16[8,32,1664]{2,1,0:T(8,128)(2,1)} all-to-all(s16[8,32,1664]{2,1,0:T(8,128)(2,1)} %shard_map.39), channel_id=1, replica_groups=mesh['y'=4,'c'=2,'x'=4,'z'=8] {'z'}, dimensions={0} | all-to-all | bytes 1703936 | tf_op jit(solution)/shard_map/all_to_all | solution.py:222
  190.9 2.3 %shard_map.40 = f32[32,1536]{1,0:T(8,128)} custom-call(s16[8,32,1664]{2,1,0:T(8,128)(2,1)} %all_to_all.5.q), custom_call_target="tpu_custom_call" | custom-call | tf_op jit(solution)/shard_map/pallas_call | solution.py:182
  (1 shorter events, 0.0 us)
Async XLA Ops:
  0.0 62.2 %copy-start.1 = (bf16[128,6144]{1,0:T(8,128)(2,1)S(1)}, bf16[128,6144]{1,0:T(8,128)(2,1)}, u32[]{:S(2)}) copy-start(bf16[128,6144]{1,0:T(8,128)(2,1)} %refs_3_.1) | copy-start | bytes 4718596
  0.0 43.2 %copy-start.6 = (s32[12,1,24]{2,1,0:T(1,128)S(1)}, s32[12,1,24]{2,1,0:T(1,128)}, u32[]{:S(2)}) copy-start(s32[12,1,24]{2,1,0:T(1,128)} %param.5) | copy-start | bytes 3460
  0.0 36.5 %collective-permute-start = (bf16[128,6144]{1,0:T(8,128)(2,1)}, bf16[128,6144]{1,0:T(8,128)(2,1)}, u32[]{:S(2)}, u32[]{:S(2)}) collective-permute-start(bf16[128,6144]{1,0:T(8,128)(2,1)} %refs_3_.1), channel_id=1, source_target_pairs={{0,64},{64,128},{128,192},{192,0},{1,65},{65,129},{129,193},{193,1... | collective-permute-start | bytes 4718600 | tf_op jit(solution)/shard_map/ppermute | solution.py:17
  1.6 36.2 %collective-permute-start.2 = (bf16[128,6144]{1,0:T(8,128)(2,1)}, bf16[128,6144]{1,0:T(8,128)(2,1)}, u32[]{:S(2)}, u32[]{:S(2)}) collective-permute-start(bf16[128,6144]{1,0:T(8,128)(2,1)} %refs_3_.1), channel_id=1, source_target_pairs={{0,192},{64,0},{128,64},{192,128},{1,193},{65,1},{129,65},{193,129... | collective-permute-start | bytes 4718600 | tf_op jit(solution)/shard_map/ppermute | solution.py:17
  2.2 60.0 %collective-permute-start.6 = (bf16[128,6144]{1,0:T(8,128)(2,1)}, bf16[128,6144]{1,0:T(8,128)(2,1)}, u32[]{:S(2)}, u32[]{:S(2)}) collective-permute-start(bf16[128,6144]{1,0:T(8,128)(2,1)} %refs_3_.1), channel_id=1, source_target_pairs={{0,32},{32,0},{1,33},{33,1},{2,34},{34,2},{3,35},{35,3},{4,36},{36... | collective-permute-start | bytes 4718600 | tf_op jit(solution)/shard_map/ppermute | solution.py:17
  36.5 25.8 %collective-permute-start.7 = (bf16[128,6144]{1,0:T(8,128)(2,1)}, bf16[128,6144]{1,0:T(8,128)(2,1)}, u32[]{:S(2)}, u32[]{:S(2)}) collective-permute-start(bf16[128,6144]{1,0:T(8,128)(2,1)} %collective-permute-done.refs_5_), channel_id=1, source_target_pairs={{0,32},{32,0},{1,33},{33,1},{2,34},{34,2},{3,35},{35,3},{4,36},{36... | collective-permute-start | bytes 4718600 | tf_op jit(solution)/shard_map/ppermute | solution.py:17
  37.8 24.5 %collective-permute-start.8 = (bf16[128,6144]{1,0:T(8,128)(2,1)}, bf16[128,6144]{1,0:T(8,128)(2,1)}, u32[]{:S(2)}, u32[]{:S(2)}) collective-permute-start(bf16[128,6144]{1,0:T(8,128)(2,1)} %collective-permute-done.2.refs_6_), channel_id=1, source_target_pairs={{0,32},{32,0},{1,33},{33,1},{2,34},{34,2},{3,35},{35,3},{4,36},{36... | collective-permute-start | bytes 4718600 | tf_op jit(solution)/shard_map/ppermute | solution.py:17
  39.9 20.2 %collective-permute-start.1 = (bf16[64,6144]{1,0:T(8,128)(2,1)}, bf16[64,6144]{1,0:T(8,128)(2,1)S(1)}, u32[]{:S(2)}, u32[]{:S(2)}) collective-permute-start(bf16[64,6144]{1,0:T(8,128)(2,1)} %slice.8), channel_id=1, source_target_pairs={{0,64},{64,128},{128,192},{192,0},{1,65},{65,129},{129,193},{193,1... | collective-permute-start | bytes 2359304 | tf_op jit(solution)/shard_map/ppermute | solution.py:17
  42.4 19.9 %collective-permute-start.3 = (bf16[64,6144]{1,0:T(8,128)(2,1)S(1)}, bf16[64,6144]{1,0:T(8,128)(2,1)}, u32[]{:S(2)}, u32[]{:S(2)}) collective-permute-start(bf16[64,6144]{1,0:T(8,128)(2,1)S(1)} %slice.9), channel_id=1, source_target_pairs={{0,192},{64,0},{128,64},{192,128},{1,193},{65,1},{129,65},{193,129... | collective-permute-start | bytes 2359304 | tf_op jit(solution)/shard_map/ppermute | solution.py:17
  60.0 31.7 %collective-permute-start.4 = (bf16[64,6144]{1,0:T(8,128)(2,1)S(1)}, bf16[64,6144]{1,0:T(8,128)(2,1)S(1)}, u32[]{:S(2)}, u32[]{:S(2)}) collective-permute-start(bf16[64,6144]{1,0:T(8,128)(2,1)S(1)} %collective-permute-done.1.refs_3_), channel_id=1, source_target_pairs={{0,32},{32,0},{1,33},{33,1},{2,34},{34,2},{3,35},{35,3},{4,36},{36... | collective-permute-start | bytes 2359304 | tf_op jit(solution)/shard_map/ppermute | solution.py:17
  62.2 29.6 %collective-permute-start.5 = (bf16[64,6144]{1,0:T(8,128)(2,1)}, bf16[64,6144]{1,0:T(8,128)(2,1)S(1)}, u32[]{:S(2)}, u32[]{:S(2)}) collective-permute-start(bf16[64,6144]{1,0:T(8,128)(2,1)} %collective-permute-done.3.refs_4_), channel_id=1, source_target_pairs={{0,32},{32,0},{1,33},{33,1},{2,34},{34,2},{3,35},{35,3},{4,36},{36... | collective-permute-start | bytes 2359304 | tf_op jit(solution)/shard_map/ppermute | solution.py:17
  90.8 0.9 copy-start.2
  103.4 0.9 copy-start
  104.3 23.3 %collective-permute-start.10 = (s16[256,1664]{1,0:T(8,128)(2,1)S(1)}, s16[256,1664]{1,0:T(8,128)(2,1)S(1)}, u32[]{:S(2)}, u32[]{:S(2)}) collective-permute-start(s16[256,1664]{1,0:T(8,128)(2,1)S(1)} %get-tuple-element.19), channel_id=1, source_target_pairs={{0,16},{8,24},{16,0},{24,8},{1,17},{9,25},{17,1},{25,9},{2,18},{10... | collective-permute-start | bytes 2555912 | tf_op jit(solution)/shard_map/ppermute | solution.py:17
  107.5 38.2 %collective-permute-start.11 = (s16[256,1664]{1,0:T(8,128)(2,1)}, s16[256,1664]{1,0:T(8,128)(2,1)S(1)}, u32[]{:S(2)}, u32[]{:S(2)}) collective-permute-start(s16[256,1664]{1,0:T(8,128)(2,1)} %get-tuple-element.20), channel_id=1, source_target_pairs={{0,24},{8,0},{16,8},{24,16},{1,25},{9,1},{17,9},{25,17},{2,26},{10... | collective-permute-start | bytes 2555912 | tf_op jit(solution)/shard_map/ppermute | solution.py:17
  108.6 37.0 %collective-permute-start.9 = (s16[256,1664]{1,0:T(8,128)(2,1)S(1)}, s16[256,1664]{1,0:T(8,128)(2,1)S(1)}, u32[]{:S(2)}, u32[]{:S(2)}) collective-permute-start(s16[256,1664]{1,0:T(8,128)(2,1)S(1)} %get-tuple-element.18), channel_id=1, source_target_pairs={{0,8},{8,16},{16,24},{24,0},{1,9},{9,17},{17,25},{25,1},{2,10},{10... | collective-permute-start | bytes 2555912 | tf_op jit(solution)/shard_map/ppermute | solution.py:17
  127.5 18.2 %copy-start.3 = (s16[256,1664]{1,0:T(8,128)(2,1)}, s16[256,1664]{1,0:T(8,128)(2,1)S(1)}, u32[]{:S(2)}) copy-start(s16[256,1664]{1,0:T(8,128)(2,1)S(1)} %collective-permute-done.10.refs_2_) | copy-start | bytes 2555908
  145.7 0.9 copy-start.4
  145.7 1.2 copy-start.5

commit v2 on v0

v2 whole, which is shorter than its diff:
```python
import jax
import jax.numpy as jnp
from jax import lax
from jax.experimental import pallas as pl
from jax.experimental.pallas import tpu as pltpu
from jax.sharding import Mesh, PartitionSpec as P

NY, NC, NX, NZ = 4, 2, 4, 8
TILE = 128
ROWS = 32
QW = 4
CHUNKS = ((0, 16), (16, 16))
LEVELS = 32767.0


def shift(value, axis, size, step):
    return lax.ppermute(value, axis, [(i, (i + step) % size) for i in range(size)])


def encode(total):
    top = jnp.maximum(jnp.max(jnp.abs(total), axis=1, keepdims=True), 1e-30)
    code = jnp.ceil(jnp.log2(top) * 256.0) + 1.0
    scaled = total * (jnp.exp2(code * (-1.0 / 256.0)) * LEVELS)
    return jnp.round(scaled).astype(jnp.int32).astype(jnp.int16), code


def scales(codes):
    return jnp.exp2(codes.astype(jnp.int32).astype(jnp.float32) * (1.0 / 256.0)) * (1.0 / LEVELS)


def contract(pos, cd_tiles, integrals, blocks, heights, partial=None):
    n_tiles, n_slots = integrals.shape[0], integrals.shape[1]
    width = n_tiles * TILE
    depth = blocks[0][0].shape[1]
    rows = sum(b[2] for b in blocks)
    arrays = []
    for b in blocks:
        if not any(b[0] is a for a in arrays):
            arrays.append(b[0])
    n_arr, n_blk, n_out = len(arrays), len(blocks), 4 * len(heights)
    where = [next(i for i, a in enumerate(arrays) if a is b[0]) for b in blocks]
    starts = [sum(b[2] for b in blocks[:i]) for i in range(n_blk)]
    n_in = 0 if partial is None else n_out

    def body(*refs):
        pos_ref, cd_ref = refs[:2]
        w_hbm = refs[2]
        a_hbm = refs[3 : 3 + n_arr]
        outs = refs[3 + n_arr + n_in : 3 + n_arr + n_in + n_out]
        wv, av, ov, tot, codes, wsem, asem, osem = refs[3 + n_arr + n_in + n_out :]

        def load(i):
            b = blocks[i]
            return pltpu.make_async_copy(
                a_hbm[where[i]].at[pl.ds(b[1], b[2]), :], av.at[pl.ds(starts[i], b[2]), :], asem.at[i]
            )

        def load_weights(t):
            return pltpu.make_async_copy(w_hbm.at[t], wv.at[t], wsem.at[t])

        load_weights(0).start()
        for i in range(n_blk):
            load(i).start()
        for t in range(1, n_tiles):
            load_weights(t).start()
        for i in range(n_blk):
            load(i).wait()
        codes[...] = jnp.zeros_like(codes)
        tot[...] = jnp.zeros_like(tot)
        lane = lax.broadcasted_iota(jnp.int32, (rows, TILE), 1)

        def put(t, column):
            value, code = encode(tot[...])
            ov[:, pl.ds(column, TILE)] = value
            codes[...] = jnp.where(lane == t, code, codes[...])

        def one_tile(t, carry):
            load_weights(t).wait()
            put(t - 1, pl.multiple_of(jnp.maximum(t - 1, 0) * TILE, TILE))
            weights = jnp.concatenate([wv[t, k] for k in range(n_slots)], axis=1)
            picked = jnp.concatenate(
                [av[:, pl.ds(pl.multiple_of(cd_ref[t, k] * TILE, TILE), TILE)] for k in range(n_slots)], axis=1
            )
            tot[...] = lax.dot_general(
                picked, weights, (((1,), (1,)), ((), ())), preferred_element_type=jnp.float32
            )
            return carry

        lax.fori_loop(0, n_tiles, one_tile, 0)
        put(n_tiles - 1, (n_tiles - 1) * TILE)
        ov[:, width:] = codes[...].astype(jnp.int32).astype(jnp.int16)
        y, c, x = pos_ref[0], pos_ref[1], pos_ref[2]
        for i, b in enumerate(blocks):
            slot = (y + b[4] - x + NX) % NX
            first = pl.multiple_of(((c + b[5]) % NC) * (QW * heights[b[3]]) + b[6], 8)
            for s in range(NX):

                @pl.when(slot == s)
                def _():
                    pltpu.make_async_copy(
                        ov.at[pl.ds(starts[i], b[2]), :], outs[4 * b[3] + s].at[pl.ds(first, b[2]), :], osem.at[i]
                    ).start()

        for i, b in enumerate(blocks):
            pltpu.make_async_copy(
                ov.at[pl.ds(starts[i], b[2]), :], outs[4 * b[3]].at[pl.ds(0, b[2]), :], osem.at[i]
            ).wait()

    hbm = pl.BlockSpec(memory_space=pltpu.HBM)
    return pl.pallas_call(
        body,
        out_shape=[
            jax.ShapeDtypeStruct((NC * QW * h, width + TILE), jnp.int16) for h in heights for _ in range(4)
        ],
        grid_spec=pltpu.PrefetchScalarGridSpec(
            num_scalar_prefetch=2,
            grid=(1,),
            in_specs=[hbm] * (1 + n_arr + n_in),
            out_specs=[hbm] * n_out,
            scratch_shapes=[
                pltpu.VMEM(integrals.shape, integrals.dtype),
                pltpu.VMEM((rows, depth), blocks[0][0].dtype),
                pltpu.VMEM((rows, width + TILE), jnp.int16),
                pltpu.VMEM((rows, TILE), jnp.float32),
                pltpu.VMEM((rows, TILE), jnp.float32),
                pltpu.SemaphoreType.DMA((n_tiles,)),
                pltpu.SemaphoreType.DMA((n_blk,)),
                pltpu.SemaphoreType.DMA((n_blk,)),
            ],
        ),
        input_output_aliases={} if partial is None else {3 + n_arr + s: s for s in range(n_out)},
        compiler_params=pltpu.CompilerParams(vmem_limit_bytes=20 << 20),
        cost_estimate=pl.CostEstimate(flops=1, transcendentals=0, bytes_accessed=1),
    )(pos, cd_tiles, integrals, *arrays, *(partial or ()))


def decode(q, scale, tile):
    part = q[:, tile * TILE : (tile + 1) * TILE].astype(jnp.int32).astype(jnp.float32)
    return part * scale[:, tile : tile + 1]


def add_and_encode(pos, parts, h):
    rows, wide = parts[0].shape
    n_tiles = wide // TILE - 1

    def body(pos_ref, *refs):
        four, outs, (scale, codes, res) = refs[:4], refs[4 : 4 + NZ], refs[4 + NZ :]
        lane = lax.broadcasted_iota(jnp.int32, (rows, TILE), 1)
        for i in range(4):
            scale[i] = scales(four[i][:, n_tiles * TILE :])
        codes[...] = jnp.zeros_like(codes)

        def one_tile(t, carry):
            column = pl.ds(pl.multiple_of(t * TILE, TILE), TILE)
            total = None
            for i in range(4):
                factor = jnp.sum(jnp.where(lane == t, scale[i], 0.0), axis=1, keepdims=True)
                part = four[i][:, column].astype(jnp.int32).astype(jnp.float32) * factor
                total = part if total is None else total + part
            value, code = encode(total)
            res[:, column] = value
            codes[...] = jnp.where(lane == t, code, codes[...])
            return carry

        lax.fori_loop(0, n_tiles, one_tile, 0)
        res[:, n_tiles * TILE :] = codes[...].astype(jnp.int32).astype(jnp.int16)
        for s in range(NZ):
            first = pl.multiple_of(((pos_ref[3] + s) % NZ) * h, h)
            outs[s][...] = res[pl.ds(first, h), :]

    vmem = pl.BlockSpec(memory_space=pltpu.VMEM)
    return pl.pallas_call(
        body,
        out_shape=[jax.ShapeDtypeStruct((h, wide), jnp.int16)] * NZ,
        in_specs=[pl.BlockSpec(memory_space=pltpu.SMEM)] + [vmem] * 4,
        out_specs=[vmem] * NZ,
        scratch_shapes=[
            pltpu.VMEM((4, rows, TILE), jnp.float32),
            pltpu.VMEM((rows, TILE), jnp.float32),
            pltpu.VMEM((rows, wide), jnp.int16),
        ],
        compiler_params=pltpu.CompilerParams(vmem_limit_bytes=8 << 20),
    )(pos, *parts)


def add_last(arrived):
    wide = arrived[0][0].shape[1]
    n_tiles = wide // TILE - 1
    heights = [eight[0].shape[0] for eight in arrived]

    def body(*refs):
        out = refs[-1]
        row = 0
        for i, h in enumerate(heights):
            eight = [r[...] for r in refs[NZ * i : NZ * (i + 1)]]
            scale = [scales(q[:, n_tiles * TILE :]) for q in eight]
            for t in range(n_tiles):
                out[row : row + h, t * TILE : (t + 1) * TILE] = sum(decode(q, c, t) for q, c in zip(eight, scale))
            row += h

    return pl.pallas_call(
        body,
        out_shape=jax.ShapeDtypeStruct((sum(heights), n_tiles * TILE), jnp.float32),
        compiler_params=pltpu.CompilerParams(vmem_limit_bytes=8 << 20),
    )(*[q for eight in arrived for q in eight])


def after(values, *others):
    return lax.optimization_barrier((values, others))[0]


def per_device(amplitudes, integrals, cd_tiles):
    integrals = integrals[:, 0]
    cd_tiles = cd_tiles[:, 0]
    depth = amplitudes.shape[1]
    pos = jnp.stack([lax.axis_index(a) for a in ("y", "c", "x", "z")]).astype(jnp.int32)
    heights = [h for _, h in CHUNKS]

    def y_halves(own):
        return shift(own, "y", NY, 1), shift(own, "y", NY, -1)

    def far_halves(up, down):
        half = up.shape[0] // 2
        return shift(up[:half], "y", NY, 1), shift(down[half:], "y", NY, -1)

    def swap(pair):
        return tuple(shift(v, "c", NC, 1) for v in pair)

    def near(i, pair, core):
        up, down = pair
        return [(up, 0, up.shape[0], i, -1, core, 0), (down, 0, down.shape[0], i, 1, core, 0)]

    def far(i, pair, core):
        lo, hi = pair
        return [(lo, 0, lo.shape[0], i, 2, core, 0), (hi, 0, hi.shape[0], i, 2, core, lo.shape[0])]

    parts = [
        amplitudes.reshape(QW, ROWS, depth)[:, first : first + h].reshape(QW * h, depth) for first, h in CHUNKS
    ]
    near_own = [y_halves(parts[0])]
    other = shift(amplitudes, "c", NC, 1)
    blocks = []
    for i, (first, h) in enumerate(CHUNKS):
        for source, core in ((amplitudes, 0), (other, 1)):
            blocks += [(source, q * ROWS + first, h, i, 0, core, q * h) for q in range(QW)]
    coded = contract(pos, cd_tiles, integrals, blocks, heights)
    coded = [coded[4 * i : 4 * i + 4] for i in range(len(CHUNKS))]

    met_x = []
    for i, h in enumerate(heights):
        if i:
            near_own.append(y_halves(after(parts[i], near_other)))
        near_own[i] = after(near_own[i], coded[i])
        far_own = far_halves(*near_own[i])
        near_other = swap(near_own[i])
        blocks = [b for pair, core in ((near_own[i], 0), (near_other, 1)) for b in near(0, pair, core)]
        coded[i] = contract(pos, cd_tiles, integrals, blocks, [h], coded[i])
        far_own = after(far_own, coded[i])
        far_other = swap(far_own)
        if i:
            far_own, met_x[i - 1] = lax.optimization_barrier((far_own, met_x[i - 1]))
        blocks = [b for pair, core in ((far_own, 0), (far_other, 1)) for b in far(0, pair, core)]
        coded[i] = contract(pos, cd_tiles, integrals, blocks, [h], coded[i])
        if i + 1 < len(heights):
            coded[i + 1] = after(coded[i + 1], coded[i])
        met_x.append([coded[i][0]] + [shift(coded[i][s], "x", NX, s) for s in (1, 2, 3)])
    met_z = []
    for i, h in enumerate(heights):
        if i + 1 < len(heights):
            met_x[i] = after(met_x[i], coded[i + 1])
        sums = add_and_encode(pos, met_x[i], h)
        met_z.append([sums[0]] + [shift(sums[s], "z", NZ, s) for s in range(1, NZ)])
    return add_last(met_z)


def solution(mesh):
    fine = Mesh(mesh.devices.reshape(NY, NC, NX, NZ), ("y", "c", "x", "z"))
    return jax.shard_map(
        per_device,
        mesh=fine,
        in_specs=(P(("y", "c"), ("x", "z")), P(("y", "c"), ("x", "z")), P(("y", "c"), ("x", "z"))),
        out_specs=P(("x", "z"), ("y", "c")),
        check_vma=False,
    )
```

time: 408 us -> 145 us (0.36)
  waiting for transfers between devices: 301 us -> 26.7 us
  Pallas kernels: 0 us -> 57.5 us
  starting transfers between devices: 0.04 us -> 53.2 us
  local copies, waits for them, and re-layouts: 56.4 us -> 6.59 us
  matrix products: 35.1 us -> 0 us
  between operations: 13.4 us -> 0.19 us
    reduce_scatter x1 -> x0, waiting for transfers between devices: 225 us -> none  [per_device(): return lax.psum_scatter(partial_sum, 'vv', scatter_dimension=0, tiled=True)]
    all_gather x1 -> x0, waiting for transfers between devices: 76.1 us -> none  [per_device(): lax.all_gather(amplitudes, 'pair', axis=0, tiled=True)]
    pallas_call x0 -> x8, Pallas kernels: none -> 57.5 us  [the longest x5 49 us: contract(): pl.pallas_call(body, out_shape=[jax.ShapeDtypeStruct((NC * QW * h, width...]
    ppermute x0 -> x37, starting transfers between devices: none -> 53.2 us  [shift(): lax.ppermute(value, axis, [(i, (i + step) % size) for i in range(size)])]
    dot_general x1 -> x0, matrix products: 35.1 us -> none  [contract(): jnp.einsum('nakc,akdc->nad', picked, weights, preferred_element_type=jnp....]
    gather x1 -> x0, local copies, waits for them, and re-layouts: 30.6 us -> none  [contract(): picked = jnp.take(tiled, cd_tiles.reshape(-1), axis=1)]
    ppermute x0 -> x37, waiting for transfers between devices: none -> 26.7 us  [shift(): lax.ppermute(value, axis, [(i, (i + step) % size) for i in range(size)])]
    reshape x3 -> x0, local copies, waits for them, and re-layouts: 23.2 us -> none  [the longest x1 16.5 us: contract(): tiled = block_rows.reshape(height, -1, tile_width)]
  transfers between devices with their start and end apart: 2 -> 37, of which waited for: 2 -> 14; matrix products, arithmetic and copies ran while one was open for 0% -> 2% of each run, Pallas kernels for 0% -> 34%
where the time goes in v2:
time: 145 us; the launch traced here: 144 us
  Pallas kernels  57.5 us (40%)
  starting transfers between devices  53.2 us (37%)
  waiting for transfers between devices  26.7 us (18%)
  local copies, waits for them, and re-layouts  6.59 us (5%)
    ppermute x37, starting transfers between devices, shift(): lax.ppermute(value, axis, [(i, (i + step) % size) for i in range(size)])  53.2 us
    pallas_call x5, Pallas kernels, contract(): pl.pallas_call(body, out_shape=[jax.ShapeDtypeStruct((NC * QW * h, width...  49 us
    ppermute x37, waiting for transfers between devices, shift(): lax.ppermute(value, axis, [(i, (i + step) % size) for i in range(size)])  26.7 us
    pallas_call x2, Pallas kernels, add_and_encode(): pl.pallas_call(body, out_shape=[jax.ShapeDtypeStruct((h, wide), jnp.int16...  7.31 us
    unnamed x9, local copies, waits for them, and re-layouts  3.69 us
  transfers between devices with their start and end apart: 37, of which 14 were waited for; matrix products, arithmetic and copies ran while one was open for 2% of the time, Pallas kernels for 34%

profile of v2, /device:TPU:8, one launch (start us, length us, event | category | flops | bytes accessed | tf_op | source)
XLA Modules:
  0.0 144.3 jit_solution(11912933757810862948)
XLA Ops:
  0.0 2.8 %fusion = (bf16[4,16,6144]{2,1,0:T(8,128)(2,1)}, bf16[4,16,6144]{2,1,0:T(8,128)(2,1)}) fusion(bf16[4,32,6144]{2,1,0:T(8,128)(2,1)} %bitcast.16), kind=kLoop, calls=%fused_computation.2 | loop fusion | bytes 3145728 | tf_op jit(solution)/shard_map/slice | solution.py:238
  2.8 1.6 %collective-permute-start = (bf16[64,6144]{1,0:T(8,128)(2,1)}, bf16[64,6144]{1,0:T(8,128)(2,1)S(1)}, u32[]{:S(2)}, u32[]{:S(2)}) collective-permute-start(bf16[64,6144]{1,0:T(8,128)(2,1)} %bitcast.6), channel_id=1, source_target_pairs={{0,64},{64,128},{128,192},{192,0},{1,65},{65,129},{129,193},{193,1... | collective-permute-start | bytes 2359304 | tf_op jit(solution)/shard_map/ppermute | solution.py:17
  4.4 0.6 collective-permute-start.1
  5.1 3.7 %copy-done = bf16[12,1,24,128,128]{4,3,2,1,0:T(8,128)(2,1)S(1)} copy-done((bf16[12,1,24,128,128]{4,3,2,1,0:T(8,128)(2,1)S(1)}, bf16[12,1,24,128,128]{4,3,2,1,0:T(8,128)(2,1)}, u32[]{:S(2)}) %copy-start) | copy-done | bytes 9437208
  8.8 13.1 %shard_map.37 = (s16[128,1664]{1,0:T(8,128)(2,1)S(1)}, s16[128,1664]{1,0:T(8,128)(2,1)S(1)}, s16[128,1664]{1,0:T(8,128)(2,1)S(1)}, s16[128,1664]{1,0:T(8,128)(2,...) custom-call(s32[4]{0:T(128)S(1)} %pad_add_fusion.refs_0_.pos_ref, ...), custom_call_target="tpu_custom_call" | custom-call | flops 1 | bytes 1 | tf_op jit(solution)/shard_map/pallas_call | solution.py:110
  21.8 1.6 %collective-permute-done.refs_3_ = bf16[64,6144]{1,0:T(8,128)(2,1)S(1)} collective-permute-done((bf16[64,6144]{1,0:T(8,128)(2,1)}, bf16[64,6144]{1,0:T(8,128)(2,1)S(1)}, u32[]{:S(2)}, u32[]{:S(2)}) %collective-permute-start) | collective-permute-done | bytes 786464 | tf_op jit(solution)/shard_map/ppermute | solution.py:17
  23.4 0.9 collective-permute-done.1.refs_4_
  24.3 0.5 collective-permute-start.4
  24.8 1.6 %collective-permute-start.7 = (bf16[32,6144]{1,0:T(8,128)(2,1)S(1)}, bf16[32,6144]{1,0:T(8,128)(2,1)S(1)}, u32[]{:S(2)}, u32[]{:S(2)}) collective-permute-start(bf16[32,6144]{1,0:T(8,128)(2,1)S(1)} %slice.20), channel_id=1, source_target_pairs={{0,64},{64,128},{128,192},{192,0},{1,65},{65,129},{129,193},{193,1... | collective-permute-start | bytes 1179656 | tf_op jit(solution)/shard_map/ppermute | solution.py:17
  26.4 0.7 collective-permute-start.8
  27.1 0.6 collective-permute-done.4.refs_6_
  27.7 1.8 %collective-permute-start.5 = (bf16[64,6144]{1,0:T(8,128)(2,1)S(1)}, bf16[64,6144]{1,0:T(8,128)(2,1)S(1)}, u32[]{:S(2)}, u32[]{:S(2)}) collective-permute-start(bf16[64,6144]{1,0:T(8,128)(2,1)S(1)} %bitcast.22), channel_id=1, source_target_pairs={{0,64},{64,128},{128,192},{192,0},{1,65},{65,129},{129,193},{193,1... | collective-permute-start | bytes 2359304 | tf_op jit(solution)/shard_map/ppermute | solution.py:17
  29.5 1.0 collective-permute-start.6
  30.4 10.3 %shard_map.38 = (s16[128,1664]{1,0:T(8,128)(2,1)S(1)}, s16[128,1664]{1,0:T(8,128)(2,1)S(1)}, s16[128,1664]{1,0:T(8,128)(2,1)S(1)}, s16[128,1664]{1,0:T(8,128)(2,1)S(1)}) custom-call(s32[4]{0:T(128)S(1)} %pad_add_fusion.refs_0_.pos_ref, s32[12,24]{1,0:T(8,128)S(1)} %bitcast.18, ...), custom_call_target="tpu_custom_call", output_to_operand_aliasing={{0}: (7, {}), {1}: (8, {}), {2}: (9, {}), {3}: (10, {})} | custom-call | flops 1 | bytes 1 | tf_op jit(solution)/shard_map/pallas_call | solution.py:110
  41.4 1.2 collective-permute-done.10.refs_6_
  42.6 0.6 collective-permute-done.9.refs_5_
  43.1 7.7 %shard_map.39 = (s16[128,1664]{1,0:T(8,128)(2,1)S(1)}, s16[128,1664]{1,0:T(8,128)(2,1)S(1)}, s16[128,1664]{1,0:T(8,128)(2,1)S(1)}, s16[128,1664]{1,0:T(8,128)(2,1)S(1)}) custom-call(s32[4]{0:T(128)S(1)} %pad_add_fusion.refs_0_.pos_ref, s32[12,24]{1,0:T(8,128)S(1)} %bitcast.19, ...), custom_call_target="tpu_custom_call", output_to_operand_aliasing={{0}: (7, {}), {1}: (8, {}), {2}: (9, {}), {3}: (10, {})} | custom-call | flops 1 | bytes 1 | tf_op jit(solution)/shard_map/pallas_call | solution.py:110
  50.8 2.3 %collective-permute-done.5.refs_3_ = bf16[64,6144]{1,0:T(8,128)(2,1)S(1)} collective-permute-done((bf16[64,6144]{1,0:T(8,128)(2,1)S(1)}, bf16[64,6144]{1,0:T(8,128)(2,1)S(1)}, u32[]{:S(2)}, u32[]{:S(2)}) %collective-permute-start.5) | collective-permute-done | bytes 786464 | tf_op jit(solution)/shard_map/ppermute | solution.py:17
  53.2 2.1 %collective-permute-done.6.refs_4_ = bf16[64,6144]{1,0:T(8,128)(2,1)S(1)} collective-permute-done((bf16[64,6144]{1,0:T(8,128)(2,1)S(1)}, bf16[64,6144]{1,0:T(8,128)(2,1)S(1)}, u32[]{:S(2)}, u32[]{:S(2)}) %collective-permute-start.6) | collective-permute-done | bytes 786464 | tf_op jit(solution)/shard_map/ppermute | solution.py:17
  55.2 0.5 collective-permute-start.14
  55.8 1.8 %collective-permute-start.11 = (bf16[32,6144]{1,0:T(8,128)(2,1)S(1)}, bf16[32,6144]{1,0:T(8,128)(2,1)S(1)}, u32[]{:S(2)}, u32[]{:S(2)}) collective-permute-start(bf16[32,6144]{1,0:T(8,128)(2,1)S(1)} %slice.22), channel_id=1, source_target_pairs={{0,64},{64,128},{128,192},{192,0},{1,65},{65,129},{129,193},{193,1... | collective-permute-start | bytes 1179656 | tf_op jit(solution)/shard_map/ppermute | solution.py:17
  58.0 2.7 %collective-permute-start.16 = (s16[128,1664]{1,0:T(8,128)(2,1)S(1)}, s16[128,1664]{1,0:T(8,128)(2,1)S(1)}, u32[]{:S(2)}, u32[]{:S(2)}) collective-permute-start(s16[128,1664]{1,0:T(8,128)(2,1)S(1)} %get-tuple-element.87), channel_id=1, source_target_pairs={{0,16},{8,24},{16,0},{24,8},{1,17},{9,25},{17,1},{25,9},{2,18},{10... | collective-permute-start | bytes 1277960 | tf_op jit(solution)/shard_map/ppermute | solution.py:17
  60.7 1.4 collective-permute-start.17
  62.1 10.3 %shard_map.40 = (s16[128,1664]{1,0:T(8,128)(2,1)S(1)}, s16[128,1664]{1,0:T(8,128)(2,1)S(1)}, s16[128,1664]{1,0:T(8,128)(2,1)S(1)}, s16[128,1664]{1,0:T(8,128)(2,1)S(1)}) custom-call(s32[4]{0:T(128)S(1)} %pad_add_fusion.refs_0_.pos_ref, s32[12,24]{1,0:T(8,128)S(1)} %bitcast.20, ...), custom_call_target="tpu_custom_call", output_to_operand_aliasing={{0}: (7, {}), {1}: (8, {}), {2}: (9, {}), {3}: (10, {})} | custom-call | flops 1 | bytes 1 | tf_op jit(solution)/shard_map/pallas_call | solution.py:110
  73.1 6.3 %collective-permute-done.15.refs_1_ = s16[128,1664]{1,0:T(8,128)(2,1)S(1)} collective-permute-done((s16[128,1664]{1,0:T(8,128)(2,1)S(1)}, s16[128,1664]{1,0:T(8,128)(2,1)S(1)}, u32[]{:S(2)}, u32[]{:S(2)}) %collective-permute-start.15) | collective-permute-done | bytes 426016 | tf_op jit(solution)/shard_map/ppermute | solution.py:17
  79.4 0.6 collective-permute-done.17.refs_3_
  80.0 7.7 %shard_map.41 = (s16[128,1664]{1,0:T(8,128)(2,1)S(1)}, s16[128,1664]{1,0:T(8,128)(2,1)S(1)}, s16[128,1664]{1,0:T(8,128)(2,1)S(1)}, s16[128,1664]{1,0:T(8,128)(2,1)S(1)}) custom-call(s32[4]{0:T(128)S(1)} %pad_add_fusion.refs_0_.pos_ref, s32[12,24]{1,0:T(8,128)S(1)} %bitcast.21, ...), custom_call_target="tpu_custom_call", output_to_operand_aliasing={{0}: (7, {}), {1}: (8, {}), {2}: (9, {}), {3}: (10, {})} | custom-call | flops 1 | bytes 1 | tf_op jit(solution)/shard_map/pallas_call | solution.py:110
  87.7 1.1 collective-permute-start.27
  88.8 3.1 %collective-permute-start.28 = (s16[128,1664]{1,0:T(8,128)(2,1)S(1)}, s16[128,1664]{1,0:T(8,128)(2,1)S(1)}, u32[]{:S(2)}, u32[]{:S(2)}) collective-permute-start(s16[128,1664]{1,0:T(8,128)(2,1)S(1)} %get-tuple-element.109), channel_id=1, source_target_pairs={{0,16},{8,24},{16,0},{24,8},{1,17},{9,25},{17,1},{25,9},{2,18},{10... | collective-permute-start | bytes 1277960 | tf_op jit(solution)/shard_map/ppermute | solution.py:17
  92.0 3.7 %shard_map.42 = (s16[16,1664]{1,0:T(8,128)(2,1)S(1)}, s16[16,1664]{1,0:T(8,128)(2,1)S(1)}, s16[16,1664]{1,0:T(8,128)(2,1)S(1)}, s16[16,1664]{1,0:T(8,128)(2,1)S(...) custom-call(s32[4]{0:T(128)S(1)} %pad_add_fusion.refs_0_.pos_ref, ...), custom_call_target="tpu_custom_call" | custom-call | tf_op jit(solution)/shard_map/pallas_call | solution.py:172
  95.7 2.0 %collective-permute-start.20 = (s16[16,1664]{1,0:T(8,128)(2,1)S(1)}, s16[16,1664]{1,0:T(8,128)(2,1)S(1)}, u32[]{:S(2)}, u32[]{:S(2)}) collective-permute-start(s16[16,1664]{1,0:T(8,128)(2,1)S(1)} %get-tuple-element.116), channel_id=1, source_target_pairs={{0,1},{1,2},{2,3},{3,4},{4,5},{5,6},{6,7},{7,0},{8,9},{9,10},{10,1... | collective-permute-start | bytes 159752 | tf_op jit(solution)/shard_map/ppermute | solution.py:17
  97.7 3.3 %collective-permute-start.21 = (s16[16,1664]{1,0:T(8,128)(2,1)S(1)}, s16[16,1664]{1,0:T(8,128)(2,1)S(1)}, u32[]{:S(2)}, u32[]{:S(2)}) collective-permute-start(s16[16,1664]{1,0:T(8,128)(2,1)S(1)} %get-tuple-element.117), channel_id=1, source_target_pairs={{0,2},{1,3},{2,4},{3,5},{4,6},{5,7},{6,0},{7,1},{8,10},{9,11},{10,... | collective-permute-start | bytes 159752 | tf_op jit(solution)/shard_map/ppermute | solution.py:17
  101.0 4.1 %collective-permute-start.22 = (s16[16,1664]{1,0:T(8,128)(2,1)S(1)}, s16[16,1664]{1,0:T(8,128)(2,1)S(1)}, u32[]{:S(2)}, u32[]{:S(2)}) collective-permute-start(s16[16,1664]{1,0:T(8,128)(2,1)S(1)} %get-tuple-element.118), channel_id=1, source_target_pairs={{0,3},{1,4},{2,5},{3,6},{4,7},{5,0},{6,1},{7,2},{8,11},{9,12},{10,... | collective-permute-start | bytes 159752 | tf_op jit(solution)/shard_map/ppermute | solution.py:17
  105.0 5.7 %collective-permute-done.28.refs_2_ = s16[128,1664]{1,0:T(8,128)(2,1)S(1)} collective-permute-done((s16[128,1664]{1,0:T(8,128)(2,1)S(1)}, s16[128,1664]{1,0:T(8,128)(2,1)S(1)}, u32[]{:S(2)}, u32[]{:S(2)}) %collective-permute-start.28) | collective-permute-done | bytes 426016 | tf_op jit(solution)/shard_map/ppermute | solution.py:17
  110.7 5.9 %collective-permute-start.23 = (s16[16,1664]{1,0:T(8,128)(2,1)S(1)}, s16[16,1664]{1,0:T(8,128)(2,1)S(1)}, u32[]{:S(2)}, u32[]{:S(2)}) collective-permute-start(s16[16,1664]{1,0:T(8,128)(2,1)S(1)} %get-tuple-element.119), channel_id=1, source_target_pairs={{0,4},{1,5},{2,6},{3,7},{4,0},{5,1},{6,2},{7,3},{8,12},{9,13},{10,... | collective-permute-start | bytes 159752 | tf_op jit(solution)/shard_map/ppermute | solution.py:17
  116.7 3.7 %shard_map.43 = (s16[16,1664]{1,0:T(8,128)(2,1)S(1)}, s16[16,1664]{1,0:T(8,128)(2,1)S(1)}, s16[16,1664]{1,0:T(8,128)(2,1)S(1)}, s16[16,1664]{1,0:T(8,128)(2,1)S(...) custom-call(s32[4]{0:T(128)S(1)} %pad_add_fusion.refs_0_.pos_ref, ...), custom_call_target="tpu_custom_call" | custom-call | tf_op jit(solution)/shard_map/pallas_call | solution.py:172
  120.3 4.6 %collective-permute-start.25 = (s16[16,1664]{1,0:T(8,128)(2,1)S(1)}, s16[16,1664]{1,0:T(8,128)(2,1)S(1)}, u32[]{:S(2)}, u32[]{:S(2)}) collective-permute-start(s16[16,1664]{1,0:T(8,128)(2,1)S(1)} %get-tuple-element.121), channel_id=1, source_target_pairs={{0,6},{1,7},{2,0},{3,1},{4,2},{5,3},{6,4},{7,5},{8,14},{9,15},{10,... | collective-permute-start | bytes 159752 | tf_op jit(solution)/shard_map/ppermute | solution.py:17
  125.0 1.0 collective-permute-start.26
  126.0 1.0 collective-permute-start.30
  127.0 3.4 %collective-permute-start.32 = (s16[16,1664]{1,0:T(8,128)(2,1)S(1)}, s16[16,1664]{1,0:T(8,128)(2,1)S(1)}, u32[]{:S(2)}, u32[]{:S(2)}) collective-permute-start(s16[16,1664]{1,0:T(8,128)(2,1)S(1)} %get-tuple-element.126), channel_id=1, source_target_pairs={{0,3},{1,4},{2,5},{3,6},{4,7},{5,0},{6,1},{7,2},{8,11},{9,12},{10,... | collective-permute-start | bytes 159752 | tf_op jit(solution)/shard_map/ppermute | solution.py:17
  130.4 2.6 %collective-permute-start.33 = (s16[16,1664]{1,0:T(8,128)(2,1)S(1)}, s16[16,1664]{1,0:T(8,128)(2,1)S(1)}, u32[]{:S(2)}, u32[]{:S(2)}) collective-permute-start(s16[16,1664]{1,0:T(8,128)(2,1)S(1)} %get-tuple-element.127), channel_id=1, source_target_pairs={{0,4},{1,5},{2,6},{3,7},{4,0},{5,1},{6,2},{7,3},{8,12},{9,13},{10,... | collective-permute-start | bytes 159752 | tf_op jit(solution)/shard_map/ppermute | solution.py:17
  133.0 2.8 %collective-permute-start.34 = (s16[16,1664]{1,0:T(8,128)(2,1)S(1)}, s16[16,1664]{1,0:T(8,128)(2,1)S(1)}, u32[]{:S(2)}, u32[]{:S(2)}) collective-permute-start(s16[16,1664]{1,0:T(8,128)(2,1)S(1)} %get-tuple-element.128), channel_id=1, source_target_pairs={{0,5},{1,6},{2,7},{3,0},{4,1},{5,2},{6,3},{7,4},{8,13},{9,14},{10,... | collective-permute-start | bytes 159752 | tf_op jit(solution)/shard_map/ppermute | solution.py:17
  135.9 1.8 %collective-permute-start.35 = (s16[16,1664]{1,0:T(8,128)(2,1)S(1)}, s16[16,1664]{1,0:T(8,128)(2,1)S(1)}, u32[]{:S(2)}, u32[]{:S(2)}) collective-permute-start(s16[16,1664]{1,0:T(8,128)(2,1)S(1)} %get-tuple-element.129), channel_id=1, source_target_pairs={{0,6},{1,7},{2,0},{3,1},{4,2},{5,3},{6,4},{7,5},{8,14},{9,15},{10,... | collective-permute-start | bytes 159752 | tf_op jit(solution)/shard_map/ppermute | solution.py:17
  137.7 0.6 collective-permute-start.36
  138.2 1.8 %collective-permute-done.33.refs_12_ = s16[16,1664]{1,0:T(8,128)(2,1)S(1)} collective-permute-done((s16[16,1664]{1,0:T(8,128)(2,1)S(1)}, s16[16,1664]{1,0:T(8,128)(2,1)S(1)}, u32[]{:S(2)}, u32[]{:S(2)}) %collective-permute-start.33) | collective-permute-done | bytes 53280 | tf_op jit(solution)/shard_map/ppermute | solution.py:17
  140.5 2.1 %collective-permute-done.35.refs_14_ = s16[16,1664]{1,0:T(8,128)(2,1)S(1)} collective-permute-done((s16[16,1664]{1,0:T(8,128)(2,1)S(1)}, s16[16,1664]{1,0:T(8,128)(2,1)S(1)}, u32[]{:S(2)}, u32[]{:S(2)}) %collective-permute-start.35) | collective-permute-done | bytes 53280 | tf_op jit(solution)/shard_map/ppermute | solution.py:17
  142.6 0.5 collective-permute-done.36.refs_15_
  143.1 1.2 shard_map.44
  (49 shorter events, 2.4 us)
Async XLA Ops:
  0.0 5.1 %collective-permute-start.2 = (bf16[128,6144]{1,0:T(8,128)(2,1)}, bf16[128,6144]{1,0:T(8,128)(2,1)}, u32[]{:S(2)}, u32[]{:S(2)}) collective-permute-start(bf16[128,6144]{1,0:T(8,128)(2,1)} %refs_3_.1), channel_id=1, source_target_pairs={{0,32},{32,0},{1,33},{33,1},{2,34},{34,2},{3,35},{35,3},{4,36},{36... | collective-permute-start | bytes 4718600 | tf_op jit(solution)/shard_map/ppermute | solution.py:17
  0.0 5.0 %copy-start.3 = (s32[12,1,24]{2,1,0:T(1,128)S(1)}, s32[12,1,24]{2,1,0:T(1,128)}, u32[]{:S(2)}) copy-start(s32[12,1,24]{2,1,0:T(1,128)} %param.5) | copy-start | bytes 3460
  0.0 5.1 %copy-start.1 = (bf16[128,6144]{1,0:T(8,128)(2,1)S(1)}, bf16[128,6144]{1,0:T(8,128)(2,1)}, u32[]{:S(2)}) copy-start(bf16[128,6144]{1,0:T(8,128)(2,1)} %refs_3_.1) | copy-start | bytes 4718596
  2.8 20.6 %collective-permute-start = (bf16[64,6144]{1,0:T(8,128)(2,1)}, bf16[64,6144]{1,0:T(8,128)(2,1)S(1)}, u32[]{:S(2)}, u32[]{:S(2)}) collective-permute-start(bf16[64,6144]{1,0:T(8,128)(2,1)} %bitcast.6), channel_id=1, source_target_pairs={{0,64},{64,128},{128,192},{192,0},{1,65},{65,129},{129,193},{193,1... | collective-permute-start | bytes 2359304 | tf_op jit(solution)/shard_map/ppermute | solution.py:17
  4.4 19.9 %collective-permute-start.1 = (bf16[64,6144]{1,0:T(8,128)(2,1)}, bf16[64,6144]{1,0:T(8,128)(2,1)S(1)}, u32[]{:S(2)}, u32[]{:S(2)}) collective-permute-start(bf16[64,6144]{1,0:T(8,128)(2,1)} %bitcast.6), channel_id=1, source_target_pairs={{0,192},{64,0},{128,64},{192,128},{1,193},{65,1},{129,65},{193,129... | collective-permute-start | bytes 2359304 | tf_op jit(solution)/shard_map/ppermute | solution.py:17
  5.1 3.7 %copy-start = (bf16[12,1,24,128,128]{4,3,2,1,0:T(8,128)(2,1)S(1)}, bf16[12,1,24,128,128]{4,3,2,1,0:T(8,128)(2,1)}, u32[]{:S(2)}) copy-start(bf16[12,1,24,128,128]{4,3,2,1,0:T(8,128)(2,1)} %param.4) | copy-start | bytes 28311556
  21.8 5.9 %copy-start.2 = (bf16[4,16,6144]{2,1,0:T(8,128)(2,1)S(1)}, bf16[4,16,6144]{2,1,0:T(8,128)(2,1)}, u32[]{:S(2)}) copy-start(bf16[4,16,6144]{2,1,0:T(8,128)(2,1)} %get-tuple-element.132) | copy-start | bytes 2359300
  24.3 2.9 %collective-permute-start.3 = (bf16[64,6144]{1,0:T(8,128)(2,1)S(1)}, bf16[64,6144]{1,0:T(8,128)(2,1)S(1)}, u32[]{:S(2)}, u32[]{:S(2)}) collective-permute-start(bf16[64,6144]{1,0:T(8,128)(2,1)S(1)} %collective-permute-done.refs_3_), channel_id=1, source_target_pairs={{0,32},{32,0},{1,33},{33,1},{2,34},{34,2},{3,35},{35,3},{4,36},{36... | collective-permute-start | bytes 2359304 | tf_op jit(solution)/shard_map/ppermute | solution.py:17
  24.3 3.4 %collective-permute-start.4 = (bf16[64,6144]{1,0:T(8,128)(2,1)S(1)}, bf16[64,6144]{1,0:T(8,128)(2,1)S(1)}, u32[]{:S(2)}, u32[]{:S(2)}) collective-permute-start(bf16[64,6144]{1,0:T(8,128)(2,1)S(1)} %collective-permute-done.1.refs_4_), channel_id=1, source_target_pairs={{0,32},{32,0},{1,33},{33,1},{2,34},{34,2},{3,35},{35,3},{4,36},{36... | collective-permute-start | bytes 2359304 | tf_op jit(solution)/shard_map/ppermute | solution.py:17
  24.8 15.9 %collective-permute-start.7 = (bf16[32,6144]{1,0:T(8,128)(2,1)S(1)}, bf16[32,6144]{1,0:T(8,128)(2,1)S(1)}, u32[]{:S(2)}, u32[]{:S(2)}) collective-permute-start(bf16[32,6144]{1,0:T(8,128)(2,1)S(1)} %slice.20), channel_id=1, source_target_pairs={{0,64},{64,128},{128,192},{192,0},{1,65},{65,129},{129,193},{193,1... | collective-permute-start | bytes 1179656 | tf_op jit(solution)/shard_map/ppermute | solution.py:17
  26.4 14.3 %collective-permute-start.8 = (bf16[32,6144]{1,0:T(8,128)(2,1)S(1)}, bf16[32,6144]{1,0:T(8,128)(2,1)S(1)}, u32[]{:S(2)}, u32[]{:S(2)}) collective-permute-start(bf16[32,6144]{1,0:T(8,128)(2,1)S(1)} %slice.21), channel_id=1, source_target_pairs={{0,192},{64,0},{128,64},{192,128},{1,193},{65,1},{129,65},{193,129... | collective-permute-start | bytes 1179656 | tf_op jit(solution)/shard_map/ppermute | solution.py:17
  27.7 25.5 %collective-permute-start.5 = (bf16[64,6144]{1,0:T(8,128)(2,1)S(1)}, bf16[64,6144]{1,0:T(8,128)(2,1)S(1)}, u32[]{:S(2)}, u32[]{:S(2)}) collective-permute-start(bf16[64,6144]{1,0:T(8,128)(2,1)S(1)} %bitcast.22), channel_id=1, source_target_pairs={{0,64},{64,128},{128,192},{192,0},{1,65},{65,129},{129,193},{193,1... | collective-permute-start | bytes 2359304 | tf_op jit(solution)/shard_map/ppermute | solution.py:17
  29.5 25.8 %collective-permute-start.6 = (bf16[64,6144]{1,0:T(8,128)(2,1)S(1)}, bf16[64,6144]{1,0:T(8,128)(2,1)S(1)}, u32[]{:S(2)}, u32[]{:S(2)}) collective-permute-start(bf16[64,6144]{1,0:T(8,128)(2,1)S(1)} %bitcast.23), channel_id=1, source_target_pairs={{0,192},{64,0},{128,64},{192,128},{1,193},{65,1},{129,65},{193,129... | collective-permute-start | bytes 2359304 | tf_op jit(solution)/shard_map/ppermute | solution.py:17
  40.8 1.8 %collective-permute-start.10 = (bf16[32,6144]{1,0:T(8,128)(2,1)S(1)}, bf16[32,6144]{1,0:T(8,128)(2,1)S(1)}, u32[]{:S(2)}, u32[]{:S(2)}) collective-permute-start(bf16[32,6144]{1,0:T(8,128)(2,1)S(1)} %collective-permute-done.8.refs_4_), channel_id=1, source_target_pairs={{0,32},{32,0},{1,33},{33,1},{2,34},{34,2},{3,35},{35,3},{4,36},{36... | collective-permute-start | bytes 1179656 | tf_op jit(solution)/shard_map/ppermute | solution.py:17
  40.9 2.3 %collective-permute-start.9 = (bf16[32,6144]{1,0:T(8,128)(2,1)S(1)}, bf16[32,6144]{1,0:T(8,128)(2,1)S(1)}, u32[]{:S(2)}, u32[]{:S(2)}) collective-permute-start(bf16[32,6144]{1,0:T(8,128)(2,1)S(1)} %collective-permute-done.7.refs_3_), channel_id=1, source_target_pairs={{0,32},{32,0},{1,33},{33,1},{2,34},{34,2},{3,35},{35,3},{4,36},{36... | collective-permute-start | bytes 1179656 | tf_op jit(solution)/shard_map/ppermute | solution.py:17
  55.2 2.7 %collective-permute-start.13 = (bf16[64,6144]{1,0:T(8,128)(2,1)S(1)}, bf16[64,6144]{1,0:T(8,128)(2,1)S(1)}, u32[]{:S(2)}, u32[]{:S(2)}) collective-permute-start(bf16[64,6144]{1,0:T(8,128)(2,1)S(1)} %collective-permute-done.5.refs_3_), channel_id=1, source_target_pairs={{0,32},{32,0},{1,33},{33,1},{2,34},{34,2},{3,35},{35,3},{4,36},{36... | collective-permute-start | bytes 2359304 | tf_op jit(solution)/shard_map/ppermute | solution.py:17
  55.2 5.5 %collective-permute-start.14 = (bf16[64,6144]{1,0:T(8,128)(2,1)S(1)}, bf16[64,6144]{1,0:T(8,128)(2,1)S(1)}, u32[]{:S(2)}, u32[]{:S(2)}) collective-permute-start(bf16[64,6144]{1,0:T(8,128)(2,1)S(1)} %collective-permute-done.6.refs_4_), channel_id=1, source_target_pairs={{0,32},{32,0},{1,33},{33,1},{2,34},{34,2},{3,35},{35,3},{4,36},{36... | collective-permute-start | bytes 2359304 | tf_op jit(solution)/shard_map/ppermute | solution.py:17
  55.8 16.7 %collective-permute-start.11 = (bf16[32,6144]{1,0:T(8,128)(2,1)S(1)}, bf16[32,6144]{1,0:T(8,128)(2,1)S(1)}, u32[]{:S(2)}, u32[]{:S(2)}) collective-permute-start(bf16[32,6144]{1,0:T(8,128)(2,1)S(1)} %slice.22), channel_id=1, source_target_pairs={{0,64},{64,128},{128,192},{192,0},{1,65},{65,129},{129,193},{193,1... | collective-permute-start | bytes 1179656 | tf_op jit(solution)/shard_map/ppermute | solution.py:17
  57.6 14.8 %collective-permute-start.12 = (bf16[32,6144]{1,0:T(8,128)(2,1)S(1)}, bf16[32,6144]{1,0:T(8,128)(2,1)S(1)}, u32[]{:S(2)}, u32[]{:S(2)}) collective-permute-start(bf16[32,6144]{1,0:T(8,128)(2,1)S(1)} %slice.23), channel_id=1, source_target_pairs={{0,192},{64,0},{128,64},{192,128},{1,193},{65,1},{129,65},{193,129... | collective-permute-start | bytes 1179656 | tf_op jit(solution)/shard_map/ppermute | solution.py:17
  57.9 21.5 %collective-permute-start.15 = (s16[128,1664]{1,0:T(8,128)(2,1)S(1)}, s16[128,1664]{1,0:T(8,128)(2,1)S(1)}, u32[]{:S(2)}, u32[]{:S(2)}) collective-permute-start(s16[128,1664]{1,0:T(8,128)(2,1)S(1)} %get-tuple-element.86), channel_id=1, source_target_pairs={{0,8},{8,16},{16,24},{24,0},{1,9},{9,17},{17,25},{25,1},{2,10},{10... | collective-permute-start | bytes 1277960 | tf_op jit(solution)/shard_map/ppermute | solution.py:17
  58.0 21.4 %collective-permute-start.16 = (s16[128,1664]{1,0:T(8,128)(2,1)S(1)}, s16[128,1664]{1,0:T(8,128)(2,1)S(1)}, u32[]{:S(2)}, u32[]{:S(2)}) collective-permute-start(s16[128,1664]{1,0:T(8,128)(2,1)S(1)} %get-tuple-element.87), channel_id=1, source_target_pairs={{0,16},{8,24},{16,0},{24,8},{1,17},{9,25},{17,1},{25,9},{2,18},{10... | collective-permute-start | bytes 1277960 | tf_op jit(solution)/shard_map/ppermute | solution.py:17
  60.7 19.3 %collective-permute-start.17 = (s16[128,1664]{1,0:T(8,128)(2,1)S(1)}, s16[128,1664]{1,0:T(8,128)(2,1)S(1)}, u32[]{:S(2)}, u32[]{:S(2)}) collective-permute-start(s16[128,1664]{1,0:T(8,128)(2,1)S(1)} %get-tuple-element.88), channel_id=1, source_target_pairs={{0,24},{8,0},{16,8},{24,16},{1,25},{9,1},{17,9},{25,17},{2,26},{10... | collective-permute-start | bytes 1277960 | tf_op jit(solution)/shard_map/ppermute | solution.py:17
  72.5 7.6 %collective-permute-start.18 = (bf16[32,6144]{1,0:T(8,128)(2,1)S(1)}, bf16[32,6144]{1,0:T(8,128)(2,1)S(1)}, u32[]{:S(2)}, u32[]{:S(2)}) collective-permute-start(bf16[32,6144]{1,0:T(8,128)(2,1)S(1)} %collective-permute-done.11.refs_3_), channel_id=1, source_target_pairs={{0,32},{32,0},{1,33},{33,1},{2,34},{34,2},{3,35},{35,3},{4,36},{36... | collective-permute-start | bytes 1179656 | tf_op jit(solution)/shard_map/ppermute | solution.py:17
  72.6 7.5 %collective-permute-start.19 = (bf16[32,6144]{1,0:T(8,128)(2,1)S(1)}, bf16[32,6144]{1,0:T(8,128)(2,1)S(1)}, u32[]{:S(2)}, u32[]{:S(2)}) collective-permute-start(bf16[32,6144]{1,0:T(8,128)(2,1)S(1)} %collective-permute-done.12.refs_4_), channel_id=1, source_target_pairs={{0,32},{32,0},{1,33},{33,1},{2,34},{34,2},{3,35},{35,3},{4,36},{36... | collective-permute-start | bytes 1179656 | tf_op jit(solution)/shard_map/ppermute | solution.py:17
  87.7 13.3 %collective-permute-start.27 = (s16[128,1664]{1,0:T(8,128)(2,1)S(1)}, s16[128,1664]{1,0:T(8,128)(2,1)S(1)}, u32[]{:S(2)}, u32[]{:S(2)}) collective-permute-start(s16[128,1664]{1,0:T(8,128)(2,1)S(1)} %get-tuple-element.108), channel_id=1, source_target_pairs={{0,8},{8,16},{16,24},{24,0},{1,9},{9,17},{17,25},{25,1},{2,10},{10... | collective-permute-start | bytes 1277960 | tf_op jit(solution)/shard_map/ppermute | solution.py:17
  88.8 22.0 %collective-permute-start.28 = (s16[128,1664]{1,0:T(8,128)(2,1)S(1)}, s16[128,1664]{1,0:T(8,128)(2,1)S(1)}, u32[]{:S(2)}, u32[]{:S(2)}) collective-permute-start(s16[128,1664]{1,0:T(8,128)(2,1)S(1)} %get-tuple-element.109), channel_id=1, source_target_pairs={{0,16},{8,24},{16,0},{24,8},{1,17},{9,25},{17,1},{25,9},{2,18},{10... | collective-permute-start | bytes 1277960 | tf_op jit(solution)/shard_map/ppermute | solution.py:17
  91.9 24.7 %collective-permute-start.29 = (s16[128,1664]{1,0:T(8,128)(2,1)S(1)}, s16[128,1664]{1,0:T(8,128)(2,1)S(1)}, u32[]{:S(2)}, u32[]{:S(2)}) collective-permute-start(s16[128,1664]{1,0:T(8,128)(2,1)S(1)} %get-tuple-element.110), channel_id=1, source_target_pairs={{0,24},{8,0},{16,8},{24,16},{1,25},{9,1},{17,9},{25,17},{2,26},{10... | collective-permute-start | bytes 1277960 | tf_op jit(solution)/shard_map/ppermute | solution.py:17
  95.7 24.6 %collective-permute-start.20 = (s16[16,1664]{1,0:T(8,128)(2,1)S(1)}, s16[16,1664]{1,0:T(8,128)(2,1)S(1)}, u32[]{:S(2)}, u32[]{:S(2)}) collective-permute-start(s16[16,1664]{1,0:T(8,128)(2,1)S(1)} %get-tuple-element.116), channel_id=1, source_target_pairs={{0,1},{1,2},{2,3},{3,4},{4,5},{5,6},{6,7},{7,0},{8,9},{9,10},{10,1... | collective-permute-start | bytes 159752 | tf_op jit(solution)/shard_map/ppermute | solution.py:17
  97.7 27.3 %collective-permute-start.21 = (s16[16,1664]{1,0:T(8,128)(2,1)S(1)}, s16[16,1664]{1,0:T(8,128)(2,1)S(1)}, u32[]{:S(2)}, u32[]{:S(2)}) collective-permute-start(s16[16,1664]{1,0:T(8,128)(2,1)S(1)} %get-tuple-element.117), channel_id=1, source_target_pairs={{0,2},{1,3},{2,4},{3,5},{4,6},{5,7},{6,0},{7,1},{8,10},{9,11},{10,... | collective-permute-start | bytes 159752 | tf_op jit(solution)/shard_map/ppermute | solution.py:17
  101.0 25.0 %collective-permute-start.22 = (s16[16,1664]{1,0:T(8,128)(2,1)S(1)}, s16[16,1664]{1,0:T(8,128)(2,1)S(1)}, u32[]{:S(2)}, u32[]{:S(2)}) collective-permute-start(s16[16,1664]{1,0:T(8,128)(2,1)S(1)} %get-tuple-element.118), channel_id=1, source_target_pairs={{0,3},{1,4},{2,5},{3,6},{4,7},{5,0},{6,1},{7,2},{8,11},{9,12},{10,... | collective-permute-start | bytes 159752 | tf_op jit(solution)/shard_map/ppermute | solution.py:17
  110.7 16.3 %collective-permute-start.23 = (s16[16,1664]{1,0:T(8,128)(2,1)S(1)}, s16[16,1664]{1,0:T(8,128)(2,1)S(1)}, u32[]{:S(2)}, u32[]{:S(2)}) collective-permute-start(s16[16,1664]{1,0:T(8,128)(2,1)S(1)} %get-tuple-element.119), channel_id=1, source_target_pairs={{0,4},{1,5},{2,6},{3,7},{4,0},{5,1},{6,2},{7,3},{8,12},{9,13},{10,... | collective-permute-start | bytes 159752 | tf_op jit(solution)/shard_map/ppermute | solution.py:17
  116.7 10.4 %collective-permute-start.24 = (s16[16,1664]{1,0:T(8,128)(2,1)S(1)}, s16[16,1664]{1,0:T(8,128)(2,1)S(1)}, u32[]{:S(2)}, u32[]{:S(2)}) collective-permute-start(s16[16,1664]{1,0:T(8,128)(2,1)S(1)} %get-tuple-element.120), channel_id=1, source_target_pairs={{0,5},{1,6},{2,7},{3,0},{4,1},{5,2},{6,3},{7,4},{8,13},{9,14},{10,... | collective-permute-start | bytes 159752 | tf_op jit(solution)/shard_map/ppermute | solution.py:17
  120.3 10.1 %collective-permute-start.25 = (s16[16,1664]{1,0:T(8,128)(2,1)S(1)}, s16[16,1664]{1,0:T(8,128)(2,1)S(1)}, u32[]{:S(2)}, u32[]{:S(2)}) collective-permute-start(s16[16,1664]{1,0:T(8,128)(2,1)S(1)} %get-tuple-element.121), channel_id=1, source_target_pairs={{0,6},{1,7},{2,0},{3,1},{4,2},{5,3},{6,4},{7,5},{8,14},{9,15},{10,... | collective-permute-start | bytes 159752 | tf_op jit(solution)/shard_map/ppermute | solution.py:17
  125.0 8.1 %collective-permute-start.26 = (s16[16,1664]{1,0:T(8,128)(2,1)S(1)}, s16[16,1664]{1,0:T(8,128)(2,1)S(1)}, u32[]{:S(2)}, u32[]{:S(2)}) collective-permute-start(s16[16,1664]{1,0:T(8,128)(2,1)S(1)} %get-tuple-element.122), channel_id=1, source_target_pairs={{0,7},{1,0},{2,1},{3,2},{4,3},{5,4},{6,5},{7,6},{8,15},{9,8},{10,9... | collective-permute-start | bytes 159752 | tf_op jit(solution)/shard_map/ppermute | solution.py:17
  126.0 9.9 %collective-permute-start.30 = (s16[16,1664]{1,0:T(8,128)(2,1)S(1)}, s16[16,1664]{1,0:T(8,128)(2,1)S(1)}, u32[]{:S(2)}, u32[]{:S(2)}) collective-permute-start(s16[16,1664]{1,0:T(8,128)(2,1)S(1)} %get-tuple-element.124), channel_id=1, source_target_pairs={{0,1},{1,2},{2,3},{3,4},{4,5},{5,6},{6,7},{7,0},{8,9},{9,10},{10,1... | collective-permute-start | bytes 159752 | tf_op jit(solution)/shard_map/ppermute | solution.py:17
  127.0 10.7 %collective-permute-start.31 = (s16[16,1664]{1,0:T(8,128)(2,1)S(1)}, s16[16,1664]{1,0:T(8,128)(2,1)S(1)}, u32[]{:S(2)}, u32[]{:S(2)}) collective-permute-start(s16[16,1664]{1,0:T(8,128)(2,1)S(1)} %get-tuple-element.125), channel_id=1, source_target_pairs={{0,2},{1,3},{2,4},{3,5},{4,6},{5,7},{6,0},{7,1},{8,10},{9,11},{10,... | collective-permute-start | bytes 159752 | tf_op jit(solution)/shard_map/ppermute | solution.py:17
  127.0 11.2 %collective-permute-start.32 = (s16[16,1664]{1,0:T(8,128)(2,1)S(1)}, s16[16,1664]{1,0:T(8,128)(2,1)S(1)}, u32[]{:S(2)}, u32[]{:S(2)}) collective-permute-start(s16[16,1664]{1,0:T(8,128)(2,1)S(1)} %get-tuple-element.126), channel_id=1, source_target_pairs={{0,3},{1,4},{2,5},{3,6},{4,7},{5,0},{6,1},{7,2},{8,11},{9,12},{10,... | collective-permute-start | bytes 159752 | tf_op jit(solution)/shard_map/ppermute | solution.py:17
  130.4 9.6 %collective-permute-start.33 = (s16[16,1664]{1,0:T(8,128)(2,1)S(1)}, s16[16,1664]{1,0:T(8,128)(2,1)S(1)}, u32[]{:S(2)}, u32[]{:S(2)}) collective-permute-start(s16[16,1664]{1,0:T(8,128)(2,1)S(1)} %get-tuple-element.127), channel_id=1, source_target_pairs={{0,4},{1,5},{2,6},{3,7},{4,0},{5,1},{6,2},{7,3},{8,12},{9,13},{10,... | collective-permute-start | bytes 159752 | tf_op jit(solution)/shard_map/ppermute | solution.py:17
  133.0 7.5 %collective-permute-start.34 = (s16[16,1664]{1,0:T(8,128)(2,1)S(1)}, s16[16,1664]{1,0:T(8,128)(2,1)S(1)}, u32[]{:S(2)}, u32[]{:S(2)}) collective-permute-start(s16[16,1664]{1,0:T(8,128)(2,1)S(1)} %get-tuple-element.128), channel_id=1, source_target_pairs={{0,5},{1,6},{2,7},{3,0},{4,1},{5,2},{6,3},{7,4},{8,13},{9,14},{10,... | collective-permute-start | bytes 159752 | tf_op jit(solution)/shard_map/ppermute | solution.py:17
  135.9 6.7 %collective-permute-start.35 = (s16[16,1664]{1,0:T(8,128)(2,1)S(1)}, s16[16,1664]{1,0:T(8,128)(2,1)S(1)}, u32[]{:S(2)}, u32[]{:S(2)}) collective-permute-start(s16[16,1664]{1,0:T(8,128)(2,1)S(1)} %get-tuple-element.129), channel_id=1, source_target_pairs={{0,6},{1,7},{2,0},{3,1},{4,2},{5,3},{6,4},{7,5},{8,14},{9,15},{10,... | collective-permute-start | bytes 159752 | tf_op jit(solution)/shard_map/ppermute | solution.py:17
  137.7 5.4 %collective-permute-start.36 = (s16[16,1664]{1,0:T(8,128)(2,1)S(1)}, s16[16,1664]{1,0:T(8,128)(2,1)S(1)}, u32[]{:S(2)}, u32[]{:S(2)}) collective-permute-start(s16[16,1664]{1,0:T(8,128)(2,1)S(1)} %get-tuple-element.130), channel_id=1, source_target_pairs={{0,7},{1,0},{2,1},{3,2},{4,3},{5,4},{6,5},{7,6},{8,15},{9,8},{10,9... | collective-permute-start | bytes 159752 | tf_op jit(solution)/shard_map/ppermute | solution.py:17

commit v3 on v2

--- a/solution.py
+++ b/solution.py
@@ -129,7 +129,7 @@
             ],
         ),
         input_output_aliases={} if partial is None else {3 + n_arr + s: s for s in range(n_out)},
-        compiler_params=pltpu.CompilerParams(vmem_limit_bytes=20 << 20),
+        compiler_params=pltpu.CompilerParams(vmem_limit_bytes=50 << 20),
         cost_estimate=pl.CostEstimate(flops=1, transcendentals=0, bytes_accessed=1),
     )(pos, cd_tiles, integrals, *arrays, *(partial or ()))
 
@@ -137,6 +137,43 @@
 def decode(q, scale, tile):
     part = q[:, tile * TILE : (tile + 1) * TILE].astype(jnp.int32).astype(jnp.float32)
     return part * scale[:, tile : tile + 1]
+
+
+def column_sum(four, scale, lane, t, column):
+    total = None
+    for i in range(4):
+        factor = jnp.sum(jnp.where(lane == t, scale[i], 0.0), axis=1, keepdims=True)
+        part = four[i][:, column].astype(jnp.int32).astype(jnp.float32) * factor
+        total = part if total is None else total + part
+    return total
+
+
+def add_plain(parts):
+    rows, wide = parts[0].shape
+    n_tiles = wide // TILE - 1
+
+    def body(*refs):
+        four, out, scale = refs[:4], refs[4], refs[5]
+        lane = lax.broadcasted_iota(jnp.int32, (rows, TILE), 1)
+        for i in range(4):
+            scale[i] = scales(four[i][:, n_tiles * TILE :])
+
+        def one_tile(t, carry):
+            column = pl.ds(pl.multiple_of(t * TILE, TILE), TILE)
+            out[:, column] = column_sum(four, scale, lane, t, column)
+            return carry
+
+        lax.fori_loop(0, n_tiles, one_tile, 0)
+
+    vmem = pl.BlockSpec(memory_space=pltpu.VMEM)
+    return pl.pallas_call(
+        body,
+        out_shape=jax.ShapeDtypeStruct((rows, n_tiles * TILE), jnp.float32),
+        in_specs=[vmem] * 4,
+        out_specs=vmem,
+        scratch_shapes=[pltpu.VMEM((4, rows, TILE), jnp.float32)],
+        compiler_params=pltpu.CompilerParams(vmem_limit_bytes=8 << 20),
+    )(*parts)
 
 
 def add_and_encode(pos, parts, h):
@@ -152,12 +189,7 @@
 
         def one_tile(t, carry):
             column = pl.ds(pl.multiple_of(t * TILE, TILE), TILE)
-            total = None
-            for i in range(4):
-                factor = jnp.sum(jnp.where(lane == t, scale[i], 0.0), axis=1, keepdims=True)
-                part = four[i][:, column].astype(jnp.int32).astype(jnp.float32) * factor
-                total = part if total is None else total + part
-            value, code = encode(total)
+            value, code = encode(column_sum(four, scale, lane, t, column))
             res[:, column] = value
             codes[...] = jnp.where(lane == t, code, codes[...])
             return carry
@@ -183,26 +215,27 @@
     )(pos, *parts)
 
 
-def add_last(arrived):
-    wide = arrived[0][0].shape[1]
+def add_last(eight, summed):
+    height, wide = eight[0].shape
     n_tiles = wide // TILE - 1
-    heights = [eight[0].shape[0] for eight in arrived]
+    first = sum(v.shape[0] for v in summed)
 
     def body(*refs):
         out = refs[-1]
         row = 0
-        for i, h in enumerate(heights):
-            eight = [r[...] for r in refs[NZ * i : NZ * (i + 1)]]
-            scale = [scales(q[:, n_tiles * TILE :]) for q in eight]
-            for t in range(n_tiles):
-                out[row : row + h, t * TILE : (t + 1) * TILE] = sum(decode(q, c, t) for q, c in zip(eight, scale))
-            row += h
+        for r in refs[NZ:-1]:
+            out[row : row + r.shape[0], :] = r[...]
+            row += r.shape[0]
+        parts = [r[...] for r in refs[:NZ]]
+        scale = [scales(q[:, n_tiles * TILE :]) for q in parts]
+        for t in range(n_tiles):
+            out[row:, t * TILE : (t + 1) * TILE] = sum(decode(q, c, t) for q, c in zip(parts, scale))
 
     return pl.pallas_call(
         body,
-        out_shape=jax.ShapeDtypeStruct((sum(heights), n_tiles * TILE), jnp.float32),
+        out_shape=jax.ShapeDtypeStruct((first + height, n_tiles * TILE), jnp.float32),
         compiler_params=pltpu.CompilerParams(vmem_limit_bytes=8 << 20),
-    )(*[q for eight in arrived for q in eight])
+    )(*eight, *summed)
 
 
 def after(values, *others):
@@ -234,10 +267,10 @@
         lo, hi = pair
         return [(lo, 0, lo.shape[0], i, 2, core, 0), (hi, 0, hi.shape[0], i, 2, core, lo.shape[0])]
 
-    parts = [
-        amplitudes.reshape(QW, ROWS, depth)[:, first : first + h].reshape(QW * h, depth) for first, h in CHUNKS
-    ]
-    near_own = [y_halves(parts[0])]
+    def rows_of(source, first, h):
+        return source.reshape(QW, ROWS, depth)[:, first : first + h].reshape(QW * h, depth)
+
+    near_own = [y_halves(rows_of(amplitudes, *CHUNKS[0]))]
     other = shift(amplitudes, "c", NC, 1)
     blocks = []
     for i, (first, h) in enumerate(CHUNKS):
@@ -246,7 +279,9 @@
     coded = contract(pos, cd_tiles, integrals, blocks, heights)
     coded = [coded[4 * i : 4 * i + 4] for i in range(len(CHUNKS))]
 
+    parts = [rows_of(after(amplitudes, coded), *chunk) for chunk in CHUNKS]
     met_x = []
+    summed = []
     for i, h in enumerate(heights):
         if i:
             near_own.append(y_halves(after(parts[i], near_other)))
@@ -258,19 +293,16 @@
         far_own = after(far_own, coded[i])
         far_other = swap(far_own)
         if i:
-            far_own, met_x[i - 1] = lax.optimization_barrier((far_own, met_x[i - 1]))
+            total = add_plain(after(met_x[i - 1], far_other))
+            summed.append(lax.psum_scatter(total, "z", scatter_dimension=0, tiled=True))
+            far_own = after(far_own, total)
         blocks = [b for pair, core in ((far_own, 0), (far_other, 1)) for b in far(0, pair, core)]
         coded[i] = contract(pos, cd_tiles, integrals, blocks, [h], coded[i])
         if i + 1 < len(heights):
             coded[i + 1] = after(coded[i + 1], coded[i])
         met_x.append([coded[i][0]] + [shift(coded[i][s], "x", NX, s) for s in (1, 2, 3)])
-    met_z = []
-    for i, h in enumerate(heights):
-        if i + 1 < len(heights):
-            met_x[i] = after(met_x[i], coded[i + 1])
-        sums = add_and_encode(pos, met_x[i], h)
-        met_z.append([sums[0]] + [shift(sums[s], "z", NZ, s) for s in range(1, NZ)])
-    return add_last(met_z)
+    sums = add_and_encode(pos, met_x[-1], heights[-1])
+    return add_last([sums[0]] + [shift(sums[s], "z", NZ, s) for s in range(1, NZ)], summed)
 
 
 def solution(mesh):

time: 145 us -> 159 us (1.097); the launches traced: 144 us -> 156 us
  starting transfers between devices: 53.2 us -> 37 us
  between operations: 0.19 us -> 13.6 us
  waiting for transfers between devices: 26.7 us -> 33.9 us
  Pallas kernels: 57.5 us -> 63.6 us
    ppermute x37 -> x30, starting transfers between devices: 53.2 us -> 37 us  [shift(): lax.ppermute(value, axis, [(i, (i + step) % size) for i in range(size)])]
    pallas_call x5, Pallas kernels: 49 us -> 56.3 us  [contract(): pl.pallas_call(body, out_shape=[jax.ShapeDtypeStruct((NC * QW * h, width...]
    ppermute x37 -> x30, waiting for transfers between devices: 26.7 us -> 33.9 us  [shift(): lax.ppermute(value, axis, [(i, (i + step) % size) for i in range(size)])]
    pallas_call x2 -> x1, Pallas kernels: 7.31 us -> 3.65 us  [add_and_encode(): pl.pallas_call(body, out_shape=[jax.ShapeDtypeStruct((h, wide), jnp.int16...]
    pallas_call x1 -> x2, Pallas kernels: 1.21 us -> 3.66 us  [the longest x1 2.68 us: add_plain(): pl.pallas_call(body, out_shape=jax.ShapeDtypeStruct((rows, n_tiles * TILE...]
    unnamed x9 -> x27, local copies, waits for them, and re-layouts: 3.69 us -> 5.93 us
  transfers between devices with their start and end apart: 37 -> 31, of which waited for: 14 -> 13; matrix products, arithmetic and copies ran while one was open for 2% -> 1% of each run, Pallas kernels for 34% -> 38%
where the time goes in v3:
time: 159 us; the launch traced here: 156 us
  Pallas kernels  63.6 us (40%)
  starting transfers between devices  37 us (23%)
  waiting for transfers between devices  33.9 us (21%)
  between operations  13.6 us (9%)
  local copies, waits for them, and re-layouts  8.17 us (5%)
    pallas_call x5, Pallas kernels, contract(): pl.pallas_call(body, out_shape=[jax.ShapeDtypeStruct((NC * QW * h, width...  56.3 us
    ppermute x30, starting transfers between devices, shift(): lax.ppermute(value, axis, [(i, (i + step) % size) for i in range(size)])  37 us
    ppermute x30, waiting for transfers between devices, shift(): lax.ppermute(value, axis, [(i, (i + step) % size) for i in range(size)])  33.9 us
    unnamed x27, local copies, waits for them, and re-layouts  5.93 us
    pallas_call x1, Pallas kernels, add_and_encode(): pl.pallas_call(body, out_shape=[jax.ShapeDtypeStruct((h, wide), jnp.int16...  3.65 us
  transfers between devices with their start and end apart: 31, of which 13 were waited for; matrix products, arithmetic and copies ran while one was open for 1% of the time, Pallas kernels for 38%

profile of v3, /device:TPU:8, one launch (start us, length us, event | category | flops | bytes accessed | tf_op | source)
XLA Modules:
  0.0 156.4 jit_solution(7338555790870331960)
XLA Ops:
  6.5 2.1 %slice.25 = bf16[4,16,6144]{2,1,0:T(8,128)(2,1)} slice(bf16[4,32,6144]{2,1,0:T(8,128)(2,1)} %bitcast.22), slice={[0:4], [0:16], [0:6144]} | slice | bytes 1572864 | tf_op jit(solution)/shard_map/slice | solution.py:271
  8.6 1.6 %collective-permute-start.1 = (bf16[64,6144]{1,0:T(8,128)(2,1)}, bf16[64,6144]{1,0:T(8,128)(2,1)S(1)}, u32[]{:S(2)}, u32[]{:S(2)}) collective-permute-start(bf16[64,6144]{1,0:T(8,128)(2,1)} %bitcast.8), channel_id=1, source_target_pairs={{0,64},{64,128},{128,192},{192,0},{1,65},{65,129},{129,193},{193,1... | collective-permute-start | bytes 2359304 | tf_op jit(solution)/shard_map/ppermute | solution.py:17
  10.2 0.6 collective-permute-start.2
  10.9 14.3 %shard_map.37 = (s16[128,1664]{1,0:T(8,128)(2,1)S(1)}, s16[128,1664]{1,0:T(8,128)(2,1)S(1)}, s16[128,1664]{1,0:T(8,128)(2,1)S(1)}, s16[128,1664]{1,0:T(8,128)(2,...) custom-call(s32[4]{0:T(128)S(1)} %pad_add_fusion.refs_0_.pos_ref, ...), custom_call_target="tpu_custom_call" | custom-call | flops 1 | bytes 1 | tf_op jit(solution)/shard_map/pallas_call | solution.py:110
  25.2 4.0 %collective-permute-done.1.refs_3_ = bf16[64,6144]{1,0:T(8,128)(2,1)S(1)} collective-permute-done((bf16[64,6144]{1,0:T(8,128)(2,1)}, bf16[64,6144]{1,0:T(8,128)(2,1)S(1)}, u32[]{:S(2)}, u32[]{:S(2)}) %collective-permute-start.1) | collective-permute-done | bytes 786464 | tf_op jit(solution)/shard_map/ppermute | solution.py:17
  29.2 0.9 collective-permute-done.2.refs_4_
  30.1 0.5 collective-permute-start.4
  30.7 1.6 %collective-permute-start.7 = (bf16[32,6144]{1,0:T(8,128)(2,1)S(1)}, bf16[32,6144]{1,0:T(8,128)(2,1)S(1)}, u32[]{:S(2)}, u32[]{:S(2)}) collective-permute-start(bf16[32,6144]{1,0:T(8,128)(2,1)S(1)} %slice.20), channel_id=1, source_target_pairs={{0,64},{64,128},{128,192},{192,0},{1,65},{65,129},{129,193},{193,1... | collective-permute-start | bytes 1179656 | tf_op jit(solution)/shard_map/ppermute | solution.py:17
  32.3 0.7 collective-permute-start.8
  33.0 0.5 collective-permute-done.4.refs_6_
  33.5 1.9 %collective-permute-start.5 = (bf16[64,6144]{1,0:T(8,128)(2,1)S(1)}, bf16[64,6144]{1,0:T(8,128)(2,1)S(1)}, u32[]{:S(2)}, u32[]{:S(2)}) collective-permute-start(bf16[64,6144]{1,0:T(8,128)(2,1)S(1)} %bitcast.24), channel_id=1, source_target_pairs={{0,64},{64,128},{128,192},{192,0},{1,65},{65,129},{129,193},{193,1... | collective-permute-start | bytes 2359304 | tf_op jit(solution)/shard_map/ppermute | solution.py:17
  35.4 1.0 collective-permute-start.6
  36.3 13.2 %shard_map.38 = (s16[128,1664]{1,0:T(8,128)(2,1)S(1)}, s16[128,1664]{1,0:T(8,128)(2,1)S(1)}, s16[128,1664]{1,0:T(8,128)(2,1)S(1)}, s16[128,1664]{1,0:T(8,128)(2,1)S(1)}) custom-call(s32[4]{0:T(128)S(1)} %pad_add_fusion.refs_0_.pos_ref, s32[12,24]{1,0:T(8,128)S(1)} %bitcast.13, ...), custom_call_target="tpu_custom_call", output_to_operand_aliasing={{0}: (7, {}), {1}: (8, {}), {2}: (9, {}), {3}: (10, {})} | custom-call | flops 1 | bytes 1 | tf_op jit(solution)/shard_map/pallas_call | solution.py:110
  49.6 0.5 collective-permute-start.9
  50.1 1.2 collective-permute-done.10.refs_6_
  51.3 0.6 collective-permute-done.9.refs_5_
  51.9 7.8 %shard_map.39 = (s16[128,1664]{1,0:T(8,128)(2,1)S(1)}, s16[128,1664]{1,0:T(8,128)(2,1)S(1)}, s16[128,1664]{1,0:T(8,128)(2,1)S(1)}, s16[128,1664]{1,0:T(8,128)(2,1)S(1)}) custom-call(s32[4]{0:T(128)S(1)} %pad_add_fusion.refs_0_.pos_ref, s32[12,24]{1,0:T(8,128)S(1)} %bitcast.14, ...), custom_call_target="tpu_custom_call", output_to_operand_aliasing={{0}: (7, {}), {1}: (8, {}), {2}: (9, {}), {3}: (10, {})} | custom-call | flops 1 | bytes 1 | tf_op jit(solution)/shard_map/pallas_call | solution.py:110
  59.8 1.3 collective-permute-done.6.refs_4_
  61.0 0.5 collective-permute-start.14
  61.6 2.0 %collective-permute-start.11 = (bf16[32,6144]{1,0:T(8,128)(2,1)S(1)}, bf16[32,6144]{1,0:T(8,128)(2,1)S(1)}, u32[]{:S(2)}, u32[]{:S(2)}) collective-permute-start(bf16[32,6144]{1,0:T(8,128)(2,1)S(1)} %slice.22), channel_id=1, source_target_pairs={{0,64},{64,128},{128,192},{192,0},{1,65},{65,129},{129,193},{193,1... | collective-permute-start | bytes 1179656 | tf_op jit(solution)/shard_map/ppermute | solution.py:17
  64.0 2.7 %collective-permute-start.16 = (s16[128,1664]{1,0:T(8,128)(2,1)S(1)}, s16[128,1664]{1,0:T(8,128)(2,1)S(1)}, u32[]{:S(2)}, u32[]{:S(2)}) collective-permute-start(s16[128,1664]{1,0:T(8,128)(2,1)S(1)} %get-tuple-element.77), channel_id=1, source_target_pairs={{0,16},{8,24},{16,0},{24,8},{1,17},{9,25},{17,1},{25,9},{2,18},{10... | collective-permute-start | bytes 1277960 | tf_op jit(solution)/shard_map/ppermute | solution.py:17
  66.7 1.4 collective-permute-start.17
  68.1 13.2 %shard_map.40 = (s16[128,1664]{1,0:T(8,128)(2,1)S(1)}, s16[128,1664]{1,0:T(8,128)(2,1)S(1)}, s16[128,1664]{1,0:T(8,128)(2,1)S(1)}, s16[128,1664]{1,0:T(8,128)(2,1)S(1)}) custom-call(s32[4]{0:T(128)S(1)} %pad_add_fusion.refs_0_.pos_ref, s32[12,24]{1,0:T(8,128)S(1)} %bitcast.15, ...), custom_call_target="tpu_custom_call", output_to_operand_aliasing={{0}: (7, {}), {1}: (8, {}), {2}: (9, {}), {3}: (10, {})} | custom-call | flops 1 | bytes 1 | tf_op jit(solution)/shard_map/pallas_call | solution.py:110
  81.5 0.7 copy-done
  82.2 0.5 collective-permute-start.19
  82.7 0.8 copy-done.2
  83.5 2.3 %collective-permute-done.15.refs_1_ = s16[128,1664]{1,0:T(8,128)(2,1)S(1)} collective-permute-done((s16[128,1664]{1,0:T(8,128)(2,1)S(1)}, s16[128,1664]{1,0:T(8,128)(2,1)S(1)}, u32[]{:S(2)}, u32[]{:S(2)}) %collective-permute-start.15) | collective-permute-done | bytes 426016 | tf_op jit(solution)/shard_map/ppermute | solution.py:17
  85.8 0.6 collective-permute-done.17.refs_3_
  86.4 0.7 copy-done.4
  87.2 0.8 copy-done.6
  88.0 2.7 %shard_map.41 = f32[128,1536]{1,0:T(8,128)} custom-call(s16[128,1664]{1,0:T(8,128)(2,1)S(1)} %get-tuple-element.91.refs_0_, s16[128,1664]{1,0:T(8,128)(2,1)S(1)} %collective-permute-done.15.refs_1_, s16[128,1664]{1,0:T(8,128)(2,1)S(1)} %collective-permute-done.16.refs_2_, s16[128,1664]{1,0:T(8,128)(2,1)S(1)} %collective-permute-done.17.refs_3_), custom_call_target="tpu_custom_call" | custom-call | tf_op jit(solution)/shard_map/pallas_call | solution.py:169
  90.7 1.0 copy-done.5
  91.7 1.0 copy-done.7
  92.7 7.8 %shard_map.42 = (s16[128,1664]{1,0:T(8,128)(2,1)S(1)}, s16[128,1664]{1,0:T(8,128)(2,1)S(1)}, s16[128,1664]{1,0:T(8,128)(2,1)S(1)}, s16[128,1664]{1,0:T(8,128)(2,1)S(1)}) custom-call(s32[4]{0:T(128)S(1)} %pad_add_fusion.refs_0_.pos_ref, s32[12,24]{1,0:T(8,128)S(1)} %bitcast.16, ...), custom_call_target="tpu_custom_call", output_to_operand_aliasing={{0}: (7, {}), {1}: (8, {}), {2}: (9, {}), {3}: (10, {})} | custom-call | flops 1 | bytes 1 | tf_op jit(solution)/shard_map/pallas_call | solution.py:110
  100.5 0.8 collective-permute-start.20
  101.3 3.4 %collective-permute-start.21 = (s16[128,1664]{1,0:T(8,128)(2,1)S(1)}, s16[128,1664]{1,0:T(8,128)(2,1)S(1)}, u32[]{:S(2)}, u32[]{:S(2)}) collective-permute-start(s16[128,1664]{1,0:T(8,128)(2,1)S(1)} %get-tuple-element.99), channel_id=1, source_target_pairs={{0,16},{8,24},{16,0},{24,8},{1,17},{9,25},{17,1},{25,9},{2,18},{10... | collective-permute-start | bytes 1277960 | tf_op jit(solution)/shard_map/ppermute | solution.py:17
  104.7 8.5 %collective-permute-done.20.refs_1_ = s16[128,1664]{1,0:T(8,128)(2,1)S(1)} collective-permute-done((s16[128,1664]{1,0:T(8,128)(2,1)S(1)}, s16[128,1664]{1,0:T(8,128)(2,1)S(1)}, u32[]{:S(2)}, u32[]{:S(2)}) %collective-permute-start.20) | collective-permute-done | bytes 426016 | tf_op jit(solution)/shard_map/ppermute | solution.py:17
  113.2 10.3 %collective-permute-done.21.refs_2_ = s16[128,1664]{1,0:T(8,128)(2,1)S(1)} collective-permute-done((s16[128,1664]{1,0:T(8,128)(2,1)S(1)}, s16[128,1664]{1,0:T(8,128)(2,1)S(1)}, u32[]{:S(2)}, u32[]{:S(2)}) %collective-permute-start.21) | collective-permute-done | bytes 426016 | tf_op jit(solution)/shard_map/ppermute | solution.py:17
  123.6 3.7 %shard_map.43 = (s16[16,1664]{1,0:T(8,128)(2,1)S(1)}, s16[16,1664]{1,0:T(8,128)(2,1)S(1)}, s16[16,1664]{1,0:T(8,128)(2,1)S(1)}, s16[16,1664]{1,0:T(8,128)(2,1)S(...) custom-call(s32[4]{0:T(128)S(1)} %pad_add_fusion.refs_0_.pos_ref, ...), custom_call_target="tpu_custom_call" | custom-call | tf_op jit(solution)/shard_map/pallas_call | solution.py:204
  127.6 3.2 %collective-permute-start.24 = (s16[16,1664]{1,0:T(8,128)(2,1)S(1)}, s16[16,1664]{1,0:T(8,128)(2,1)S(1)}, u32[]{:S(2)}, u32[]{:S(2)}) collective-permute-start(s16[16,1664]{1,0:T(8,128)(2,1)S(1)} %get-tuple-element.103), channel_id=1, source_target_pairs={{0,2},{1,3},{2,4},{3,5},{4,6},{5,7},{6,0},{7,1},{8,10},{9,11},{10,... | collective-permute-start | bytes 159752 | tf_op jit(solution)/shard_map/ppermute | solution.py:17
  130.8 4.1 %collective-permute-start.25 = (s16[16,1664]{1,0:T(8,128)(2,1)S(1)}, s16[16,1664]{1,0:T(8,128)(2,1)S(1)}, u32[]{:S(2)}, u32[]{:S(2)}) collective-permute-start(s16[16,1664]{1,0:T(8,128)(2,1)S(1)} %get-tuple-element.104), channel_id=1, source_target_pairs={{0,3},{1,4},{2,5},{3,6},{4,7},{5,0},{6,1},{7,2},{8,11},{9,12},{10,... | collective-permute-start | bytes 159752 | tf_op jit(solution)/shard_map/ppermute | solution.py:17
  135.4 5.0 %collective-permute-start.27 = (s16[16,1664]{1,0:T(8,128)(2,1)S(1)}, s16[16,1664]{1,0:T(8,128)(2,1)S(1)}, u32[]{:S(2)}, u32[]{:S(2)}) collective-permute-start(s16[16,1664]{1,0:T(8,128)(2,1)S(1)} %get-tuple-element.106), channel_id=1, source_target_pairs={{0,5},{1,6},{2,7},{3,0},{4,1},{5,2},{6,3},{7,4},{8,13},{9,14},{10,... | collective-permute-start | bytes 159752 | tf_op jit(solution)/shard_map/ppermute | solution.py:17
  140.4 2.6 %collective-permute-start.28 = (s16[16,1664]{1,0:T(8,128)(2,1)S(1)}, s16[16,1664]{1,0:T(8,128)(2,1)S(1)}, u32[]{:S(2)}, u32[]{:S(2)}) collective-permute-start(s16[16,1664]{1,0:T(8,128)(2,1)S(1)} %get-tuple-element.107), channel_id=1, source_target_pairs={{0,6},{1,7},{2,0},{3,1},{4,2},{5,3},{6,4},{7,5},{8,14},{9,15},{10,... | collective-permute-start | bytes 159752 | tf_op jit(solution)/shard_map/ppermute | solution.py:17
  143.1 1.0 collective-permute-start.29
  144.0 2.0 %collective-permute-done.27.refs_5_ = s16[16,1664]{1,0:T(8,128)(2,1)S(1)} collective-permute-done((s16[16,1664]{1,0:T(8,128)(2,1)S(1)}, s16[16,1664]{1,0:T(8,128)(2,1)S(1)}, u32[]{:S(2)}, u32[]{:S(2)}) %collective-permute-start.27) | collective-permute-done | bytes 53280 | tf_op jit(solution)/shard_map/ppermute | solution.py:17
  146.0 1.5 collective-permute-done.28.refs_6_
  147.6 0.9 copy-done.8
  148.5 1.0 shard_map.44
  (57 shorter events, 1.8 us)
Async XLA Ops:
  6.5 4.3 %copy-start.12 = (s32[12,1,24]{2,1,0:T(1,128)S(1)}, s32[12,1,24]{2,1,0:T(1,128)}, u32[]{:S(2)}) copy-start(s32[12,1,24]{2,1,0:T(1,128)} %param.5) | copy-start | bytes 3460
  6.5 141.1 %reduce-scatter.2.cloned.1.call-start = ((), (), s32[]{:S(2)}) async-start(), calls=%async_computation.1 | async-start | bytes 884736 | tf_op jit(solution)/shard_map/reduce_scatter | solution.py:297
  6.5 4.4 %collective-permute-start = (bf16[128,6144]{1,0:T(8,128)(2,1)}, bf16[128,6144]{1,0:T(8,128)(2,1)}, u32[]{:S(2)}, u32[]{:S(2)}) collective-permute-start(bf16[128,6144]{1,0:T(8,128)(2,1)} %refs_3_.1), channel_id=1, source_target_pairs={{0,32},{32,0},{1,33},{33,1},{2,34},{34,2},{3,35},{35,3},{4,36},{36... | collective-permute-start | bytes 4718600 | tf_op jit(solution)/shard_map/ppermute | solution.py:17
  8.6 20.6 %collective-permute-start.1 = (bf16[64,6144]{1,0:T(8,128)(2,1)}, bf16[64,6144]{1,0:T(8,128)(2,1)S(1)}, u32[]{:S(2)}, u32[]{:S(2)}) collective-permute-start(bf16[64,6144]{1,0:T(8,128)(2,1)} %bitcast.8), channel_id=1, source_target_pairs={{0,64},{64,128},{128,192},{192,0},{1,65},{65,129},{129,193},{193,1... | collective-permute-start | bytes 2359304 | tf_op jit(solution)/shard_map/ppermute | solution.py:17
  10.2 19.9 %collective-permute-start.2 = (bf16[64,6144]{1,0:T(8,128)(2,1)}, bf16[64,6144]{1,0:T(8,128)(2,1)S(1)}, u32[]{:S(2)}, u32[]{:S(2)}) collective-permute-start(bf16[64,6144]{1,0:T(8,128)(2,1)} %bitcast.8), channel_id=1, source_target_pairs={{0,192},{64,0},{128,64},{192,128},{1,193},{65,1},{129,65},{193,129... | collective-permute-start | bytes 2359304 | tf_op jit(solution)/shard_map/ppermute | solution.py:17
  25.2 7.8 %copy-start.9 = (bf16[128,6144]{1,0:T(8,128)(2,1)S(1)}, bf16[128,6144]{1,0:T(8,128)(2,1)}, u32[]{:S(2)}) copy-start(bf16[128,6144]{1,0:T(8,128)(2,1)} %refs_3_.1) | copy-start | bytes 4718596
  30.1 2.9 %collective-permute-start.3 = (bf16[64,6144]{1,0:T(8,128)(2,1)S(1)}, bf16[64,6144]{1,0:T(8,128)(2,1)S(1)}, u32[]{:S(2)}, u32[]{:S(2)}) collective-permute-start(bf16[64,6144]{1,0:T(8,128)(2,1)S(1)} %collective-permute-done.1.refs_3_), channel_id=1, source_target_pairs={{0,32},{32,0},{1,33},{33,1},{2,34},{34,2},{3,35},{35,3},{4,36},{36... | collective-permute-start | bytes 2359304 | tf_op jit(solution)/shard_map/ppermute | solution.py:17
  30.1 3.4 %collective-permute-start.4 = (bf16[64,6144]{1,0:T(8,128)(2,1)S(1)}, bf16[64,6144]{1,0:T(8,128)(2,1)S(1)}, u32[]{:S(2)}, u32[]{:S(2)}) collective-permute-start(bf16[64,6144]{1,0:T(8,128)(2,1)S(1)} %collective-permute-done.2.refs_4_), channel_id=1, source_target_pairs={{0,32},{32,0},{1,33},{33,1},{2,34},{34,2},{3,35},{35,3},{4,36},{36... | collective-permute-start | bytes 2359304 | tf_op jit(solution)/shard_map/ppermute | solution.py:17
  30.7 18.9 %collective-permute-start.7 = (bf16[32,6144]{1,0:T(8,128)(2,1)S(1)}, bf16[32,6144]{1,0:T(8,128)(2,1)S(1)}, u32[]{:S(2)}, u32[]{:S(2)}) collective-permute-start(bf16[32,6144]{1,0:T(8,128)(2,1)S(1)} %slice.20), channel_id=1, source_target_pairs={{0,64},{64,128},{128,192},{192,0},{1,65},{65,129},{129,193},{193,1... | collective-permute-start | bytes 1179656 | tf_op jit(solution)/shard_map/ppermute | solution.py:17
  32.3 17.3 %collective-permute-start.8 = (bf16[32,6144]{1,0:T(8,128)(2,1)S(1)}, bf16[32,6144]{1,0:T(8,128)(2,1)S(1)}, u32[]{:S(2)}, u32[]{:S(2)}) collective-permute-start(bf16[32,6144]{1,0:T(8,128)(2,1)S(1)} %slice.21), channel_id=1, source_target_pairs={{0,192},{64,0},{128,64},{192,128},{1,193},{65,1},{129,65},{193,129... | collective-permute-start | bytes 1179656 | tf_op jit(solution)/shard_map/ppermute | solution.py:17
  33.5 2.8 %copy-start.11 = (bf16[64,6144]{1,0:T(8,128)(2,1)}, bf16[64,6144]{1,0:T(8,128)(2,1)S(1)}, u32[]{:S(2)}) copy-start(bf16[64,6144]{1,0:T(8,128)(2,1)S(1)} %collective-permute-done.4.refs_6_) | copy-start | bytes 2359300
  33.5 26.3 %collective-permute-start.5 = (bf16[64,6144]{1,0:T(8,128)(2,1)S(1)}, bf16[64,6144]{1,0:T(8,128)(2,1)S(1)}, u32[]{:S(2)}, u32[]{:S(2)}) collective-permute-start(bf16[64,6144]{1,0:T(8,128)(2,1)S(1)} %bitcast.24), channel_id=1, source_target_pairs={{0,64},{64,128},{128,192},{192,0},{1,65},{65,129},{129,193},{193,1... | collective-permute-start | bytes 2359304 | tf_op jit(solution)/shard_map/ppermute | solution.py:17
  35.4 25.7 %collective-permute-start.6 = (bf16[64,6144]{1,0:T(8,128)(2,1)S(1)}, bf16[64,6144]{1,0:T(8,128)(2,1)S(1)}, u32[]{:S(2)}, u32[]{:S(2)}) collective-permute-start(bf16[64,6144]{1,0:T(8,128)(2,1)S(1)} %bitcast.25), channel_id=1, source_target_pairs={{0,192},{64,0},{128,64},{192,128},{1,193},{65,1},{129,65},{193,129... | collective-permute-start | bytes 2359304 | tf_op jit(solution)/shard_map/ppermute | solution.py:17
  49.5 1.8 %collective-permute-start.10 = (bf16[32,6144]{1,0:T(8,128)(2,1)S(1)}, bf16[32,6144]{1,0:T(8,128)(2,1)S(1)}, u32[]{:S(2)}, u32[]{:S(2)}) collective-permute-start(bf16[32,6144]{1,0:T(8,128)(2,1)S(1)} %collective-permute-done.8.refs_4_), channel_id=1, source_target_pairs={{0,32},{32,0},{1,33},{33,1},{2,34},{34,2},{3,35},{35,3},{4,36},{36... | collective-permute-start | bytes 1179656 | tf_op jit(solution)/shard_map/ppermute | solution.py:17
  49.6 2.3 %collective-permute-start.9 = (bf16[32,6144]{1,0:T(8,128)(2,1)S(1)}, bf16[32,6144]{1,0:T(8,128)(2,1)S(1)}, u32[]{:S(2)}, u32[]{:S(2)}) collective-permute-start(bf16[32,6144]{1,0:T(8,128)(2,1)S(1)} %collective-permute-done.7.refs_3_), channel_id=1, source_target_pairs={{0,32},{32,0},{1,33},{33,1},{2,34},{34,2},{3,35},{35,3},{4,36},{36... | collective-permute-start | bytes 1179656 | tf_op jit(solution)/shard_map/ppermute | solution.py:17
  61.0 2.9 %collective-permute-start.13 = (bf16[64,6144]{1,0:T(8,128)(2,1)S(1)}, bf16[64,6144]{1,0:T(8,128)(2,1)S(1)}, u32[]{:S(2)}, u32[]{:S(2)}) collective-permute-start(bf16[64,6144]{1,0:T(8,128)(2,1)S(1)} %collective-permute-done.5.refs_3_), channel_id=1, source_target_pairs={{0,32},{32,0},{1,33},{33,1},{2,34},{34,2},{3,35},{35,3},{4,36},{36... | collective-permute-start | bytes 2359304 | tf_op jit(solution)/shard_map/ppermute | solution.py:17
  61.0 5.7 %collective-permute-start.14 = (bf16[64,6144]{1,0:T(8,128)(2,1)S(1)}, bf16[64,6144]{1,0:T(8,128)(2,1)S(1)}, u32[]{:S(2)}, u32[]{:S(2)}) collective-permute-start(bf16[64,6144]{1,0:T(8,128)(2,1)S(1)} %collective-permute-done.6.refs_4_), channel_id=1, source_target_pairs={{0,32},{32,0},{1,33},{33,1},{2,34},{34,2},{3,35},{35,3},{4,36},{36... | collective-permute-start | bytes 2359304 | tf_op jit(solution)/shard_map/ppermute | solution.py:17
  61.6 19.7 %collective-permute-start.11 = (bf16[32,6144]{1,0:T(8,128)(2,1)S(1)}, bf16[32,6144]{1,0:T(8,128)(2,1)S(1)}, u32[]{:S(2)}, u32[]{:S(2)}) collective-permute-start(bf16[32,6144]{1,0:T(8,128)(2,1)S(1)} %slice.22), channel_id=1, source_target_pairs={{0,64},{64,128},{128,192},{192,0},{1,65},{65,129},{129,193},{193,1... | collective-permute-start | bytes 1179656 | tf_op jit(solution)/shard_map/ppermute | solution.py:17
  63.6 17.7 %collective-permute-start.12 = (bf16[32,6144]{1,0:T(8,128)(2,1)S(1)}, bf16[32,6144]{1,0:T(8,128)(2,1)S(1)}, u32[]{:S(2)}, u32[]{:S(2)}) collective-permute-start(bf16[32,6144]{1,0:T(8,128)(2,1)S(1)} %slice.23), channel_id=1, source_target_pairs={{0,192},{64,0},{128,64},{192,128},{1,193},{65,1},{129,65},{193,129... | collective-permute-start | bytes 1179656 | tf_op jit(solution)/shard_map/ppermute | solution.py:17
  63.9 21.9 %collective-permute-start.15 = (s16[128,1664]{1,0:T(8,128)(2,1)S(1)}, s16[128,1664]{1,0:T(8,128)(2,1)S(1)}, u32[]{:S(2)}, u32[]{:S(2)}) collective-permute-start(s16[128,1664]{1,0:T(8,128)(2,1)S(1)} %get-tuple-element.76), channel_id=1, source_target_pairs={{0,8},{8,16},{16,24},{24,0},{1,9},{9,17},{17,25},{25,1},{2,10},{10... | collective-permute-start | bytes 1277960 | tf_op jit(solution)/shard_map/ppermute | solution.py:17
  64.0 21.9 %collective-permute-start.16 = (s16[128,1664]{1,0:T(8,128)(2,1)S(1)}, s16[128,1664]{1,0:T(8,128)(2,1)S(1)}, u32[]{:S(2)}, u32[]{:S(2)}) collective-permute-start(s16[128,1664]{1,0:T(8,128)(2,1)S(1)} %get-tuple-element.77), channel_id=1, source_target_pairs={{0,16},{8,24},{16,0},{24,8},{1,17},{9,25},{17,1},{25,9},{2,18},{10... | collective-permute-start | bytes 1277960 | tf_op jit(solution)/shard_map/ppermute | solution.py:17
  66.7 1.4 copy-start.10
  66.7 19.7 %collective-permute-start.17 = (s16[128,1664]{1,0:T(8,128)(2,1)S(1)}, s16[128,1664]{1,0:T(8,128)(2,1)S(1)}, u32[]{:S(2)}, u32[]{:S(2)}) collective-permute-start(s16[128,1664]{1,0:T(8,128)(2,1)S(1)} %get-tuple-element.78), channel_id=1, source_target_pairs={{0,24},{8,0},{16,8},{24,16},{1,25},{9,1},{17,9},{25,17},{2,26},{10... | collective-permute-start | bytes 1277960 | tf_op jit(solution)/shard_map/ppermute | solution.py:17
  81.4 5.1 %collective-permute-start.18 = (bf16[32,6144]{1,0:T(8,128)(2,1)S(1)}, bf16[32,6144]{1,0:T(8,128)(2,1)S(1)}, u32[]{:S(2)}, u32[]{:S(2)}) collective-permute-start(bf16[32,6144]{1,0:T(8,128)(2,1)S(1)} %collective-permute-done.11.refs_3_), channel_id=1, source_target_pairs={{0,32},{32,0},{1,33},{33,1},{2,34},{34,2},{3,35},{35,3},{4,36},{36... | collective-permute-start | bytes 1179656 | tf_op jit(solution)/shard_map/ppermute | solution.py:17
  81.5 0.7 copy-start
  82.2 5.0 %collective-permute-start.19 = (bf16[32,6144]{1,0:T(8,128)(2,1)S(1)}, bf16[32,6144]{1,0:T(8,128)(2,1)S(1)}, u32[]{:S(2)}, u32[]{:S(2)}) collective-permute-start(bf16[32,6144]{1,0:T(8,128)(2,1)S(1)} %collective-permute-done.12.refs_4_), channel_id=1, source_target_pairs={{0,32},{32,0},{1,33},{33,1},{2,34},{34,2},{3,35},{35,3},{4,36},{36... | collective-permute-start | bytes 1179656 | tf_op jit(solution)/shard_map/ppermute | solution.py:17
  82.7 0.8 copy-start.2
  83.5 7.2 %copy-start.1 = (bf16[32,6144]{1,0:T(8,128)(2,1)S(1)}, bf16[32,6144]{1,0:T(8,128)(2,1)}, u32[]{:S(2)}) copy-start(bf16[32,6144]{1,0:T(8,128)(2,1)} %copy-done) | copy-start | bytes 1179652
  85.8 4.9 %copy-start.3 = (bf16[32,6144]{1,0:T(8,128)(2,1)S(1)}, bf16[32,6144]{1,0:T(8,128)(2,1)}, u32[]{:S(2)}) copy-start(bf16[32,6144]{1,0:T(8,128)(2,1)} %copy-done.2) | copy-start | bytes 1179652
  86.4 0.7 copy-start.4
  87.2 0.8 copy-start.6
  90.7 1.0 copy-start.5
  91.7 1.0 copy-start.7
  100.5 12.7 %collective-permute-start.20 = (s16[128,1664]{1,0:T(8,128)(2,1)S(1)}, s16[128,1664]{1,0:T(8,128)(2,1)S(1)}, u32[]{:S(2)}, u32[]{:S(2)}) collective-permute-start(s16[128,1664]{1,0:T(8,128)(2,1)S(1)} %get-tuple-element.98), channel_id=1, source_target_pairs={{0,8},{8,16},{16,24},{24,0},{1,9},{9,17},{17,25},{25,1},{2,10},{10... | collective-permute-start | bytes 1277960 | tf_op jit(solution)/shard_map/ppermute | solution.py:17
  101.3 22.3 %collective-permute-start.21 = (s16[128,1664]{1,0:T(8,128)(2,1)S(1)}, s16[128,1664]{1,0:T(8,128)(2,1)S(1)}, u32[]{:S(2)}, u32[]{:S(2)}) collective-permute-start(s16[128,1664]{1,0:T(8,128)(2,1)S(1)} %get-tuple-element.99), channel_id=1, source_target_pairs={{0,16},{8,24},{16,0},{24,8},{1,17},{9,25},{17,1},{25,9},{2,18},{10... | collective-permute-start | bytes 1277960 | tf_op jit(solution)/shard_map/ppermute | solution.py:17
  104.7 18.9 %collective-permute-start.22 = (s16[128,1664]{1,0:T(8,128)(2,1)S(1)}, s16[128,1664]{1,0:T(8,128)(2,1)S(1)}, u32[]{:S(2)}, u32[]{:S(2)}) collective-permute-start(s16[128,1664]{1,0:T(8,128)(2,1)S(1)} %get-tuple-element.100), channel_id=1, source_target_pairs={{0,24},{8,0},{16,8},{24,16},{1,25},{9,1},{17,9},{25,17},{2,26},{10... | collective-permute-start | bytes 1277960 | tf_op jit(solution)/shard_map/ppermute | solution.py:17
  127.2 13.2 %collective-permute-start.23 = (s16[16,1664]{1,0:T(8,128)(2,1)S(1)}, s16[16,1664]{1,0:T(8,128)(2,1)S(1)}, u32[]{:S(2)}, u32[]{:S(2)}) collective-permute-start(s16[16,1664]{1,0:T(8,128)(2,1)S(1)} %get-tuple-element.102), channel_id=1, source_target_pairs={{0,1},{1,2},{2,3},{3,4},{4,5},{5,6},{6,7},{7,0},{8,9},{9,10},{10,1... | collective-permute-start | bytes 159752 | tf_op jit(solution)/shard_map/ppermute | solution.py:17
  127.6 15.5 %collective-permute-start.24 = (s16[16,1664]{1,0:T(8,128)(2,1)S(1)}, s16[16,1664]{1,0:T(8,128)(2,1)S(1)}, u32[]{:S(2)}, u32[]{:S(2)}) collective-permute-start(s16[16,1664]{1,0:T(8,128)(2,1)S(1)} %get-tuple-element.103), channel_id=1, source_target_pairs={{0,2},{1,3},{2,4},{3,5},{4,6},{5,7},{6,0},{7,1},{8,10},{9,11},{10,... | collective-permute-start | bytes 159752 | tf_op jit(solution)/shard_map/ppermute | solution.py:17
  130.8 13.2 %collective-permute-start.25 = (s16[16,1664]{1,0:T(8,128)(2,1)S(1)}, s16[16,1664]{1,0:T(8,128)(2,1)S(1)}, u32[]{:S(2)}, u32[]{:S(2)}) collective-permute-start(s16[16,1664]{1,0:T(8,128)(2,1)S(1)} %get-tuple-element.104), channel_id=1, source_target_pairs={{0,3},{1,4},{2,5},{3,6},{4,7},{5,0},{6,1},{7,2},{8,11},{9,12},{10,... | collective-permute-start | bytes 159752 | tf_op jit(solution)/shard_map/ppermute | solution.py:17
  134.9 9.1 %collective-permute-start.26 = (s16[16,1664]{1,0:T(8,128)(2,1)S(1)}, s16[16,1664]{1,0:T(8,128)(2,1)S(1)}, u32[]{:S(2)}, u32[]{:S(2)}) collective-permute-start(s16[16,1664]{1,0:T(8,128)(2,1)S(1)} %get-tuple-element.105), channel_id=1, source_target_pairs={{0,4},{1,5},{2,6},{3,7},{4,0},{5,1},{6,2},{7,3},{8,12},{9,13},{10,... | collective-permute-start | bytes 159752 | tf_op jit(solution)/shard_map/ppermute | solution.py:17
  135.4 10.6 %collective-permute-start.27 = (s16[16,1664]{1,0:T(8,128)(2,1)S(1)}, s16[16,1664]{1,0:T(8,128)(2,1)S(1)}, u32[]{:S(2)}, u32[]{:S(2)}) collective-permute-start(s16[16,1664]{1,0:T(8,128)(2,1)S(1)} %get-tuple-element.106), channel_id=1, source_target_pairs={{0,5},{1,6},{2,7},{3,0},{4,1},{5,2},{6,3},{7,4},{8,13},{9,14},{10,... | collective-permute-start | bytes 159752 | tf_op jit(solution)/shard_map/ppermute | solution.py:17
  140.4 7.1 %collective-permute-start.28 = (s16[16,1664]{1,0:T(8,128)(2,1)S(1)}, s16[16,1664]{1,0:T(8,128)(2,1)S(1)}, u32[]{:S(2)}, u32[]{:S(2)}) collective-permute-start(s16[16,1664]{1,0:T(8,128)(2,1)S(1)} %get-tuple-element.107), channel_id=1, source_target_pairs={{0,6},{1,7},{2,0},{3,1},{4,2},{5,3},{6,4},{7,5},{8,14},{9,15},{10,... | collective-permute-start | bytes 159752 | tf_op jit(solution)/shard_map/ppermute | solution.py:17
  143.1 4.6 %collective-permute-start.29 = (s16[16,1664]{1,0:T(8,128)(2,1)S(1)}, s16[16,1664]{1,0:T(8,128)(2,1)S(1)}, u32[]{:S(2)}, u32[]{:S(2)}) collective-permute-start(s16[16,1664]{1,0:T(8,128)(2,1)S(1)} %get-tuple-element.108), channel_id=1, source_target_pairs={{0,7},{1,0},{2,1},{3,2},{4,3},{5,4},{6,5},{7,6},{8,15},{9,8},{10,9... | collective-permute-start | bytes 159752 | tf_op jit(solution)/shard_map/ppermute | solution.py:17
  147.6 0.9 copy-start.8
Sparse Core Ops, SparseCore 0:
  90.8 38.9 reduce-scatter.1

commit v4 on v2

v4 whole, which is shorter than its diff:
```python
import jax
import jax.numpy as jnp
from jax import lax
from jax.experimental import pallas as pl
from jax.experimental.pallas import tpu as pltpu
from jax.sharding import Mesh, PartitionSpec as P

NY, NC, NX, NZ = 4, 2, 4, 8
TILE = 128
ROWS = 32
QW = 4
CHUNKS = (2, 2)
LEVELS = 32767.0


def shift(value, axis, size, step):
    return lax.ppermute(value, axis, [(i, (i + step) % size) for i in range(size)])


def encode(total):
    top = jnp.maximum(jnp.max(jnp.abs(total), axis=1, keepdims=True), 1e-30)
    code = jnp.ceil(jnp.log2(top) * 256.0) + 1.0
    scaled = total * (jnp.exp2(code * (-1.0 / 256.0)) * LEVELS)
    return jnp.round(scaled).astype(jnp.int32).astype(jnp.int16), code


def scales(codes):
    return jnp.exp2(codes.astype(jnp.int32).astype(jnp.float32) * (1.0 / 256.0)) * (1.0 / LEVELS)


def contract(pos, cd_tiles, integrals, blocks, heights, partial=None):
    n_tiles, n_slots = integrals.shape[0], integrals.shape[1]
    width = n_tiles * TILE
    depth = blocks[0][0].shape[1]
    rows = sum(b[2] for b in blocks)
    arrays = []
    for b in blocks:
        if not any(b[0] is a for a in arrays):
            arrays.append(b[0])
    n_arr, n_blk, n_out = len(arrays), len(blocks), 4 * len(heights)
    where = [next(i for i, a in enumerate(arrays) if a is b[0]) for b in blocks]
    starts = [sum(b[2] for b in blocks[:i]) for i in range(n_blk)]
    n_in = 0 if partial is None else n_out

    def body(*refs):
        pos_ref, cd_ref = refs[:2]
        w_hbm = refs[2]
        a_hbm = refs[3 : 3 + n_arr]
        outs = refs[3 + n_arr + n_in : 3 + n_arr + n_in + n_out]
        wv, av, ov, tot, codes, wsem, asem, osem = refs[3 + n_arr + n_in + n_out :]

        def load(i):
            b = blocks[i]
            return pltpu.make_async_copy(
                a_hbm[where[i]].at[pl.ds(b[1], b[2]), :], av.at[pl.ds(starts[i], b[2]), :], asem.at[i]
            )

        def load_weights(t):
            return pltpu.make_async_copy(w_hbm.at[t], wv.at[t], wsem.at[t])

        load_weights(0).start()
        for i in range(n_blk):
            load(i).start()
        for t in range(1, n_tiles):
            load_weights(t).start()
        for i in range(n_blk):
            load(i).wait()
        codes[...] = jnp.zeros_like(codes)
        tot[...] = jnp.zeros_like(tot)
        lane = lax.broadcasted_iota(jnp.int32, (rows, TILE), 1)

        def put(t, column):
            value, code = encode(tot[...])
            ov[:, pl.ds(column, TILE)] = value
            codes[...] = jnp.where(lane == t, code, codes[...])

        def one_tile(t, carry):
            load_weights(t).wait()
            put(t - 1, pl.multiple_of(jnp.maximum(t - 1, 0) * TILE, TILE))
            weights = jnp.concatenate([wv[t, k] for k in range(n_slots)], axis=1)
            picked = jnp.concatenate(
                [av[:, pl.ds(pl.multiple_of(cd_ref[t, k] * TILE, TILE), TILE)] for k in range(n_slots)], axis=1
            )
            tot[...] = lax.dot_general(
                picked, weights, (((1,), (1,)), ((), ())), preferred_element_type=jnp.float32
            )
            return carry

        lax.fori_loop(0, n_tiles, one_tile, 0)
        put(n_tiles - 1, (n_tiles - 1) * TILE)
        ov[:, width:] = codes[...].astype(jnp.int32).astype(jnp.int16)
        y, c, x = pos_ref[0], pos_ref[1], pos_ref[2]
        for i, b in enumerate(blocks):
            slot = (y + b[4] - x + NX) % NX
            first = pl.multiple_of(((c + b[5]) % NC) * heights[b[3]] + b[6], 8)
            for s in range(NX):

                @pl.when(slot == s)
                def _():
                    pltpu.make_async_copy(
                        ov.at[pl.ds(starts[i], b[2]), :], outs[4 * b[3] + s].at[pl.ds(first, b[2]), :], osem.at[i]
                    ).start()

        for i, b in enumerate(blocks):
            pltpu.make_async_copy(
                ov.at[pl.ds(starts[i], b[2]), :], outs[4 * b[3]].at[pl.ds(0, b[2]), :], osem.at[i]
            ).wait()

    hbm = pl.BlockSpec(memory_space=pltpu.HBM)
    return pl.pallas_call(
        body,
        out_shape=[
            jax.ShapeDtypeStruct((NC * h, width + TILE), jnp.int16) for h in heights for _ in range(4)
        ],
        grid_spec=pltpu.PrefetchScalarGridSpec(
            num_scalar_prefetch=2,
            grid=(1,),
            in_specs=[hbm] * (1 + n_arr + n_in),
            out_specs=[hbm] * n_out,
            scratch_shapes=[
                pltpu.VMEM(integrals.shape, integrals.dtype),
                pltpu.VMEM((rows, depth), blocks[0][0].dtype),
                pltpu.VMEM((rows, width + TILE), jnp.int16),
                pltpu.VMEM((rows, TILE), jnp.float32),
                pltpu.VMEM((rows, TILE), jnp.float32),
                pltpu.SemaphoreType.DMA((n_tiles,)),
                pltpu.SemaphoreType.DMA((n_blk,)),
                pltpu.SemaphoreType.DMA((n_blk,)),
            ],
        ),
        input_output_aliases={} if partial is None else {3 + n_arr + s: s for s in range(n_out)},
        compiler_params=pltpu.CompilerParams(vmem_limit_bytes=20 << 20),
        cost_estimate=pl.CostEstimate(flops=1, transcendentals=0, bytes_accessed=1),
    )(pos, cd_tiles, integrals, *arrays, *(partial or ()))


def add_and_encode(four, scale, codes, res):
    rows, wide = res.shape
    n_tiles = wide // TILE - 1
    lane = lax.broadcasted_iota(jnp.int32, (rows, TILE), 1)
    for i in range(4):
        scale[i] = scales(four[i][:, n_tiles * TILE :])
    codes[...] = jnp.zeros_like(codes)

    def one_tile(t, carry):
        column = pl.ds(pl.multiple_of(t * TILE, TILE), TILE)
        total = None
        for i in range(4):
            factor = jnp.sum(jnp.where(lane == t, scale[i], 0.0), axis=1, keepdims=True)
            part = four[i][:, column].astype(jnp.int32).astype(jnp.float32) * factor
            total = part if total is None else total + part
        value, code = encode(total)
        res[:, column] = value
        codes[...] = jnp.where(lane == t, code, codes[...])
        return carry

    lax.fori_loop(0, n_tiles, one_tile, 0)
    res[:, n_tiles * TILE :] = codes[...].astype(jnp.int32).astype(jnp.int16)


def add_scratch(rows, wide):
    return [pltpu.VMEM((4, rows, TILE), jnp.float32), pltpu.VMEM((rows, TILE), jnp.float32)]


def add_first(parts):
    vmem = pl.BlockSpec(memory_space=pltpu.VMEM)

    def body(*refs):
        add_and_encode(refs[:4], refs[5], refs[6], refs[4])

    return pl.pallas_call(
        body,
        out_shape=jax.ShapeDtypeStruct(parts[0].shape, jnp.int16),
        in_specs=[vmem] * 4,
        out_specs=vmem,
        scratch_shapes=add_scratch(*parts[0].shape),
        compiler_params=pltpu.CompilerParams(vmem_limit_bytes=10 << 20),
    )(*parts)


def add_second(pos, parts, done):
    rows, wide = parts[0].shape
    before, here = done.shape[0] // NC, rows // NC
    vmem = pl.BlockSpec(memory_space=pltpu.VMEM)

    def body(pos_ref, *refs):
        first, outs, (res, both, scale, codes) = refs[4], refs[5 : 5 + NZ], refs[5 + NZ :]
        add_and_encode(refs[:4], scale, codes, res)
        for c in range(NC):
            at = c * (before + here)
            both[at : at + before, :] = first[c * before : (c + 1) * before, :]
            both[at + before : at + before + here, :] = res[c * here : (c + 1) * here, :]
        for s in range(NZ):
            row = pl.multiple_of(((pos_ref[3] + s) % NZ) * ROWS, ROWS)
            outs[s][...] = both[pl.ds(row, ROWS), :]

    return pl.pallas_call(
        body,
        out_shape=[jax.ShapeDtypeStruct((ROWS, wide), jnp.int16)] * NZ,
        in_specs=[pl.BlockSpec(memory_space=pltpu.SMEM)] + [vmem] * 5,
        out_specs=[vmem] * NZ,
        scratch_shapes=[pltpu.VMEM((rows, wide), jnp.int16), pltpu.VMEM((NZ * ROWS, wide), jnp.int16)]
        + add_scratch(rows, wide),
        compiler_params=pltpu.CompilerParams(vmem_limit_bytes=10 << 20),
    )(pos, *parts, done)


def add_last(eight):
    rows, wide = eight[0].shape
    n_tiles = wide // TILE - 1

    def body(*refs):
        out, scale = refs[NZ:]
        lane = lax.broadcasted_iota(jnp.int32, (rows, TILE), 1)
        for i in range(NZ):
            scale[i] = scales(refs[i][:, n_tiles * TILE :])

        def one_tile(t, carry):
            column = pl.ds(pl.multiple_of(t * TILE, TILE), TILE)
            total = None
            for i in range(NZ):
                factor = jnp.sum(jnp.where(lane == t, scale[i], 0.0), axis=1, keepdims=True)
                part = refs[i][:, column].astype(jnp.int32).astype(jnp.float32) * factor
                total = part if total is None else total + part
            out[:, column] = total
            return carry

        lax.fori_loop(0, n_tiles, one_tile, 0)

    return pl.pallas_call(
        body,
        out_shape=jax.ShapeDtypeStruct((rows, n_tiles * TILE), jnp.float32),
        scratch_shapes=[pltpu.VMEM((NZ, rows, TILE), jnp.float32)],
        compiler_params=pltpu.CompilerParams(vmem_limit_bytes=8 << 20),
    )(*eight)


def after(values, *others):
    return lax.optimization_barrier((values, others))[0]


def per_device(amplitudes, integrals, cd_tiles):
    integrals = integrals[:, 0]
    cd_tiles = cd_tiles[:, 0]
    pos = jnp.stack([lax.axis_index(a) for a in ("y", "c", "x", "z")]).astype(jnp.int32)
    heights = [ROWS * n for n in CHUNKS]
    firsts = [0, heights[0]]

    def y_near(own):
        return shift(own, "y", NY, 1), shift(own, "y", NY, -1)

    def y_far(up, down):
        half = up.shape[0] // 2
        return shift(up[:half], "y", NY, 1), shift(down[half:], "y", NY, -1)

    def swap(pair):
        return tuple(shift(v, "c", NC, 1) for v in pair)

    def near(chunk, pair, core):
        up, down = pair
        return [(up, 0, up.shape[0], chunk, -1, core, 0), (down, 0, down.shape[0], chunk, 1, core, 0)]

    def along_x(coded):
        return [coded[0]] + [shift(coded[s], "x", NX, s) for s in (1, 2, 3)]

    def rows_of(source, i):
        return source[firsts[i] : firsts[i] + heights[i]]

    near_1 = y_near(rows_of(amplitudes, 0))
    other = shift(amplitudes, "c", NC, 1)
    blocks = [
        (source, firsts[i], heights[i], i, 0, core, 0) for i in range(2) for source, core in ((amplitudes, 0), (other, 1))
    ]
    coded = contract(pos, cd_tiles, integrals, blocks, heights)
    coded_1, coded_2 = coded[:4], coded[4:]
    part_2 = rows_of(after(amplitudes, coded_1), 1)

    def far(chunk, pair, core):
        lo, hi = pair
        return [(lo, 0, lo.shape[0], chunk, 2, core, 0), (hi, 0, hi.shape[0], chunk, 2, core, lo.shape[0])]

    near_1 = after(near_1, coded_1)
    far_1 = y_far(*near_1)
    near_1_other = swap(near_1)
    near_2 = y_near(after(part_2, near_1_other))
    blocks = near(0, near_1, 0) + near(0, near_1_other, 1)
    coded_1 = contract(pos, cd_tiles, integrals, blocks, heights[:1], coded_1)
    far_1 = after(far_1, coded_1)
    blocks = far(0, far_1, 0) + far(0, swap(far_1), 1)
    coded_1 = contract(pos, cd_tiles, integrals, blocks, heights[:1], coded_1)
    met_1 = along_x(coded_1)

    coded_2 = after(coded_2, coded_1)
    near_2 = after(near_2, coded_1)
    far_2 = y_far(*near_2)
    blocks = near(0, near_2, 0) + near(0, swap(near_2), 1)
    coded_2 = contract(pos, cd_tiles, integrals, blocks, heights[1:], coded_2)
    far_2 = after(far_2, coded_2)
    far_2_other = swap(far_2)
    far_2, met_1 = lax.optimization_barrier((far_2, met_1))
    blocks = far(0, far_2, 0) + far(0, far_2_other, 1)
    coded_2 = contract(pos, cd_tiles, integrals, blocks, heights[1:], coded_2)
    met_2 = along_x(coded_2)

    sums = add_second(pos, met_2, add_first(after(met_1, coded_2)))
    return add_last([sums[0]] + [shift(sums[s], "z", NZ, s) for s in range(1, NZ)])


def solution(mesh):
    fine = Mesh(mesh.devices.reshape(NY, NC, NX, NZ), ("y", "c", "x", "z"))
    return jax.shard_map(
        per_device,
        mesh=fine,
        in_specs=(P(("y", "c"), ("x", "z")), P(("y", "c"), ("x", "z")), P(("y", "c"), ("x", "z"))),
        out_specs=P(("x", "z"), ("y", "c")),
        check_vma=False,
    )
```

time: 145 us -> 147 us (1.014)
  waiting for transfers between devices: 26.7 us -> 46.4 us
  starting transfers between devices: 53.2 us -> 36.5 us
  Pallas kernels: 57.5 us -> 55.7 us
    ppermute x37 -> x30, waiting for transfers between devices: 26.7 us -> 46.4 us  [shift(): lax.ppermute(value, axis, [(i, (i + step) % size) for i in range(size)])]
    ppermute x37 -> x30, starting transfers between devices: 53.2 us -> 36.5 us  [shift(): lax.ppermute(value, axis, [(i, (i + step) % size) for i in range(size)])]
    pallas_call x8, Pallas kernels: 57.5 us -> 55.7 us  [the longest x5 46.9 us: contract(): pl.pallas_call(body, out_shape=[jax.ShapeDtypeStruct((NC * h, width + TIL...]
    unnamed x9 -> x7, local copies, waits for them, and re-layouts: 3.69 us -> 3.69 us
  transfers between devices with their start and end apart: 37 -> 30, of which waited for: 14 -> 16; matrix products, arithmetic and copies ran while one was open for 2% -> 2% of each run, Pallas kernels for 34% -> 29%
where the time goes in v4:
time: 147 us; the launch traced here: 145 us
  Pallas kernels  55.7 us (38%)
  waiting for transfers between devices  46.4 us (32%)
  starting transfers between devices  36.5 us (25%)
  local copies, waits for them, and re-layouts  6.04 us (4%)
    pallas_call x5, Pallas kernels, contract(): pl.pallas_call(body, out_shape=[jax.ShapeDtypeStruct((NC * h, width + TIL...  46.9 us
    ppermute x30, waiting for transfers between devices, shift(): lax.ppermute(value, axis, [(i, (i + step) % size) for i in range(size)])  46.4 us
    ppermute x30, starting transfers between devices, shift(): lax.ppermute(value, axis, [(i, (i + step) % size) for i in range(size)])  36.5 us
    pallas_call x1, Pallas kernels, add_second(): pl.pallas_call(body, out_shape=[jax.ShapeDtypeStruct((ROWS, wide), jnp.in...  3.73 us
    unnamed x7, local copies, waits for them, and re-layouts  3.69 us
    pallas_call x1, Pallas kernels, add_first(): pl.pallas_call(body, out_shape=jax.ShapeDtypeStruct(parts[0].shape, jnp.i...  3.08 us
  transfers between devices with their start and end apart: 30, of which 16 were waited for; matrix products, arithmetic and copies ran while one was open for 2% of the time, Pallas kernels for 29%

profile of v4, /device:TPU:8, one launch (start us, length us, event | category | flops | bytes accessed | tf_op | source)
XLA Modules:
  0.0 145.0 jit_solution(13260512688353236332)
XLA Ops:
  0.0 2.2 %slice.19 = bf16[64,6144]{1,0:T(8,128)(2,1)} slice(bf16[128,6144]{1,0:T(8,128)(2,1)} %refs_3_.1), slice={[0:64], [0:6144]} | slice | bytes 1572864 | tf_op jit(solution)/shard_map/slice | solution.py:267
  2.2 1.6 %collective-permute-start.1 = (bf16[64,6144]{1,0:T(8,128)(2,1)}, bf16[64,6144]{1,0:T(8,128)(2,1)S(1)}, u32[]{:S(2)}, u32[]{:S(2)}) collective-permute-start(bf16[64,6144]{1,0:T(8,128)(2,1)} %slice.19), channel_id=1, source_target_pairs={{0,64},{64,128},{128,192},{192,0},{1,65},{65,129},{129,193},{193,1... | collective-permute-start | bytes 2359304 | tf_op jit(solution)/shard_map/ppermute | solution.py:17
  3.8 0.6 collective-permute-start.2
  4.5 3.7 %copy-done = bf16[12,1,24,128,128]{4,3,2,1,0:T(8,128)(2,1)S(1)} copy-done((bf16[12,1,24,128,128]{4,3,2,1,0:T(8,128)(2,1)S(1)}, bf16[12,1,24,128,128]{4,3,2,1,0:T(8,128)(2,1)}, u32[]{:S(2)}) %copy-start) | copy-done | bytes 9437208
  8.2 10.9 %shard_map.37 = (s16[128,1664]{1,0:T(8,128)(2,1)S(1)}, s16[128,1664]{1,0:T(8,128)(2,1)S(1)}, s16[128,1664]{1,0:T(8,128)(2,1)S(1)}, s16[128,1664]{1,0:T(8,128)(2,...) custom-call(s32[4]{0:T(128)S(1)} %pad_add_fusion.refs_0_.pos_ref, ...), custom_call_target="tpu_custom_call" | custom-call | flops 1 | bytes 1 | tf_op jit(solution)/shard_map/pallas_call | solution.py:110
  19.1 3.6 %collective-permute-done.1.refs_3_ = bf16[64,6144]{1,0:T(8,128)(2,1)S(1)} collective-permute-done((bf16[64,6144]{1,0:T(8,128)(2,1)}, bf16[64,6144]{1,0:T(8,128)(2,1)S(1)}, u32[]{:S(2)}, u32[]{:S(2)}) %collective-permute-start.1) | collective-permute-done | bytes 786464 | tf_op jit(solution)/shard_map/ppermute | solution.py:17
  22.7 0.9 collective-permute-done.2.refs_4_
  23.5 0.5 collective-permute-start.4
  24.1 1.6 %collective-permute-start.7 = (bf16[32,6144]{1,0:T(8,128)(2,1)S(1)}, bf16[32,6144]{1,0:T(8,128)(2,1)S(1)}, u32[]{:S(2)}, u32[]{:S(2)}) collective-permute-start(bf16[32,6144]{1,0:T(8,128)(2,1)S(1)} %slice.20), channel_id=1, source_target_pairs={{0,64},{64,128},{128,192},{192,0},{1,65},{65,129},{129,193},{193,1... | collective-permute-start | bytes 1179656 | tf_op jit(solution)/shard_map/ppermute | solution.py:17
  25.7 0.7 collective-permute-start.8
  26.5 0.5 collective-permute-done.4.refs_6_
  26.9 1.9 %collective-permute-start.5 = (bf16[64,6144]{1,0:T(8,128)(2,1)S(1)}, bf16[64,6144]{1,0:T(8,128)(2,1)S(1)}, u32[]{:S(2)}, u32[]{:S(2)}) collective-permute-start(bf16[64,6144]{1,0:T(8,128)(2,1)S(1)} %slice.18), channel_id=1, source_target_pairs={{0,64},{64,128},{128,192},{192,0},{1,65},{65,129},{129,193},{193,1... | collective-permute-start | bytes 2359304 | tf_op jit(solution)/shard_map/ppermute | solution.py:17
  28.8 1.0 collective-permute-start.6
  29.8 10.3 %shard_map.38 = (s16[128,1664]{1,0:T(8,128)(2,1)S(1)}, s16[128,1664]{1,0:T(8,128)(2,1)S(1)}, s16[128,1664]{1,0:T(8,128)(2,1)S(1)}, s16[128,1664]{1,0:T(8,128)(2,1)S(1)}) custom-call(s32[4]{0:T(128)S(1)} %pad_add_fusion.refs_0_.pos_ref, s32[12,24]{1,0:T(8,128)S(1)} %bitcast.14, ...), custom_call_target="tpu_custom_call", output_to_operand_aliasing={{0}: (7, {}), {1}: (8, {}), {2}: (9, {}), {3}: (10, {})} | custom-call | flops 1 | bytes 1 | tf_op jit(solution)/shard_map/pallas_call | solution.py:110
  40.2 0.5 collective-permute-start.9
  40.7 1.2 collective-permute-done.10.refs_6_
  41.9 0.6 collective-permute-done.9.refs_5_
  42.5 7.7 %shard_map.39 = (s16[128,1664]{1,0:T(8,128)(2,1)S(1)}, s16[128,1664]{1,0:T(8,128)(2,1)S(1)}, s16[128,1664]{1,0:T(8,128)(2,1)S(1)}, s16[128,1664]{1,0:T(8,128)(2,1)S(1)}) custom-call(s32[4]{0:T(128)S(1)} %pad_add_fusion.refs_0_.pos_ref, s32[12,24]{1,0:T(8,128)S(1)} %bitcast.15, ...), custom_call_target="tpu_custom_call", output_to_operand_aliasing={{0}: (7, {}), {1}: (8, {}), {2}: (9, {}), {3}: (10, {})} | custom-call | flops 1 | bytes 1 | tf_op jit(solution)/shard_map/pallas_call | solution.py:110
  50.2 2.3 %collective-permute-done.5.refs_3_ = bf16[64,6144]{1,0:T(8,128)(2,1)S(1)} collective-permute-done((bf16[64,6144]{1,0:T(8,128)(2,1)S(1)}, bf16[64,6144]{1,0:T(8,128)(2,1)S(1)}, u32[]{:S(2)}, u32[]{:S(2)}) %collective-permute-start.5) | collective-permute-done | bytes 786464 | tf_op jit(solution)/shard_map/ppermute | solution.py:17
  52.4 2.1 %collective-permute-done.6.refs_4_ = bf16[64,6144]{1,0:T(8,128)(2,1)S(1)} collective-permute-done((bf16[64,6144]{1,0:T(8,128)(2,1)S(1)}, bf16[64,6144]{1,0:T(8,128)(2,1)S(1)}, u32[]{:S(2)}, u32[]{:S(2)}) %collective-permute-start.6) | collective-permute-done | bytes 786464 | tf_op jit(solution)/shard_map/ppermute | solution.py:17
  54.5 0.5 collective-permute-start.14
  55.1 2.0 %collective-permute-start.11 = (bf16[32,6144]{1,0:T(8,128)(2,1)S(1)}, bf16[32,6144]{1,0:T(8,128)(2,1)S(1)}, u32[]{:S(2)}, u32[]{:S(2)}) collective-permute-start(bf16[32,6144]{1,0:T(8,128)(2,1)S(1)} %slice.22), channel_id=1, source_target_pairs={{0,64},{64,128},{128,192},{192,0},{1,65},{65,129},{129,193},{193,1... | collective-permute-start | bytes 1179656 | tf_op jit(solution)/shard_map/ppermute | solution.py:17
  57.1 0.3 collective-permute-start.12
  57.4 2.7 %collective-permute-start.16 = (s16[128,1664]{1,0:T(8,128)(2,1)S(1)}, s16[128,1664]{1,0:T(8,128)(2,1)S(1)}, u32[]{:S(2)}, u32[]{:S(2)}) collective-permute-start(s16[128,1664]{1,0:T(8,128)(2,1)S(1)} %get-tuple-element.77), channel_id=1, source_target_pairs={{0,16},{8,24},{16,0},{24,8},{1,17},{9,25},{17,1},{25,9},{2,18},{10... | collective-permute-start | bytes 1277960 | tf_op jit(solution)/shard_map/ppermute | solution.py:17
  60.2 1.4 collective-permute-start.17
  61.6 10.3 %shard_map.40 = (s16[128,1664]{1,0:T(8,128)(2,1)S(1)}, s16[128,1664]{1,0:T(8,128)(2,1)S(1)}, s16[128,1664]{1,0:T(8,128)(2,1)S(1)}, s16[128,1664]{1,0:T(8,128)(2,1)S(1)}) custom-call(s32[4]{0:T(128)S(1)} %pad_add_fusion.refs_0_.pos_ref, s32[12,24]{1,0:T(8,128)S(1)} %bitcast.16, ...), custom_call_target="tpu_custom_call", output_to_operand_aliasing={{0}: (7, {}), {1}: (8, {}), {2}: (9, {}), {3}: (10, {})} | custom-call | flops 1 | bytes 1 | tf_op jit(solution)/shard_map/pallas_call | solution.py:110
  72.0 0.5 collective-permute-start.19
  72.5 6.4 %collective-permute-done.15.refs_1_ = s16[128,1664]{1,0:T(8,128)(2,1)S(1)} collective-permute-done((s16[128,1664]{1,0:T(8,128)(2,1)S(1)}, s16[128,1664]{1,0:T(8,128)(2,1)S(1)}, u32[]{:S(2)}, u32[]{:S(2)}) %collective-permute-start.15) | collective-permute-done | bytes 426016 | tf_op jit(solution)/shard_map/ppermute | solution.py:17
  78.9 0.6 collective-permute-done.17.refs_3_
  79.5 7.7 %shard_map.41 = (s16[128,1664]{1,0:T(8,128)(2,1)S(1)}, s16[128,1664]{1,0:T(8,128)(2,1)S(1)}, s16[128,1664]{1,0:T(8,128)(2,1)S(1)}, s16[128,1664]{1,0:T(8,128)(2,1)S(1)}) custom-call(s32[4]{0:T(128)S(1)} %pad_add_fusion.refs_0_.pos_ref, s32[12,24]{1,0:T(8,128)S(1)} %bitcast.17, ...), custom_call_target="tpu_custom_call", output_to_operand_aliasing={{0}: (7, {}), {1}: (8, {}), {2}: (9, {}), {3}: (10, {})} | custom-call | flops 1 | bytes 1 | tf_op jit(solution)/shard_map/pallas_call | solution.py:110
  87.2 1.0 collective-permute-start.20
  88.2 3.1 %collective-permute-start.21 = (s16[128,1664]{1,0:T(8,128)(2,1)S(1)}, s16[128,1664]{1,0:T(8,128)(2,1)S(1)}, u32[]{:S(2)}, u32[]{:S(2)}) collective-permute-start(s16[128,1664]{1,0:T(8,128)(2,1)S(1)} %get-tuple-element.99), channel_id=1, source_target_pairs={{0,16},{8,24},{16,0},{24,8},{1,17},{9,25},{17,1},{25,9},{2,18},{10... | collective-permute-start | bytes 1277960 | tf_op jit(solution)/shard_map/ppermute | solution.py:17
  91.5 3.1 %shard_map.42.refs_4_ = s16[128,1664]{1,0:T(8,128)(2,1)S(1)} custom-call(s16[128,1664]{1,0:T(8,128)(2,1)S(1)} %get-tuple-element.105.refs_0_, s16[128,1664]{1,0:T(8,128)(2,1)S(1)} %collective-permute-done.15.refs_1_, s16[128,1664]{1,0:T(8,128)(2,1)S(1)} %collective-permute-done.16.refs_2_, s16[128,1664]{1,0:T(8,128)(2,1)S(1)} %collective-permute-done.17.refs_3_), custom_call_target="tpu_custom_call" | custom-call | tf_op jit(solution)/shard_map/pallas_call | solution.py:171
  94.6 5.3 %collective-permute-done.20.refs_1_ = s16[128,1664]{1,0:T(8,128)(2,1)S(1)} collective-permute-done((s16[128,1664]{1,0:T(8,128)(2,1)S(1)}, s16[128,1664]{1,0:T(8,128)(2,1)S(1)}, u32[]{:S(2)}, u32[]{:S(2)}) %collective-permute-start.20) | collective-permute-done | bytes 426016 | tf_op jit(solution)/shard_map/ppermute | solution.py:17
  99.9 10.3 %collective-permute-done.21.refs_2_ = s16[128,1664]{1,0:T(8,128)(2,1)S(1)} collective-permute-done((s16[128,1664]{1,0:T(8,128)(2,1)S(1)}, s16[128,1664]{1,0:T(8,128)(2,1)S(1)}, u32[]{:S(2)}, u32[]{:S(2)}) %collective-permute-start.21) | collective-permute-done | bytes 426016 | tf_op jit(solution)/shard_map/ppermute | solution.py:17
  110.2 3.7 %shard_map.43 = (s16[32,1664]{1,0:T(8,128)(2,1)S(1)}, s16[32,1664]{1,0:T(8,128)(2,1)S(1)}, s16[32,1664]{1,0:T(8,128)(2,1)S(1)}, s16[32,1664]{1,0:T(8,128)(2,1)S(...) custom-call(s32[4]{0:T(128)S(1)} %pad_add_fusion.refs_0_.pos_ref, ...), custom_call_target="tpu_custom_call" | custom-call | tf_op jit(solution)/shard_map/pallas_call | solution.py:197
  113.9 0.6 collective-permute-start.23
  114.5 3.2 %collective-permute-start.24 = (s16[32,1664]{1,0:T(8,128)(2,1)S(1)}, s16[32,1664]{1,0:T(8,128)(2,1)S(1)}, u32[]{:S(2)}, u32[]{:S(2)}) collective-permute-start(s16[32,1664]{1,0:T(8,128)(2,1)S(1)} %get-tuple-element.111), channel_id=1, source_target_pairs={{0,2},{1,3},{2,4},{3,5},{4,6},{5,7},{6,0},{7,1},{8,10},{9,11},{10,... | collective-permute-start | bytes 319496 | tf_op jit(solution)/shard_map/ppermute | solution.py:17
  117.8 4.0 %collective-permute-start.25 = (s16[32,1664]{1,0:T(8,128)(2,1)S(1)}, s16[32,1664]{1,0:T(8,128)(2,1)S(1)}, u32[]{:S(2)}, u32[]{:S(2)}) collective-permute-start(s16[32,1664]{1,0:T(8,128)(2,1)S(1)} %get-tuple-element.112), channel_id=1, source_target_pairs={{0,3},{1,4},{2,5},{3,6},{4,7},{5,0},{6,1},{7,2},{8,11},{9,12},{10,... | collective-permute-start | bytes 319496 | tf_op jit(solution)/shard_map/ppermute | solution.py:17
  121.8 0.6 collective-permute-start.26
  122.4 4.9 %collective-permute-start.27 = (s16[32,1664]{1,0:T(8,128)(2,1)S(1)}, s16[32,1664]{1,0:T(8,128)(2,1)S(1)}, u32[]{:S(2)}, u32[]{:S(2)}) collective-permute-start(s16[32,1664]{1,0:T(8,128)(2,1)S(1)} %get-tuple-element.114), channel_id=1, source_target_pairs={{0,5},{1,6},{2,7},{3,0},{4,1},{5,2},{6,3},{7,4},{8,13},{9,14},{10,... | collective-permute-start | bytes 319496 | tf_op jit(solution)/shard_map/ppermute | solution.py:17
  127.3 2.7 %collective-permute-start.28 = (s16[32,1664]{1,0:T(8,128)(2,1)S(1)}, s16[32,1664]{1,0:T(8,128)(2,1)S(1)}, u32[]{:S(2)}, u32[]{:S(2)}) collective-permute-start(s16[32,1664]{1,0:T(8,128)(2,1)S(1)} %get-tuple-element.115), channel_id=1, source_target_pairs={{0,6},{1,7},{2,0},{3,1},{4,2},{5,3},{6,4},{7,5},{8,14},{9,15},{10,... | collective-permute-start | bytes 319496 | tf_op jit(solution)/shard_map/ppermute | solution.py:17
  130.0 2.5 %collective-permute-done.24.refs_2_ = s16[32,1664]{1,0:T(8,128)(2,1)S(1)} collective-permute-done((s16[32,1664]{1,0:T(8,128)(2,1)S(1)}, s16[32,1664]{1,0:T(8,128)(2,1)S(1)}, u32[]{:S(2)}, u32[]{:S(2)}) %collective-permute-start.24) | collective-permute-done | bytes 106528 | tf_op jit(solution)/shard_map/ppermute | solution.py:17
  132.7 2.9 %collective-permute-done.25.refs_3_ = s16[32,1664]{1,0:T(8,128)(2,1)S(1)} collective-permute-done((s16[32,1664]{1,0:T(8,128)(2,1)S(1)}, s16[32,1664]{1,0:T(8,128)(2,1)S(1)}, u32[]{:S(2)}, u32[]{:S(2)}) %collective-permute-start.25) | collective-permute-done | bytes 106528 | tf_op jit(solution)/shard_map/ppermute | solution.py:17
  135.6 5.2 %collective-permute-done.27.refs_5_ = s16[32,1664]{1,0:T(8,128)(2,1)S(1)} collective-permute-done((s16[32,1664]{1,0:T(8,128)(2,1)S(1)}, s16[32,1664]{1,0:T(8,128)(2,1)S(1)}, u32[]{:S(2)}, u32[]{:S(2)}) %collective-permute-start.27) | collective-permute-done | bytes 106528 | tf_op jit(solution)/shard_map/ppermute | solution.py:17
  140.8 0.6 collective-permute-done.28.refs_6_
  141.3 1.6 %collective-permute-done.29.refs_7_ = s16[32,1664]{1,0:T(8,128)(2,1)S(1)} collective-permute-done((s16[32,1664]{1,0:T(8,128)(2,1)S(1)}, s16[32,1664]{1,0:T(8,128)(2,1)S(1)}, u32[]{:S(2)}, u32[]{:S(2)}) %collective-permute-start.29) | collective-permute-done | bytes 106528 | tf_op jit(solution)/shard_map/ppermute | solution.py:17
  142.9 2.0 %shard_map.44 = f32[32,1536]{1,0:T(8,128)} custom-call(s16[32,1664]{1,0:T(8,128)(2,1)S(1)} %get-tuple-element.109.refs_0_, s16[32,1664]{1,0:T(8,128)(2,1)S(1)} %collective-permute-done.23.refs_1_, s16[32,1664]{1,0:T(8,128)(2,1)S(1)} %collective-permute-done.24.refs_2_, s16[32,1664]{1,0:T(8,128)(2,1)S(1)} %collective-permute-done.25.refs_3_, ...), custom_call_target="tpu_custom_call" | custom-call | tf_op jit(solution)/shard_map/pallas_call | solution.py:230
  (34 shorter events, 0.8 us)
Async XLA Ops:
  0.0 4.5 %copy-start.1 = (bf16[128,6144]{1,0:T(8,128)(2,1)S(1)}, bf16[128,6144]{1,0:T(8,128)(2,1)}, u32[]{:S(2)}) copy-start(bf16[128,6144]{1,0:T(8,128)(2,1)} %refs_3_.1) | copy-start | bytes 4718596
  0.0 4.4 %copy-start.2 = (s32[12,1,24]{2,1,0:T(1,128)S(1)}, s32[12,1,24]{2,1,0:T(1,128)}, u32[]{:S(2)}) copy-start(s32[12,1,24]{2,1,0:T(1,128)} %param.5) | copy-start | bytes 3460
  0.0 4.5 %collective-permute-start = (bf16[128,6144]{1,0:T(8,128)(2,1)}, bf16[128,6144]{1,0:T(8,128)(2,1)}, u32[]{:S(2)}, u32[]{:S(2)}) collective-permute-start(bf16[128,6144]{1,0:T(8,128)(2,1)} %refs_3_.1), channel_id=1, source_target_pairs={{0,32},{32,0},{1,33},{33,1},{2,34},{34,2},{3,35},{35,3},{4,36},{36... | collective-permute-start | bytes 4718600 | tf_op jit(solution)/shard_map/ppermute | solution.py:17
  2.2 20.5 %collective-permute-start.1 = (bf16[64,6144]{1,0:T(8,128)(2,1)}, bf16[64,6144]{1,0:T(8,128)(2,1)S(1)}, u32[]{:S(2)}, u32[]{:S(2)}) collective-permute-start(bf16[64,6144]{1,0:T(8,128)(2,1)} %slice.19), channel_id=1, source_target_pairs={{0,64},{64,128},{128,192},{192,0},{1,65},{65,129},{129,193},{193,1... | collective-permute-start | bytes 2359304 | tf_op jit(solution)/shard_map/ppermute | solution.py:17
  3.8 19.7 %collective-permute-start.2 = (bf16[64,6144]{1,0:T(8,128)(2,1)}, bf16[64,6144]{1,0:T(8,128)(2,1)S(1)}, u32[]{:S(2)}, u32[]{:S(2)}) collective-permute-start(bf16[64,6144]{1,0:T(8,128)(2,1)} %slice.19), channel_id=1, source_target_pairs={{0,192},{64,0},{128,64},{192,128},{1,193},{65,1},{129,65},{193,129... | collective-permute-start | bytes 2359304 | tf_op jit(solution)/shard_map/ppermute | solution.py:17
  4.5 3.7 %copy-start = (bf16[12,1,24,128,128]{4,3,2,1,0:T(8,128)(2,1)S(1)}, bf16[12,1,24,128,128]{4,3,2,1,0:T(8,128)(2,1)}, u32[]{:S(2)}) copy-start(bf16[12,1,24,128,128]{4,3,2,1,0:T(8,128)(2,1)} %param.4) | copy-start | bytes 28311556
  23.5 2.9 %collective-permute-start.3 = (bf16[64,6144]{1,0:T(8,128)(2,1)S(1)}, bf16[64,6144]{1,0:T(8,128)(2,1)S(1)}, u32[]{:S(2)}, u32[]{:S(2)}) collective-permute-start(bf16[64,6144]{1,0:T(8,128)(2,1)S(1)} %collective-permute-done.1.refs_3_), channel_id=1, source_target_pairs={{0,32},{32,0},{1,33},{33,1},{2,34},{34,2},{3,35},{35,3},{4,36},{36... | collective-permute-start | bytes 2359304 | tf_op jit(solution)/shard_map/ppermute | solution.py:17
  23.5 3.4 %collective-permute-start.4 = (bf16[64,6144]{1,0:T(8,128)(2,1)S(1)}, bf16[64,6144]{1,0:T(8,128)(2,1)S(1)}, u32[]{:S(2)}, u32[]{:S(2)}) collective-permute-start(bf16[64,6144]{1,0:T(8,128)(2,1)S(1)} %collective-permute-done.2.refs_4_), channel_id=1, source_target_pairs={{0,32},{32,0},{1,33},{33,1},{2,34},{34,2},{3,35},{35,3},{4,36},{36... | collective-permute-start | bytes 2359304 | tf_op jit(solution)/shard_map/ppermute | solution.py:17
  24.1 16.0 %collective-permute-start.7 = (bf16[32,6144]{1,0:T(8,128)(2,1)S(1)}, bf16[32,6144]{1,0:T(8,128)(2,1)S(1)}, u32[]{:S(2)}, u32[]{:S(2)}) collective-permute-start(bf16[32,6144]{1,0:T(8,128)(2,1)S(1)} %slice.20), channel_id=1, source_target_pairs={{0,64},{64,128},{128,192},{192,0},{1,65},{65,129},{129,193},{193,1... | collective-permute-start | bytes 1179656 | tf_op jit(solution)/shard_map/ppermute | solution.py:17
  25.7 14.4 %collective-permute-start.8 = (bf16[32,6144]{1,0:T(8,128)(2,1)S(1)}, bf16[32,6144]{1,0:T(8,128)(2,1)S(1)}, u32[]{:S(2)}, u32[]{:S(2)}) collective-permute-start(bf16[32,6144]{1,0:T(8,128)(2,1)S(1)} %slice.21), channel_id=1, source_target_pairs={{0,192},{64,0},{128,64},{192,128},{1,193},{65,1},{129,65},{193,129... | collective-permute-start | bytes 1179656 | tf_op jit(solution)/shard_map/ppermute | solution.py:17
  26.9 25.5 %collective-permute-start.5 = (bf16[64,6144]{1,0:T(8,128)(2,1)S(1)}, bf16[64,6144]{1,0:T(8,128)(2,1)S(1)}, u32[]{:S(2)}, u32[]{:S(2)}) collective-permute-start(bf16[64,6144]{1,0:T(8,128)(2,1)S(1)} %slice.18), channel_id=1, source_target_pairs={{0,64},{64,128},{128,192},{192,0},{1,65},{65,129},{129,193},{193,1... | collective-permute-start | bytes 2359304 | tf_op jit(solution)/shard_map/ppermute | solution.py:17
  28.8 25.7 %collective-permute-start.6 = (bf16[64,6144]{1,0:T(8,128)(2,1)S(1)}, bf16[64,6144]{1,0:T(8,128)(2,1)S(1)}, u32[]{:S(2)}, u32[]{:S(2)}) collective-permute-start(bf16[64,6144]{1,0:T(8,128)(2,1)S(1)} %slice.18), channel_id=1, source_target_pairs={{0,192},{64,0},{128,64},{192,128},{1,193},{65,1},{129,65},{193,129... | collective-permute-start | bytes 2359304 | tf_op jit(solution)/shard_map/ppermute | solution.py:17
  40.1 1.8 %collective-permute-start.10 = (bf16[32,6144]{1,0:T(8,128)(2,1)S(1)}, bf16[32,6144]{1,0:T(8,128)(2,1)S(1)}, u32[]{:S(2)}, u32[]{:S(2)}) collective-permute-start(bf16[32,6144]{1,0:T(8,128)(2,1)S(1)} %collective-permute-done.8.refs_4_), channel_id=1, source_target_pairs={{0,32},{32,0},{1,33},{33,1},{2,34},{34,2},{3,35},{35,3},{4,36},{36... | collective-permute-start | bytes 1179656 | tf_op jit(solution)/shard_map/ppermute | solution.py:17
  40.2 2.3 %collective-permute-start.9 = (bf16[32,6144]{1,0:T(8,128)(2,1)S(1)}, bf16[32,6144]{1,0:T(8,128)(2,1)S(1)}, u32[]{:S(2)}, u32[]{:S(2)}) collective-permute-start(bf16[32,6144]{1,0:T(8,128)(2,1)S(1)} %collective-permute-done.7.refs_3_), channel_id=1, source_target_pairs={{0,32},{32,0},{1,33},{33,1},{2,34},{34,2},{3,35},{35,3},{4,36},{36... | collective-permute-start | bytes 1179656 | tf_op jit(solution)/shard_map/ppermute | solution.py:17
  54.5 2.9 %collective-permute-start.13 = (bf16[64,6144]{1,0:T(8,128)(2,1)S(1)}, bf16[64,6144]{1,0:T(8,128)(2,1)S(1)}, u32[]{:S(2)}, u32[]{:S(2)}) collective-permute-start(bf16[64,6144]{1,0:T(8,128)(2,1)S(1)} %collective-permute-done.5.refs_3_), channel_id=1, source_target_pairs={{0,32},{32,0},{1,33},{33,1},{2,34},{34,2},{3,35},{35,3},{4,36},{36... | collective-permute-start | bytes 2359304 | tf_op jit(solution)/shard_map/ppermute | solution.py:17
  54.5 5.7 %collective-permute-start.14 = (bf16[64,6144]{1,0:T(8,128)(2,1)S(1)}, bf16[64,6144]{1,0:T(8,128)(2,1)S(1)}, u32[]{:S(2)}, u32[]{:S(2)}) collective-permute-start(bf16[64,6144]{1,0:T(8,128)(2,1)S(1)} %collective-permute-done.6.refs_4_), channel_id=1, source_target_pairs={{0,32},{32,0},{1,33},{33,1},{2,34},{34,2},{3,35},{35,3},{4,36},{36... | collective-permute-start | bytes 2359304 | tf_op jit(solution)/shard_map/ppermute | solution.py:17
  55.1 16.8 %collective-permute-start.11 = (bf16[32,6144]{1,0:T(8,128)(2,1)S(1)}, bf16[32,6144]{1,0:T(8,128)(2,1)S(1)}, u32[]{:S(2)}, u32[]{:S(2)}) collective-permute-start(bf16[32,6144]{1,0:T(8,128)(2,1)S(1)} %slice.22), channel_id=1, source_target_pairs={{0,64},{64,128},{128,192},{192,0},{1,65},{65,129},{129,193},{193,1... | collective-permute-start | bytes 1179656 | tf_op jit(solution)/shard_map/ppermute | solution.py:17
  57.1 14.8 %collective-permute-start.12 = (bf16[32,6144]{1,0:T(8,128)(2,1)S(1)}, bf16[32,6144]{1,0:T(8,128)(2,1)S(1)}, u32[]{:S(2)}, u32[]{:S(2)}) collective-permute-start(bf16[32,6144]{1,0:T(8,128)(2,1)S(1)} %slice.23), channel_id=1, source_target_pairs={{0,192},{64,0},{128,64},{192,128},{1,193},{65,1},{129,65},{193,129... | collective-permute-start | bytes 1179656 | tf_op jit(solution)/shard_map/ppermute | solution.py:17
  57.4 21.5 %collective-permute-start.15 = (s16[128,1664]{1,0:T(8,128)(2,1)S(1)}, s16[128,1664]{1,0:T(8,128)(2,1)S(1)}, u32[]{:S(2)}, u32[]{:S(2)}) collective-permute-start(s16[128,1664]{1,0:T(8,128)(2,1)S(1)} %get-tuple-element.76), channel_id=1, source_target_pairs={{0,8},{8,16},{16,24},{24,0},{1,9},{9,17},{17,25},{25,1},{2,10},{10... | collective-permute-start | bytes 1277960 | tf_op jit(solution)/shard_map/ppermute | solution.py:17
  57.4 21.4 %collective-permute-start.16 = (s16[128,1664]{1,0:T(8,128)(2,1)S(1)}, s16[128,1664]{1,0:T(8,128)(2,1)S(1)}, u32[]{:S(2)}, u32[]{:S(2)}) collective-permute-start(s16[128,1664]{1,0:T(8,128)(2,1)S(1)} %get-tuple-element.77), channel_id=1, source_target_pairs={{0,16},{8,24},{16,0},{24,8},{1,17},{9,25},{17,1},{25,9},{2,18},{10... | collective-permute-start | bytes 1277960 | tf_op jit(solution)/shard_map/ppermute | solution.py:17
  60.2 19.3 %collective-permute-start.17 = (s16[128,1664]{1,0:T(8,128)(2,1)S(1)}, s16[128,1664]{1,0:T(8,128)(2,1)S(1)}, u32[]{:S(2)}, u32[]{:S(2)}) collective-permute-start(s16[128,1664]{1,0:T(8,128)(2,1)S(1)} %get-tuple-element.78), channel_id=1, source_target_pairs={{0,24},{8,0},{16,8},{24,16},{1,25},{9,1},{17,9},{25,17},{2,26},{10... | collective-permute-start | bytes 1277960 | tf_op jit(solution)/shard_map/ppermute | solution.py:17
  71.9 7.6 %collective-permute-start.18 = (bf16[32,6144]{1,0:T(8,128)(2,1)S(1)}, bf16[32,6144]{1,0:T(8,128)(2,1)S(1)}, u32[]{:S(2)}, u32[]{:S(2)}) collective-permute-start(bf16[32,6144]{1,0:T(8,128)(2,1)S(1)} %collective-permute-done.11.refs_3_), channel_id=1, source_target_pairs={{0,32},{32,0},{1,33},{33,1},{2,34},{34,2},{3,35},{35,3},{4,36},{36... | collective-permute-start | bytes 1179656 | tf_op jit(solution)/shard_map/ppermute | solution.py:17
  72.0 7.5 %collective-permute-start.19 = (bf16[32,6144]{1,0:T(8,128)(2,1)S(1)}, bf16[32,6144]{1,0:T(8,128)(2,1)S(1)}, u32[]{:S(2)}, u32[]{:S(2)}) collective-permute-start(bf16[32,6144]{1,0:T(8,128)(2,1)S(1)} %collective-permute-done.12.refs_4_), channel_id=1, source_target_pairs={{0,32},{32,0},{1,33},{33,1},{2,34},{34,2},{3,35},{35,3},{4,36},{36... | collective-permute-start | bytes 1179656 | tf_op jit(solution)/shard_map/ppermute | solution.py:17
  87.2 12.7 %collective-permute-start.20 = (s16[128,1664]{1,0:T(8,128)(2,1)S(1)}, s16[128,1664]{1,0:T(8,128)(2,1)S(1)}, u32[]{:S(2)}, u32[]{:S(2)}) collective-permute-start(s16[128,1664]{1,0:T(8,128)(2,1)S(1)} %get-tuple-element.98), channel_id=1, source_target_pairs={{0,8},{8,16},{16,24},{24,0},{1,9},{9,17},{17,25},{25,1},{2,10},{10... | collective-permute-start | bytes 1277960 | tf_op jit(solution)/shard_map/ppermute | solution.py:17
  88.2 22.0 %collective-permute-start.21 = (s16[128,1664]{1,0:T(8,128)(2,1)S(1)}, s16[128,1664]{1,0:T(8,128)(2,1)S(1)}, u32[]{:S(2)}, u32[]{:S(2)}) collective-permute-start(s16[128,1664]{1,0:T(8,128)(2,1)S(1)} %get-tuple-element.99), channel_id=1, source_target_pairs={{0,16},{8,24},{16,0},{24,8},{1,17},{9,25},{17,1},{25,9},{2,18},{10... | collective-permute-start | bytes 1277960 | tf_op jit(solution)/shard_map/ppermute | solution.py:17
  91.4 18.9 %collective-permute-start.22 = (s16[128,1664]{1,0:T(8,128)(2,1)S(1)}, s16[128,1664]{1,0:T(8,128)(2,1)S(1)}, u32[]{:S(2)}, u32[]{:S(2)}) collective-permute-start(s16[128,1664]{1,0:T(8,128)(2,1)S(1)} %get-tuple-element.100), channel_id=1, source_target_pairs={{0,24},{8,0},{16,8},{24,16},{1,25},{9,1},{17,9},{25,17},{2,26},{10... | collective-permute-start | bytes 1277960 | tf_op jit(solution)/shard_map/ppermute | solution.py:17
  113.9 13.4 %collective-permute-start.23 = (s16[32,1664]{1,0:T(8,128)(2,1)S(1)}, s16[32,1664]{1,0:T(8,128)(2,1)S(1)}, u32[]{:S(2)}, u32[]{:S(2)}) collective-permute-start(s16[32,1664]{1,0:T(8,128)(2,1)S(1)} %get-tuple-element.110), channel_id=1, source_target_pairs={{0,1},{1,2},{2,3},{3,4},{4,5},{5,6},{6,7},{7,0},{8,9},{9,10},{10,1... | collective-permute-start | bytes 319496 | tf_op jit(solution)/shard_map/ppermute | solution.py:17
  114.5 18.0 %collective-permute-start.24 = (s16[32,1664]{1,0:T(8,128)(2,1)S(1)}, s16[32,1664]{1,0:T(8,128)(2,1)S(1)}, u32[]{:S(2)}, u32[]{:S(2)}) collective-permute-start(s16[32,1664]{1,0:T(8,128)(2,1)S(1)} %get-tuple-element.111), channel_id=1, source_target_pairs={{0,2},{1,3},{2,4},{3,5},{4,6},{5,7},{6,0},{7,1},{8,10},{9,11},{10,... | collective-permute-start | bytes 319496 | tf_op jit(solution)/shard_map/ppermute | solution.py:17
  117.8 17.8 %collective-permute-start.25 = (s16[32,1664]{1,0:T(8,128)(2,1)S(1)}, s16[32,1664]{1,0:T(8,128)(2,1)S(1)}, u32[]{:S(2)}, u32[]{:S(2)}) collective-permute-start(s16[32,1664]{1,0:T(8,128)(2,1)S(1)} %get-tuple-element.112), channel_id=1, source_target_pairs={{0,3},{1,4},{2,5},{3,6},{4,7},{5,0},{6,1},{7,2},{8,11},{9,12},{10,... | collective-permute-start | bytes 319496 | tf_op jit(solution)/shard_map/ppermute | solution.py:17
  121.8 13.7 %collective-permute-start.26 = (s16[32,1664]{1,0:T(8,128)(2,1)S(1)}, s16[32,1664]{1,0:T(8,128)(2,1)S(1)}, u32[]{:S(2)}, u32[]{:S(2)}) collective-permute-start(s16[32,1664]{1,0:T(8,128)(2,1)S(1)} %get-tuple-element.113), channel_id=1, source_target_pairs={{0,4},{1,5},{2,6},{3,7},{4,0},{5,1},{6,2},{7,3},{8,12},{9,13},{10,... | collective-permute-start | bytes 319496 | tf_op jit(solution)/shard_map/ppermute | solution.py:17
  122.4 18.4 %collective-permute-start.27 = (s16[32,1664]{1,0:T(8,128)(2,1)S(1)}, s16[32,1664]{1,0:T(8,128)(2,1)S(1)}, u32[]{:S(2)}, u32[]{:S(2)}) collective-permute-start(s16[32,1664]{1,0:T(8,128)(2,1)S(1)} %get-tuple-element.114), channel_id=1, source_target_pairs={{0,5},{1,6},{2,7},{3,0},{4,1},{5,2},{6,3},{7,4},{8,13},{9,14},{10,... | collective-permute-start | bytes 319496 | tf_op jit(solution)/shard_map/ppermute | solution.py:17
  127.3 14.0 %collective-permute-start.28 = (s16[32,1664]{1,0:T(8,128)(2,1)S(1)}, s16[32,1664]{1,0:T(8,128)(2,1)S(1)}, u32[]{:S(2)}, u32[]{:S(2)}) collective-permute-start(s16[32,1664]{1,0:T(8,128)(2,1)S(1)} %get-tuple-element.115), channel_id=1, source_target_pairs={{0,6},{1,7},{2,0},{3,1},{4,2},{5,3},{6,4},{7,5},{8,14},{9,15},{10,... | collective-permute-start | bytes 319496 | tf_op jit(solution)/shard_map/ppermute | solution.py:17
  132.5 10.4 %collective-permute-start.29 = (s16[32,1664]{1,0:T(8,128)(2,1)S(1)}, s16[32,1664]{1,0:T(8,128)(2,1)S(1)}, u32[]{:S(2)}, u32[]{:S(2)}) collective-permute-start(s16[32,1664]{1,0:T(8,128)(2,1)S(1)} %get-tuple-element.116), channel_id=1, source_target_pairs={{0,7},{1,0},{2,1},{3,2},{4,3},{5,4},{6,5},{7,6},{8,15},{9,8},{10,9... | collective-permute-start | bytes 319496 | tf_op jit(solution)/shard_map/ppermute | solution.py:17

commit v5 on v4

--- a/solution.py
+++ b/solution.py
@@ -154,7 +154,7 @@
         codes[...] = jnp.where(lane == t, code, codes[...])
         return carry
 
-    lax.fori_loop(0, n_tiles, one_tile, 0)
+    lax.fori_loop(0, n_tiles, one_tile, 0, unroll=4)
     res[:, n_tiles * TILE :] = codes[...].astype(jnp.int32).astype(jnp.int16)
 
 
@@ -225,7 +225,7 @@
             out[:, column] = total
             return carry
 
-        lax.fori_loop(0, n_tiles, one_tile, 0)
+        lax.fori_loop(0, n_tiles, one_tile, 0, unroll=4)
 
     return pl.pallas_call(
         body,
@@ -261,7 +261,7 @@
         return [(up, 0, up.shape[0], chunk, -1, core, 0), (down, 0, down.shape[0], chunk, 1, core, 0)]
 
     def along_x(coded):
-        return [coded[0]] + [shift(coded[s], "x", NX, s) for s in (1, 2, 3)]
+        return [coded[0]] + [shift(coded[s], "x", NX, s) for s in (2, 1, 3)]
 
     def rows_of(source, i):
         return source[firsts[i] : firsts[i] + heights[i]]
@@ -297,13 +297,12 @@
     coded_2 = contract(pos, cd_tiles, integrals, blocks, heights[1:], coded_2)
     far_2 = after(far_2, coded_2)
     far_2_other = swap(far_2)
-    far_2, met_1 = lax.optimization_barrier((far_2, met_1))
     blocks = far(0, far_2, 0) + far(0, far_2_other, 1)
     coded_2 = contract(pos, cd_tiles, integrals, blocks, heights[1:], coded_2)
     met_2 = along_x(coded_2)
 
     sums = add_second(pos, met_2, add_first(after(met_1, coded_2)))
-    return add_last([sums[0]] + [shift(sums[s], "z", NZ, s) for s in range(1, NZ)])
+    return add_last([sums[0]] + [shift(sums[s], "z", NZ, s) for s in (4, 3, 5, 2, 6, 1, 7)])
 
 
 def solution(mesh):

time: 147 us -> 136 us (0.925)
  waiting for transfers between devices: 46.4 us -> 36.7 us
  Pallas kernels: 55.7 us -> 52.7 us
  starting transfers between devices: 36.5 us -> 38 us
    ppermute x30, waiting for transfers between devices: 46.4 us -> 36.7 us  [shift(): lax.ppermute(value, axis, [(i, (i + step) % size) for i in range(size)])]
  transfers between devices with their start and end apart: 30 -> 30, of which waited for: 16 -> 15; matrix products, arithmetic and copies ran while one was open for 2% -> 2% of each run, Pallas kernels for 29% -> 37%
where the time goes in v5:
time: 136 us; the launch traced here: 134 us
  Pallas kernels  52.7 us (39%)
  starting transfers between devices  38 us (28%)
  waiting for transfers between devices  36.7 us (27%)
  local copies, waits for them, and re-layouts  6.04 us (4%)
    pallas_call x5, Pallas kernels, contract(): pl.pallas_call(body, out_shape=[jax.ShapeDtypeStruct((NC * h, width + TIL...  46.9 us
    ppermute x30, starting transfers between devices, shift(): lax.ppermute(value, axis, [(i, (i + step) % size) for i in range(size)])  38 us
    ppermute x30, waiting for transfers between devices, shift(): lax.ppermute(value, axis, [(i, (i + step) % size) for i in range(size)])  36.7 us
    unnamed x7, local copies, waits for them, and re-layouts  3.69 us
  transfers between devices with their start and end apart: 30, of which 15 were waited for; matrix products, arithmetic and copies ran while one was open for 2% of the time, Pallas kernels for 37%

profile of v5, /device:TPU:8, one launch (start us, length us, event | category | flops | bytes accessed | tf_op | source)
XLA Modules:
  0.0 133.7 jit_solution(13637594706577363774)
XLA Ops:
  0.0 2.2 %slice.19 = bf16[64,6144]{1,0:T(8,128)(2,1)} slice(bf16[128,6144]{1,0:T(8,128)(2,1)} %refs_3_.1), slice={[0:64], [0:6144]} | slice | bytes 1572864 | tf_op jit(solution)/shard_map/slice | solution.py:267
  2.2 1.6 %collective-permute-start.1 = (bf16[64,6144]{1,0:T(8,128)(2,1)}, bf16[64,6144]{1,0:T(8,128)(2,1)S(1)}, u32[]{:S(2)}, u32[]{:S(2)}) collective-permute-start(bf16[64,6144]{1,0:T(8,128)(2,1)} %slice.19), channel_id=1, source_target_pairs={{0,64},{64,128},{128,192},{192,0},{1,65},{65,129},{129,193},{193,1... | collective-permute-start | bytes 2359304 | tf_op jit(solution)/shard_map/ppermute | solution.py:17
  3.8 0.6 collective-permute-start.2
  4.5 3.7 %copy-done = bf16[12,1,24,128,128]{4,3,2,1,0:T(8,128)(2,1)S(1)} copy-done((bf16[12,1,24,128,128]{4,3,2,1,0:T(8,128)(2,1)S(1)}, bf16[12,1,24,128,128]{4,3,2,1,0:T(8,128)(2,1)}, u32[]{:S(2)}) %copy-start) | copy-done | bytes 9437208
  8.2 10.9 %shard_map.37 = (s16[128,1664]{1,0:T(8,128)(2,1)S(1)}, s16[128,1664]{1,0:T(8,128)(2,1)S(1)}, s16[128,1664]{1,0:T(8,128)(2,1)S(1)}, s16[128,1664]{1,0:T(8,128)(2,...) custom-call(s32[4]{0:T(128)S(1)} %pad_add_fusion.refs_0_.pos_ref, ...), custom_call_target="tpu_custom_call" | custom-call | flops 1 | bytes 1 | tf_op jit(solution)/shard_map/pallas_call | solution.py:110
  19.1 3.6 %collective-permute-done.1.refs_3_ = bf16[64,6144]{1,0:T(8,128)(2,1)S(1)} collective-permute-done((bf16[64,6144]{1,0:T(8,128)(2,1)}, bf16[64,6144]{1,0:T(8,128)(2,1)S(1)}, u32[]{:S(2)}, u32[]{:S(2)}) %collective-permute-start.1) | collective-permute-done | bytes 786464 | tf_op jit(solution)/shard_map/ppermute | solution.py:17
  22.7 0.9 collective-permute-done.2.refs_4_
  23.5 0.5 collective-permute-start.4
  24.1 1.6 %collective-permute-start.7 = (bf16[32,6144]{1,0:T(8,128)(2,1)S(1)}, bf16[32,6144]{1,0:T(8,128)(2,1)S(1)}, u32[]{:S(2)}, u32[]{:S(2)}) collective-permute-start(bf16[32,6144]{1,0:T(8,128)(2,1)S(1)} %slice.20), channel_id=1, source_target_pairs={{0,64},{64,128},{128,192},{192,0},{1,65},{65,129},{129,193},{193,1... | collective-permute-start | bytes 1179656 | tf_op jit(solution)/shard_map/ppermute | solution.py:17
  25.7 0.7 collective-permute-start.8
  26.5 0.5 collective-permute-done.4.refs_6_
  26.9 1.9 %collective-permute-start.5 = (bf16[64,6144]{1,0:T(8,128)(2,1)S(1)}, bf16[64,6144]{1,0:T(8,128)(2,1)S(1)}, u32[]{:S(2)}, u32[]{:S(2)}) collective-permute-start(bf16[64,6144]{1,0:T(8,128)(2,1)S(1)} %slice.18), channel_id=1, source_target_pairs={{0,64},{64,128},{128,192},{192,0},{1,65},{65,129},{129,193},{193,1... | collective-permute-start | bytes 2359304 | tf_op jit(solution)/shard_map/ppermute | solution.py:17
  28.8 1.0 collective-permute-start.6
  29.8 10.3 %shard_map.38 = (s16[128,1664]{1,0:T(8,128)(2,1)S(1)}, s16[128,1664]{1,0:T(8,128)(2,1)S(1)}, s16[128,1664]{1,0:T(8,128)(2,1)S(1)}, s16[128,1664]{1,0:T(8,128)(2,1)S(1)}) custom-call(s32[4]{0:T(128)S(1)} %pad_add_fusion.refs_0_.pos_ref, s32[12,24]{1,0:T(8,128)S(1)} %bitcast.14, ...), custom_call_target="tpu_custom_call", output_to_operand_aliasing={{0}: (7, {}), {1}: (8, {}), {2}: (9, {}), {3}: (10, {})} | custom-call | flops 1 | bytes 1 | tf_op jit(solution)/shard_map/pallas_call | solution.py:110
  40.2 0.5 collective-permute-start.9
  40.7 1.2 collective-permute-done.10.refs_6_
  41.9 0.6 collective-permute-done.9.refs_5_
  42.5 7.7 %shard_map.39 = (s16[128,1664]{1,0:T(8,128)(2,1)S(1)}, s16[128,1664]{1,0:T(8,128)(2,1)S(1)}, s16[128,1664]{1,0:T(8,128)(2,1)S(1)}, s16[128,1664]{1,0:T(8,128)(2,1)S(1)}) custom-call(s32[4]{0:T(128)S(1)} %pad_add_fusion.refs_0_.pos_ref, s32[12,24]{1,0:T(8,128)S(1)} %bitcast.15, ...), custom_call_target="tpu_custom_call", output_to_operand_aliasing={{0}: (7, {}), {1}: (8, {}), {2}: (9, {}), {3}: (10, {})} | custom-call | flops 1 | bytes 1 | tf_op jit(solution)/shard_map/pallas_call | solution.py:110
  50.2 2.2 %collective-permute-done.5.refs_3_ = bf16[64,6144]{1,0:T(8,128)(2,1)S(1)} collective-permute-done((bf16[64,6144]{1,0:T(8,128)(2,1)S(1)}, bf16[64,6144]{1,0:T(8,128)(2,1)S(1)}, u32[]{:S(2)}, u32[]{:S(2)}) %collective-permute-start.5) | collective-permute-done | bytes 786464 | tf_op jit(solution)/shard_map/ppermute | solution.py:17
  52.4 2.1 %collective-permute-done.6.refs_4_ = bf16[64,6144]{1,0:T(8,128)(2,1)S(1)} collective-permute-done((bf16[64,6144]{1,0:T(8,128)(2,1)S(1)}, bf16[64,6144]{1,0:T(8,128)(2,1)S(1)}, u32[]{:S(2)}, u32[]{:S(2)}) %collective-permute-start.6) | collective-permute-done | bytes 786464 | tf_op jit(solution)/shard_map/ppermute | solution.py:17
  54.5 0.5 collective-permute-start.14
  55.1 2.0 %collective-permute-start.11 = (bf16[32,6144]{1,0:T(8,128)(2,1)S(1)}, bf16[32,6144]{1,0:T(8,128)(2,1)S(1)}, u32[]{:S(2)}, u32[]{:S(2)}) collective-permute-start(bf16[32,6144]{1,0:T(8,128)(2,1)S(1)} %slice.22), channel_id=1, source_target_pairs={{0,64},{64,128},{128,192},{192,0},{1,65},{65,129},{129,193},{193,1... | collective-permute-start | bytes 1179656 | tf_op jit(solution)/shard_map/ppermute | solution.py:17
  57.1 0.3 collective-permute-start.12
  57.4 1.6 %collective-permute-start.20 = (s16[128,1664]{1,0:T(8,128)(2,1)S(1)}, s16[128,1664]{1,0:T(8,128)(2,1)S(1)}, u32[]{:S(2)}, u32[]{:S(2)}) collective-permute-start(s16[128,1664]{1,0:T(8,128)(2,1)S(1)} %get-tuple-element.71), channel_id=1, source_target_pairs={{0,16},{8,24},{16,0},{24,8},{1,17},{9,25},{17,1},{25,9},{2,18},{10... | collective-permute-start | bytes 1277960 | tf_op jit(solution)/shard_map/ppermute | solution.py:17
  59.0 10.3 %shard_map.40 = (s16[128,1664]{1,0:T(8,128)(2,1)S(1)}, s16[128,1664]{1,0:T(8,128)(2,1)S(1)}, s16[128,1664]{1,0:T(8,128)(2,1)S(1)}, s16[128,1664]{1,0:T(8,128)(2,1)S(1)}) custom-call(s32[4]{0:T(128)S(1)} %pad_add_fusion.refs_0_.pos_ref, s32[12,24]{1,0:T(8,128)S(1)} %bitcast.16, ...), custom_call_target="tpu_custom_call", output_to_operand_aliasing={{0}: (7, {}), {1}: (8, {}), {2}: (9, {}), {3}: (10, {})} | custom-call | flops 1 | bytes 1 | tf_op jit(solution)/shard_map/pallas_call | solution.py:110
  69.4 0.5 collective-permute-start.16
  69.9 0.6 collective-permute-start.21
  70.5 2.7 %collective-permute-start.22 = (s16[128,1664]{1,0:T(8,128)(2,1)S(1)}, s16[128,1664]{1,0:T(8,128)(2,1)S(1)}, u32[]{:S(2)}, u32[]{:S(2)}) collective-permute-start(s16[128,1664]{1,0:T(8,128)(2,1)S(1)} %get-tuple-element.72), channel_id=1, source_target_pairs={{0,24},{8,0},{16,8},{24,16},{1,25},{9,1},{17,9},{25,17},{2,26},{10... | collective-permute-start | bytes 1277960 | tf_op jit(solution)/shard_map/ppermute | solution.py:17
  73.1 7.7 %shard_map.41 = (s16[128,1664]{1,0:T(8,128)(2,1)S(1)}, s16[128,1664]{1,0:T(8,128)(2,1)S(1)}, s16[128,1664]{1,0:T(8,128)(2,1)S(1)}, s16[128,1664]{1,0:T(8,128)(2,1)S(1)}) custom-call(s32[4]{0:T(128)S(1)} %pad_add_fusion.refs_0_.pos_ref, s32[12,24]{1,0:T(8,128)S(1)} %bitcast.17, ...), custom_call_target="tpu_custom_call", output_to_operand_aliasing={{0}: (7, {}), {1}: (8, {}), {2}: (9, {}), {3}: (10, {})} | custom-call | flops 1 | bytes 1 | tf_op jit(solution)/shard_map/pallas_call | solution.py:110
  80.8 0.9 collective-permute-start.17
  81.8 3.1 %collective-permute-start.19 = (s16[128,1664]{1,0:T(8,128)(2,1)S(1)}, s16[128,1664]{1,0:T(8,128)(2,1)S(1)}, u32[]{:S(2)}, u32[]{:S(2)}) collective-permute-start(s16[128,1664]{1,0:T(8,128)(2,1)S(1)} %get-tuple-element.92), channel_id=1, source_target_pairs={{0,24},{8,0},{16,8},{24,16},{1,25},{9,1},{17,9},{25,17},{2,26},{10... | collective-permute-start | bytes 1277960 | tf_op jit(solution)/shard_map/ppermute | solution.py:17
  84.9 7.1 %collective-permute-done.22.refs_3_ = s16[128,1664]{1,0:T(8,128)(2,1)S(1)} collective-permute-done((s16[128,1664]{1,0:T(8,128)(2,1)S(1)}, s16[128,1664]{1,0:T(8,128)(2,1)S(1)}, u32[]{:S(2)}, u32[]{:S(2)}) %collective-permute-start.22) | collective-permute-done | bytes 426016 | tf_op jit(solution)/shard_map/ppermute | solution.py:17
  92.0 1.9 %shard_map.42.refs_4_ = s16[128,1664]{1,0:T(8,128)(2,1)S(1)} custom-call(s16[128,1664]{1,0:T(8,128)(2,1)S(1)} %get-tuple-element.93.refs_0_, s16[128,1664]{1,0:T(8,128)(2,1)S(1)} %collective-permute-done.20.refs_1_, s16[128,1664]{1,0:T(8,128)(2,1)S(1)} %collective-permute-done.21.refs_2_, s16[128,1664]{1,0:T(8,128)(2,1)S(1)} %collective-permute-done.22.refs_3_), custom_call_target="tpu_custom_call" | custom-call | tf_op jit(solution)/shard_map/pallas_call | solution.py:171
  93.9 1.3 collective-permute-done.17.refs_1_
  95.2 7.6 %collective-permute-done.18.refs_2_ = s16[128,1664]{1,0:T(8,128)(2,1)S(1)} collective-permute-done((s16[128,1664]{1,0:T(8,128)(2,1)S(1)}, s16[128,1664]{1,0:T(8,128)(2,1)S(1)}, u32[]{:S(2)}, u32[]{:S(2)}) %collective-permute-start.18) | collective-permute-done | bytes 426016 | tf_op jit(solution)/shard_map/ppermute | solution.py:17
  102.8 2.5 %shard_map.43 = (s16[32,1664]{1,0:T(8,128)(2,1)S(1)}, s16[32,1664]{1,0:T(8,128)(2,1)S(1)}, s16[32,1664]{1,0:T(8,128)(2,1)S(1)}, s16[32,1664]{1,0:T(8,128)(2,1)S(...) custom-call(s32[4]{0:T(128)S(1)} %pad_add_fusion.refs_0_.pos_ref, ...), custom_call_target="tpu_custom_call" | custom-call | tf_op jit(solution)/shard_map/pallas_call | solution.py:197
  105.4 7.0 %collective-permute-start.23 = (s16[32,1664]{1,0:T(8,128)(2,1)S(1)}, s16[32,1664]{1,0:T(8,128)(2,1)S(1)}, u32[]{:S(2)}, u32[]{:S(2)}) collective-permute-start(s16[32,1664]{1,0:T(8,128)(2,1)S(1)} %get-tuple-element.98), channel_id=1, source_target_pairs={{0,4},{1,5},{2,6},{3,7},{4,0},{5,1},{6,2},{7,3},{8,12},{9,13},{10,... | collective-permute-start | bytes 319496 | tf_op jit(solution)/shard_map/ppermute | solution.py:17
  112.4 2.0 %collective-permute-start.24 = (s16[32,1664]{1,0:T(8,128)(2,1)S(1)}, s16[32,1664]{1,0:T(8,128)(2,1)S(1)}, u32[]{:S(2)}, u32[]{:S(2)}) collective-permute-start(s16[32,1664]{1,0:T(8,128)(2,1)S(1)} %get-tuple-element.99), channel_id=1, source_target_pairs={{0,3},{1,4},{2,5},{3,6},{4,7},{5,0},{6,1},{7,2},{8,11},{9,12},{10,... | collective-permute-start | bytes 319496 | tf_op jit(solution)/shard_map/ppermute | solution.py:17
  114.4 3.1 %collective-permute-start.25 = (s16[32,1664]{1,0:T(8,128)(2,1)S(1)}, s16[32,1664]{1,0:T(8,128)(2,1)S(1)}, u32[]{:S(2)}, u32[]{:S(2)}) collective-permute-start(s16[32,1664]{1,0:T(8,128)(2,1)S(1)} %get-tuple-element.100), channel_id=1, source_target_pairs={{0,5},{1,6},{2,7},{3,0},{4,1},{5,2},{6,3},{7,4},{8,13},{9,14},{10,... | collective-permute-start | bytes 319496 | tf_op jit(solution)/shard_map/ppermute | solution.py:17
  117.4 1.5 %collective-permute-start.26 = (s16[32,1664]{1,0:T(8,128)(2,1)S(1)}, s16[32,1664]{1,0:T(8,128)(2,1)S(1)}, u32[]{:S(2)}, u32[]{:S(2)}) collective-permute-start(s16[32,1664]{1,0:T(8,128)(2,1)S(1)} %get-tuple-element.101), channel_id=1, source_target_pairs={{0,2},{1,3},{2,4},{3,5},{4,6},{5,7},{6,0},{7,1},{8,10},{9,11},{10,... | collective-permute-start | bytes 319496 | tf_op jit(solution)/shard_map/ppermute | solution.py:17
  119.0 2.6 %collective-permute-start.27 = (s16[32,1664]{1,0:T(8,128)(2,1)S(1)}, s16[32,1664]{1,0:T(8,128)(2,1)S(1)}, u32[]{:S(2)}, u32[]{:S(2)}) collective-permute-start(s16[32,1664]{1,0:T(8,128)(2,1)S(1)} %get-tuple-element.102), channel_id=1, source_target_pairs={{0,6},{1,7},{2,0},{3,1},{4,2},{5,3},{6,4},{7,5},{8,14},{9,15},{10,... | collective-permute-start | bytes 319496 | tf_op jit(solution)/shard_map/ppermute | solution.py:17
  121.6 1.1 collective-permute-start.28
  122.7 3.9 %collective-permute-done.24.refs_2_ = s16[32,1664]{1,0:T(8,128)(2,1)S(1)} collective-permute-done((s16[32,1664]{1,0:T(8,128)(2,1)S(1)}, s16[32,1664]{1,0:T(8,128)(2,1)S(1)}, u32[]{:S(2)}, u32[]{:S(2)}) %collective-permute-start.24) | collective-permute-done | bytes 106528 | tf_op jit(solution)/shard_map/ppermute | solution.py:17
  126.6 1.1 collective-permute-done.26.refs_4_
  127.7 2.9 %collective-permute-done.27.refs_5_ = s16[32,1664]{1,0:T(8,128)(2,1)S(1)} collective-permute-done((s16[32,1664]{1,0:T(8,128)(2,1)S(1)}, s16[32,1664]{1,0:T(8,128)(2,1)S(1)}, u32[]{:S(2)}, u32[]{:S(2)}) %collective-permute-start.27) | collective-permute-done | bytes 106528 | tf_op jit(solution)/shard_map/ppermute | solution.py:17
  130.6 0.9 collective-permute-done.28.refs_6_
  131.5 0.8 collective-permute-done.29.refs_7_
  132.4 1.4 %shard_map.44 = f32[32,1536]{1,0:T(8,128)} custom-call(s16[32,1664]{1,0:T(8,128)(2,1)S(1)} %get-tuple-element.97.refs_0_, s16[32,1664]{1,0:T(8,128)(2,1)S(1)} %collective-permute-done.23.refs_1_, s16[32,1664]{1,0:T(8,128)(2,1)S(1)} %collective-permute-done.24.refs_2_, s16[32,1664]{1,0:T(8,128)(2,1)S(1)} %collective-permute-done.25.refs_3_, ...), custom_call_target="tpu_custom_call" | custom-call | tf_op jit(solution)/shard_map/pallas_call | solution.py:230
  (34 shorter events, 0.6 us)
Async XLA Ops:
  0.0 4.5 %copy-start.1 = (bf16[128,6144]{1,0:T(8,128)(2,1)S(1)}, bf16[128,6144]{1,0:T(8,128)(2,1)}, u32[]{:S(2)}) copy-start(bf16[128,6144]{1,0:T(8,128)(2,1)} %refs_3_.1) | copy-start | bytes 4718596
  0.0 4.4 %copy-start.2 = (s32[12,1,24]{2,1,0:T(1,128)S(1)}, s32[12,1,24]{2,1,0:T(1,128)}, u32[]{:S(2)}) copy-start(s32[12,1,24]{2,1,0:T(1,128)} %param.5) | copy-start | bytes 3460
  0.0 4.5 %collective-permute-start = (bf16[128,6144]{1,0:T(8,128)(2,1)}, bf16[128,6144]{1,0:T(8,128)(2,1)}, u32[]{:S(2)}, u32[]{:S(2)}) collective-permute-start(bf16[128,6144]{1,0:T(8,128)(2,1)} %refs_3_.1), channel_id=1, source_target_pairs={{0,32},{32,0},{1,33},{33,1},{2,34},{34,2},{3,35},{35,3},{4,36},{36... | collective-permute-start | bytes 4718600 | tf_op jit(solution)/shard_map/ppermute | solution.py:17
  2.2 20.5 %collective-permute-start.1 = (bf16[64,6144]{1,0:T(8,128)(2,1)}, bf16[64,6144]{1,0:T(8,128)(2,1)S(1)}, u32[]{:S(2)}, u32[]{:S(2)}) collective-permute-start(bf16[64,6144]{1,0:T(8,128)(2,1)} %slice.19), channel_id=1, source_target_pairs={{0,64},{64,128},{128,192},{192,0},{1,65},{65,129},{129,193},{193,1... | collective-permute-start | bytes 2359304 | tf_op jit(solution)/shard_map/ppermute | solution.py:17
  3.8 19.7 %collective-permute-start.2 = (bf16[64,6144]{1,0:T(8,128)(2,1)}, bf16[64,6144]{1,0:T(8,128)(2,1)S(1)}, u32[]{:S(2)}, u32[]{:S(2)}) collective-permute-start(bf16[64,6144]{1,0:T(8,128)(2,1)} %slice.19), channel_id=1, source_target_pairs={{0,192},{64,0},{128,64},{192,128},{1,193},{65,1},{129,65},{193,129... | collective-permute-start | bytes 2359304 | tf_op jit(solution)/shard_map/ppermute | solution.py:17
  4.5 3.7 %copy-start = (bf16[12,1,24,128,128]{4,3,2,1,0:T(8,128)(2,1)S(1)}, bf16[12,1,24,128,128]{4,3,2,1,0:T(8,128)(2,1)}, u32[]{:S(2)}) copy-start(bf16[12,1,24,128,128]{4,3,2,1,0:T(8,128)(2,1)} %param.4) | copy-start | bytes 28311556
  23.5 2.9 %collective-permute-start.3 = (bf16[64,6144]{1,0:T(8,128)(2,1)S(1)}, bf16[64,6144]{1,0:T(8,128)(2,1)S(1)}, u32[]{:S(2)}, u32[]{:S(2)}) collective-permute-start(bf16[64,6144]{1,0:T(8,128)(2,1)S(1)} %collective-permute-done.1.refs_3_), channel_id=1, source_target_pairs={{0,32},{32,0},{1,33},{33,1},{2,34},{34,2},{3,35},{35,3},{4,36},{36... | collective-permute-start | bytes 2359304 | tf_op jit(solution)/shard_map/ppermute | solution.py:17
  23.5 3.4 %collective-permute-start.4 = (bf16[64,6144]{1,0:T(8,128)(2,1)S(1)}, bf16[64,6144]{1,0:T(8,128)(2,1)S(1)}, u32[]{:S(2)}, u32[]{:S(2)}) collective-permute-start(bf16[64,6144]{1,0:T(8,128)(2,1)S(1)} %collective-permute-done.2.refs_4_), channel_id=1, source_target_pairs={{0,32},{32,0},{1,33},{33,1},{2,34},{34,2},{3,35},{35,3},{4,36},{36... | collective-permute-start | bytes 2359304 | tf_op jit(solution)/shard_map/ppermute | solution.py:17
  24.1 16.0 %collective-permute-start.7 = (bf16[32,6144]{1,0:T(8,128)(2,1)S(1)}, bf16[32,6144]{1,0:T(8,128)(2,1)S(1)}, u32[]{:S(2)}, u32[]{:S(2)}) collective-permute-start(bf16[32,6144]{1,0:T(8,128)(2,1)S(1)} %slice.20), channel_id=1, source_target_pairs={{0,64},{64,128},{128,192},{192,0},{1,65},{65,129},{129,193},{193,1... | collective-permute-start | bytes 1179656 | tf_op jit(solution)/shard_map/ppermute | solution.py:17
  25.7 14.4 %collective-permute-start.8 = (bf16[32,6144]{1,0:T(8,128)(2,1)S(1)}, bf16[32,6144]{1,0:T(8,128)(2,1)S(1)}, u32[]{:S(2)}, u32[]{:S(2)}) collective-permute-start(bf16[32,6144]{1,0:T(8,128)(2,1)S(1)} %slice.21), channel_id=1, source_target_pairs={{0,192},{64,0},{128,64},{192,128},{1,193},{65,1},{129,65},{193,129... | collective-permute-start | bytes 1179656 | tf_op jit(solution)/shard_map/ppermute | solution.py:17
  26.9 25.5 %collective-permute-start.5 = (bf16[64,6144]{1,0:T(8,128)(2,1)S(1)}, bf16[64,6144]{1,0:T(8,128)(2,1)S(1)}, u32[]{:S(2)}, u32[]{:S(2)}) collective-permute-start(bf16[64,6144]{1,0:T(8,128)(2,1)S(1)} %slice.18), channel_id=1, source_target_pairs={{0,64},{64,128},{128,192},{192,0},{1,65},{65,129},{129,193},{193,1... | collective-permute-start | bytes 2359304 | tf_op jit(solution)/shard_map/ppermute | solution.py:17
  28.8 25.7 %collective-permute-start.6 = (bf16[64,6144]{1,0:T(8,128)(2,1)S(1)}, bf16[64,6144]{1,0:T(8,128)(2,1)S(1)}, u32[]{:S(2)}, u32[]{:S(2)}) collective-permute-start(bf16[64,6144]{1,0:T(8,128)(2,1)S(1)} %slice.18), channel_id=1, source_target_pairs={{0,192},{64,0},{128,64},{192,128},{1,193},{65,1},{129,65},{193,129... | collective-permute-start | bytes 2359304 | tf_op jit(solution)/shard_map/ppermute | solution.py:17
  40.1 1.8 %collective-permute-start.10 = (bf16[32,6144]{1,0:T(8,128)(2,1)S(1)}, bf16[32,6144]{1,0:T(8,128)(2,1)S(1)}, u32[]{:S(2)}, u32[]{:S(2)}) collective-permute-start(bf16[32,6144]{1,0:T(8,128)(2,1)S(1)} %collective-permute-done.8.refs_4_), channel_id=1, source_target_pairs={{0,32},{32,0},{1,33},{33,1},{2,34},{34,2},{3,35},{35,3},{4,36},{36... | collective-permute-start | bytes 1179656 | tf_op jit(solution)/shard_map/ppermute | solution.py:17
  40.2 2.3 %collective-permute-start.9 = (bf16[32,6144]{1,0:T(8,128)(2,1)S(1)}, bf16[32,6144]{1,0:T(8,128)(2,1)S(1)}, u32[]{:S(2)}, u32[]{:S(2)}) collective-permute-start(bf16[32,6144]{1,0:T(8,128)(2,1)S(1)} %collective-permute-done.7.refs_3_), channel_id=1, source_target_pairs={{0,32},{32,0},{1,33},{33,1},{2,34},{34,2},{3,35},{35,3},{4,36},{36... | collective-permute-start | bytes 1179656 | tf_op jit(solution)/shard_map/ppermute | solution.py:17
  54.5 4.5 %collective-permute-start.13 = (bf16[64,6144]{1,0:T(8,128)(2,1)S(1)}, bf16[64,6144]{1,0:T(8,128)(2,1)S(1)}, u32[]{:S(2)}, u32[]{:S(2)}) collective-permute-start(bf16[64,6144]{1,0:T(8,128)(2,1)S(1)} %collective-permute-done.5.refs_3_), channel_id=1, source_target_pairs={{0,32},{32,0},{1,33},{33,1},{2,34},{34,2},{3,35},{35,3},{4,36},{36... | collective-permute-start | bytes 2359304 | tf_op jit(solution)/shard_map/ppermute | solution.py:17
  54.5 4.5 %collective-permute-start.14 = (bf16[64,6144]{1,0:T(8,128)(2,1)S(1)}, bf16[64,6144]{1,0:T(8,128)(2,1)S(1)}, u32[]{:S(2)}, u32[]{:S(2)}) collective-permute-start(bf16[64,6144]{1,0:T(8,128)(2,1)S(1)} %collective-permute-done.6.refs_4_), channel_id=1, source_target_pairs={{0,32},{32,0},{1,33},{33,1},{2,34},{34,2},{3,35},{35,3},{4,36},{36... | collective-permute-start | bytes 2359304 | tf_op jit(solution)/shard_map/ppermute | solution.py:17
  55.1 14.2 %collective-permute-start.11 = (bf16[32,6144]{1,0:T(8,128)(2,1)S(1)}, bf16[32,6144]{1,0:T(8,128)(2,1)S(1)}, u32[]{:S(2)}, u32[]{:S(2)}) collective-permute-start(bf16[32,6144]{1,0:T(8,128)(2,1)S(1)} %slice.22), channel_id=1, source_target_pairs={{0,64},{64,128},{128,192},{192,0},{1,65},{65,129},{129,193},{193,1... | collective-permute-start | bytes 1179656 | tf_op jit(solution)/shard_map/ppermute | solution.py:17
  57.1 12.2 %collective-permute-start.12 = (bf16[32,6144]{1,0:T(8,128)(2,1)S(1)}, bf16[32,6144]{1,0:T(8,128)(2,1)S(1)}, u32[]{:S(2)}, u32[]{:S(2)}) collective-permute-start(bf16[32,6144]{1,0:T(8,128)(2,1)S(1)} %slice.23), channel_id=1, source_target_pairs={{0,192},{64,0},{128,64},{192,128},{1,193},{65,1},{129,65},{193,129... | collective-permute-start | bytes 1179656 | tf_op jit(solution)/shard_map/ppermute | solution.py:17
  57.4 24.4 %collective-permute-start.20 = (s16[128,1664]{1,0:T(8,128)(2,1)S(1)}, s16[128,1664]{1,0:T(8,128)(2,1)S(1)}, u32[]{:S(2)}, u32[]{:S(2)}) collective-permute-start(s16[128,1664]{1,0:T(8,128)(2,1)S(1)} %get-tuple-element.71), channel_id=1, source_target_pairs={{0,16},{8,24},{16,0},{24,8},{1,17},{9,25},{17,1},{25,9},{2,18},{10... | collective-permute-start | bytes 1277960 | tf_op jit(solution)/shard_map/ppermute | solution.py:17
  69.3 3.8 %collective-permute-start.15 = (bf16[32,6144]{1,0:T(8,128)(2,1)S(1)}, bf16[32,6144]{1,0:T(8,128)(2,1)S(1)}, u32[]{:S(2)}, u32[]{:S(2)}) collective-permute-start(bf16[32,6144]{1,0:T(8,128)(2,1)S(1)} %collective-permute-done.11.refs_3_), channel_id=1, source_target_pairs={{0,32},{32,0},{1,33},{33,1},{2,34},{34,2},{3,35},{35,3},{4,36},{36... | collective-permute-start | bytes 1179656 | tf_op jit(solution)/shard_map/ppermute | solution.py:17
  69.4 3.7 %collective-permute-start.16 = (bf16[32,6144]{1,0:T(8,128)(2,1)S(1)}, bf16[32,6144]{1,0:T(8,128)(2,1)S(1)}, u32[]{:S(2)}, u32[]{:S(2)}) collective-permute-start(bf16[32,6144]{1,0:T(8,128)(2,1)S(1)} %collective-permute-done.12.refs_4_), channel_id=1, source_target_pairs={{0,32},{32,0},{1,33},{33,1},{2,34},{34,2},{3,35},{35,3},{4,36},{36... | collective-permute-start | bytes 1179656 | tf_op jit(solution)/shard_map/ppermute | solution.py:17
  69.9 15.0 %collective-permute-start.21 = (s16[128,1664]{1,0:T(8,128)(2,1)S(1)}, s16[128,1664]{1,0:T(8,128)(2,1)S(1)}, u32[]{:S(2)}, u32[]{:S(2)}) collective-permute-start(s16[128,1664]{1,0:T(8,128)(2,1)S(1)} %get-tuple-element.70), channel_id=1, source_target_pairs={{0,8},{8,16},{16,24},{24,0},{1,9},{9,17},{17,25},{25,1},{2,10},{10... | collective-permute-start | bytes 1277960 | tf_op jit(solution)/shard_map/ppermute | solution.py:17
  70.5 21.6 %collective-permute-start.22 = (s16[128,1664]{1,0:T(8,128)(2,1)S(1)}, s16[128,1664]{1,0:T(8,128)(2,1)S(1)}, u32[]{:S(2)}, u32[]{:S(2)}) collective-permute-start(s16[128,1664]{1,0:T(8,128)(2,1)S(1)} %get-tuple-element.72), channel_id=1, source_target_pairs={{0,24},{8,0},{16,8},{24,16},{1,25},{9,1},{17,9},{25,17},{2,26},{10... | collective-permute-start | bytes 1277960 | tf_op jit(solution)/shard_map/ppermute | solution.py:17
  80.8 14.4 %collective-permute-start.17 = (s16[128,1664]{1,0:T(8,128)(2,1)S(1)}, s16[128,1664]{1,0:T(8,128)(2,1)S(1)}, u32[]{:S(2)}, u32[]{:S(2)}) collective-permute-start(s16[128,1664]{1,0:T(8,128)(2,1)S(1)} %get-tuple-element.90), channel_id=1, source_target_pairs={{0,16},{8,24},{16,0},{24,8},{1,17},{9,25},{17,1},{25,9},{2,18},{10... | collective-permute-start | bytes 1277960 | tf_op jit(solution)/shard_map/ppermute | solution.py:17
  81.7 21.1 %collective-permute-start.18 = (s16[128,1664]{1,0:T(8,128)(2,1)S(1)}, s16[128,1664]{1,0:T(8,128)(2,1)S(1)}, u32[]{:S(2)}, u32[]{:S(2)}) collective-permute-start(s16[128,1664]{1,0:T(8,128)(2,1)S(1)} %get-tuple-element.91), channel_id=1, source_target_pairs={{0,8},{8,16},{16,24},{24,0},{1,9},{9,17},{17,25},{25,1},{2,10},{10... | collective-permute-start | bytes 1277960 | tf_op jit(solution)/shard_map/ppermute | solution.py:17
  81.8 21.0 %collective-permute-start.19 = (s16[128,1664]{1,0:T(8,128)(2,1)S(1)}, s16[128,1664]{1,0:T(8,128)(2,1)S(1)}, u32[]{:S(2)}, u32[]{:S(2)}) collective-permute-start(s16[128,1664]{1,0:T(8,128)(2,1)S(1)} %get-tuple-element.92), channel_id=1, source_target_pairs={{0,24},{8,0},{16,8},{24,16},{1,25},{9,1},{17,9},{25,17},{2,26},{10... | collective-permute-start | bytes 1277960 | tf_op jit(solution)/shard_map/ppermute | solution.py:17
  105.4 16.2 %collective-permute-start.23 = (s16[32,1664]{1,0:T(8,128)(2,1)S(1)}, s16[32,1664]{1,0:T(8,128)(2,1)S(1)}, u32[]{:S(2)}, u32[]{:S(2)}) collective-permute-start(s16[32,1664]{1,0:T(8,128)(2,1)S(1)} %get-tuple-element.98), channel_id=1, source_target_pairs={{0,4},{1,5},{2,6},{3,7},{4,0},{5,1},{6,2},{7,3},{8,12},{9,13},{10,... | collective-permute-start | bytes 319496 | tf_op jit(solution)/shard_map/ppermute | solution.py:17
  112.4 14.2 %collective-permute-start.24 = (s16[32,1664]{1,0:T(8,128)(2,1)S(1)}, s16[32,1664]{1,0:T(8,128)(2,1)S(1)}, u32[]{:S(2)}, u32[]{:S(2)}) collective-permute-start(s16[32,1664]{1,0:T(8,128)(2,1)S(1)} %get-tuple-element.99), channel_id=1, source_target_pairs={{0,3},{1,4},{2,5},{3,6},{4,7},{5,0},{6,1},{7,2},{8,11},{9,12},{10,... | collective-permute-start | bytes 319496 | tf_op jit(solution)/shard_map/ppermute | solution.py:17
  114.4 12.2 %collective-permute-start.25 = (s16[32,1664]{1,0:T(8,128)(2,1)S(1)}, s16[32,1664]{1,0:T(8,128)(2,1)S(1)}, u32[]{:S(2)}, u32[]{:S(2)}) collective-permute-start(s16[32,1664]{1,0:T(8,128)(2,1)S(1)} %get-tuple-element.100), channel_id=1, source_target_pairs={{0,5},{1,6},{2,7},{3,0},{4,1},{5,2},{6,3},{7,4},{8,13},{9,14},{10,... | collective-permute-start | bytes 319496 | tf_op jit(solution)/shard_map/ppermute | solution.py:17
  117.4 10.3 %collective-permute-start.26 = (s16[32,1664]{1,0:T(8,128)(2,1)S(1)}, s16[32,1664]{1,0:T(8,128)(2,1)S(1)}, u32[]{:S(2)}, u32[]{:S(2)}) collective-permute-start(s16[32,1664]{1,0:T(8,128)(2,1)S(1)} %get-tuple-element.101), channel_id=1, source_target_pairs={{0,2},{1,3},{2,4},{3,5},{4,6},{5,7},{6,0},{7,1},{8,10},{9,11},{10,... | collective-permute-start | bytes 319496 | tf_op jit(solution)/shard_map/ppermute | solution.py:17
  119.0 11.6 %collective-permute-start.27 = (s16[32,1664]{1,0:T(8,128)(2,1)S(1)}, s16[32,1664]{1,0:T(8,128)(2,1)S(1)}, u32[]{:S(2)}, u32[]{:S(2)}) collective-permute-start(s16[32,1664]{1,0:T(8,128)(2,1)S(1)} %get-tuple-element.102), channel_id=1, source_target_pairs={{0,6},{1,7},{2,0},{3,1},{4,2},{5,3},{6,4},{7,5},{8,14},{9,15},{10,... | collective-permute-start | bytes 319496 | tf_op jit(solution)/shard_map/ppermute | solution.py:17
  121.6 9.9 %collective-permute-start.28 = (s16[32,1664]{1,0:T(8,128)(2,1)S(1)}, s16[32,1664]{1,0:T(8,128)(2,1)S(1)}, u32[]{:S(2)}, u32[]{:S(2)}) collective-permute-start(s16[32,1664]{1,0:T(8,128)(2,1)S(1)} %get-tuple-element.103), channel_id=1, source_target_pairs={{0,1},{1,2},{2,3},{3,4},{4,5},{5,6},{6,7},{7,0},{8,9},{9,10},{10,1... | collective-permute-start | bytes 319496 | tf_op jit(solution)/shard_map/ppermute | solution.py:17
  126.6 5.8 %collective-permute-start.29 = (s16[32,1664]{1,0:T(8,128)(2,1)S(1)}, s16[32,1664]{1,0:T(8,128)(2,1)S(1)}, u32[]{:S(2)}, u32[]{:S(2)}) collective-permute-start(s16[32,1664]{1,0:T(8,128)(2,1)S(1)} %get-tuple-element.104), channel_id=1, source_target_pairs={{0,7},{1,0},{2,1},{3,2},{4,3},{5,4},{6,5},{7,6},{8,15},{9,8},{10,9... | collective-permute-start | bytes 319496 | tf_op jit(solution)/shard_map/ppermute | solution.py:17

commit v6 on v5

--- a/solution.py
+++ b/solution.py
@@ -44,10 +44,10 @@
 
     def body(*refs):
         pos_ref, cd_ref = refs[:2]
-        w_hbm = refs[2]
+        w_ref = refs[2]
         a_hbm = refs[3 : 3 + n_arr]
         outs = refs[3 + n_arr + n_in : 3 + n_arr + n_in + n_out]
-        wv, av, ov, tot, codes, wsem, asem, osem = refs[3 + n_arr + n_in + n_out :]
+        av, ov, tot, codes, asem, osem = refs[3 + n_arr + n_in + n_out :]
 
         def load(i):
             b = blocks[i]
@@ -55,14 +55,8 @@
                 a_hbm[where[i]].at[pl.ds(b[1], b[2]), :], av.at[pl.ds(starts[i], b[2]), :], asem.at[i]
             )
 
-        def load_weights(t):
-            return pltpu.make_async_copy(w_hbm.at[t], wv.at[t], wsem.at[t])
-
-        load_weights(0).start()
         for i in range(n_blk):
             load(i).start()
-        for t in range(1, n_tiles):
-            load_weights(t).start()
         for i in range(n_blk):
             load(i).wait()
         codes[...] = jnp.zeros_like(codes)
@@ -75,9 +69,8 @@
             codes[...] = jnp.where(lane == t, code, codes[...])
 
         def one_tile(t, carry):
-            load_weights(t).wait()
             put(t - 1, pl.multiple_of(jnp.maximum(t - 1, 0) * TILE, TILE))
-            weights = jnp.concatenate([wv[t, k] for k in range(n_slots)], axis=1)
+            weights = jnp.concatenate([w_ref[t, k] for k in range(n_slots)], axis=1)
             picked = jnp.concatenate(
                 [av[:, pl.ds(pl.multiple_of(cd_ref[t, k] * TILE, TILE), TILE)] for k in range(n_slots)], axis=1
             )
@@ -115,21 +108,19 @@
         grid_spec=pltpu.PrefetchScalarGridSpec(
             num_scalar_prefetch=2,
             grid=(1,),
-            in_specs=[hbm] * (1 + n_arr + n_in),
+            in_specs=[pl.BlockSpec(memory_space=pltpu.VMEM)] + [hbm] * (n_arr + n_in),
             out_specs=[hbm] * n_out,
             scratch_shapes=[
-                pltpu.VMEM(integrals.shape, integrals.dtype),
                 pltpu.VMEM((rows, depth), blocks[0][0].dtype),
                 pltpu.VMEM((rows, width + TILE), jnp.int16),
                 pltpu.VMEM((rows, TILE), jnp.float32),
                 pltpu.VMEM((rows, TILE), jnp.float32),
-                pltpu.SemaphoreType.DMA((n_tiles,)),
                 pltpu.SemaphoreType.DMA((n_blk,)),
                 pltpu.SemaphoreType.DMA((n_blk,)),
             ],
         ),
         input_output_aliases={} if partial is None else {3 + n_arr + s: s for s in range(n_out)},
-        compiler_params=pltpu.CompilerParams(vmem_limit_bytes=20 << 20),
+        compiler_params=pltpu.CompilerParams(vmem_limit_bytes=10 << 20),
         cost_estimate=pl.CostEstimate(flops=1, transcendentals=0, bytes_accessed=1),
     )(pos, cd_tiles, integrals, *arrays, *(partial or ()))
 
@@ -273,12 +264,12 @@
     ]
     coded = contract(pos, cd_tiles, integrals, blocks, heights)
     coded_1, coded_2 = coded[:4], coded[4:]
-    part_2 = rows_of(after(amplitudes, coded_1), 1)
 
     def far(chunk, pair, core):
         lo, hi = pair
         return [(lo, 0, lo.shape[0], chunk, 2, core, 0), (hi, 0, hi.shape[0], chunk, 2, core, lo.shape[0])]
 
+    part_2 = rows_of(after(amplitudes, coded_1), 1)
     near_1 = after(near_1, coded_1)
     far_1 = y_far(*near_1)
     near_1_other = swap(near_1)
@@ -292,8 +283,11 @@
 
     coded_2 = after(coded_2, coded_1)
     near_2 = after(near_2, coded_1)
-    far_2 = y_far(*near_2)
-    blocks = near(0, near_2, 0) + near(0, swap(near_2), 1)
+    half = heights[1] // 2
+    far_2 = near_2[0][:half], near_2[1][half:]
+    near_2_other = swap(after(near_2, far_2))
+    far_2 = shift(far_2[0], "y", NY, 1), shift(far_2[1], "y", NY, -1)
+    blocks = near(0, near_2, 0) + near(0, near_2_other, 1)
     coded_2 = contract(pos, cd_tiles, integrals, blocks, heights[1:], coded_2)
     far_2 = after(far_2, coded_2)
     far_2_other = swap(far_2)

time: 136 us -> 134 us (0.985)
  Pallas kernels: 52.7 us -> 49.7 us
  waiting for transfers between devices: 36.7 us -> 38.2 us
    pallas_call x5, Pallas kernels: 46.9 us -> 43.9 us  [contract(): pl.pallas_call(body, out_shape=[jax.ShapeDtypeStruct((NC * h, width + TIL...]
    ppermute x30, waiting for transfers between devices: 36.7 us -> 38.2 us  [shift(): lax.ppermute(value, axis, [(i, (i + step) % size) for i in range(size)])]
    unnamed x7 -> x9, local copies, waits for them, and re-layouts: 3.69 us -> 3.69 us
  transfers between devices with their start and end apart: 30 -> 30, of which waited for: 15 -> 15; matrix products, arithmetic and copies ran while one was open for 2% -> 2% of each run, Pallas kernels for 37% -> 35%
where the time goes in v6:
time: 134 us; the launch traced here: 132 us
  Pallas kernels  49.7 us (37%)
  waiting for transfers between devices  38.2 us (29%)
  starting transfers between devices  37.8 us (28%)
  local copies, waits for them, and re-layouts  6.03 us (4%)
    pallas_call x5, Pallas kernels, contract(): pl.pallas_call(body, out_shape=[jax.ShapeDtypeStruct((NC * h, width + TIL...  43.9 us
    ppermute x30, waiting for transfers between devices, shift(): lax.ppermute(value, axis, [(i, (i + step) % size) for i in range(size)])  38.2 us
    ppermute x30, starting transfers between devices, shift(): lax.ppermute(value, axis, [(i, (i + step) % size) for i in range(size)])  37.8 us
    unnamed x9, local copies, waits for them, and re-layouts  3.69 us
  transfers between devices with their start and end apart: 30, of which 15 were waited for; matrix products, arithmetic and copies ran while one was open for 2% of the time, Pallas kernels for 35%

profile of v6, /device:TPU:8, one launch (start us, length us, event | category | flops | bytes accessed | tf_op | source)
XLA Modules:
  0.0 132.0 jit_solution(5736308124518307093)
XLA Ops:
  0.0 2.2 %slice.19 = bf16[64,6144]{1,0:T(8,128)(2,1)} slice(bf16[128,6144]{1,0:T(8,128)(2,1)} %refs_3_.1), slice={[0:64], [0:6144]} | slice | bytes 1572864 | tf_op jit(solution)/shard_map/slice | solution.py:258
  2.2 1.6 %collective-permute-start.1 = (bf16[64,6144]{1,0:T(8,128)(2,1)}, bf16[64,6144]{1,0:T(8,128)(2,1)S(1)}, u32[]{:S(2)}, u32[]{:S(2)}) collective-permute-start(bf16[64,6144]{1,0:T(8,128)(2,1)} %slice.19), channel_id=1, source_target_pairs={{0,64},{64,128},{128,192},{192,0},{1,65},{65,129},{129,193},{193,1... | collective-permute-start | bytes 2359304 | tf_op jit(solution)/shard_map/ppermute | solution.py:17
  3.8 0.6 collective-permute-start.2
  4.5 3.7 %copy-done = bf16[12,1,24,128,128]{4,3,2,1,0:T(8,128)(2,1)S(1)} copy-done((bf16[12,1,24,128,128]{4,3,2,1,0:T(8,128)(2,1)S(1)}, bf16[12,1,24,128,128]{4,3,2,1,0:T(8,128)(2,1)}, u32[]{:S(2)}) %copy-start) | copy-done | bytes 9437208
  8.2 11.0 %shard_map.37 = (s16[128,1664]{1,0:T(8,128)(2,1)S(1)}, s16[128,1664]{1,0:T(8,128)(2,1)S(1)}, s16[128,1664]{1,0:T(8,128)(2,1)S(1)}, s16[128,1664]{1,0:T(8,128)(2,...) custom-call(s32[4]{0:T(128)S(1)} %pad_add_fusion.refs_0_.pos_ref, ...), custom_call_target="tpu_custom_call" | custom-call | flops 1 | bytes 1 | tf_op jit(solution)/shard_map/pallas_call | solution.py:103
  19.2 3.5 %collective-permute-done.1.refs_3_ = bf16[64,6144]{1,0:T(8,128)(2,1)S(1)} collective-permute-done((bf16[64,6144]{1,0:T(8,128)(2,1)}, bf16[64,6144]{1,0:T(8,128)(2,1)S(1)}, u32[]{:S(2)}, u32[]{:S(2)}) %collective-permute-start.1) | collective-permute-done | bytes 786464 | tf_op jit(solution)/shard_map/ppermute | solution.py:17
  22.7 0.9 collective-permute-done.2.refs_4_
  23.5 0.5 collective-permute-start.4
  24.1 1.6 %collective-permute-start.7 = (bf16[32,6144]{1,0:T(8,128)(2,1)S(1)}, bf16[32,6144]{1,0:T(8,128)(2,1)S(1)}, u32[]{:S(2)}, u32[]{:S(2)}) collective-permute-start(bf16[32,6144]{1,0:T(8,128)(2,1)S(1)} %slice.20), channel_id=1, source_target_pairs={{0,64},{64,128},{128,192},{192,0},{1,65},{65,129},{129,193},{193,1... | collective-permute-start | bytes 1179656 | tf_op jit(solution)/shard_map/ppermute | solution.py:17
  25.7 0.7 collective-permute-start.8
  26.4 0.5 collective-permute-done.4.refs_6_
  26.9 1.9 %collective-permute-start.5 = (bf16[64,6144]{1,0:T(8,128)(2,1)S(1)}, bf16[64,6144]{1,0:T(8,128)(2,1)S(1)}, u32[]{:S(2)}, u32[]{:S(2)}) collective-permute-start(bf16[64,6144]{1,0:T(8,128)(2,1)S(1)} %slice.18), channel_id=1, source_target_pairs={{0,64},{64,128},{128,192},{192,0},{1,65},{65,129},{129,193},{193,1... | collective-permute-start | bytes 2359304 | tf_op jit(solution)/shard_map/ppermute | solution.py:17
  28.8 1.0 collective-permute-start.6
  29.8 9.5 %shard_map.38 = (s16[128,1664]{1,0:T(8,128)(2,1)S(1)}, s16[128,1664]{1,0:T(8,128)(2,1)S(1)}, s16[128,1664]{1,0:T(8,128)(2,1)S(1)}, s16[128,1664]{1,0:T(8,128)(2,1)S(1)}) custom-call(s32[4]{0:T(128)S(1)} %pad_add_fusion.refs_0_.pos_ref, s32[12,24]{1,0:T(8,128)S(1)} %bitcast.14, ...), custom_call_target="tpu_custom_call", output_to_operand_aliasing={{0}: (7, {}), {1}: (8, {}), {2}: (9, {}), {3}: (10, {})} | custom-call | flops 1 | bytes 1 | tf_op jit(solution)/shard_map/pallas_call | solution.py:103
  39.4 0.5 collective-permute-start.9
  39.9 1.2 collective-permute-done.10.refs_6_
  41.1 0.6 collective-permute-done.9.refs_5_
  41.7 7.0 %shard_map.39 = (s16[128,1664]{1,0:T(8,128)(2,1)S(1)}, s16[128,1664]{1,0:T(8,128)(2,1)S(1)}, s16[128,1664]{1,0:T(8,128)(2,1)S(1)}, s16[128,1664]{1,0:T(8,128)(2,1)S(1)}) custom-call(s32[4]{0:T(128)S(1)} %pad_add_fusion.refs_0_.pos_ref, s32[12,24]{1,0:T(8,128)S(1)} %bitcast.15, ...), custom_call_target="tpu_custom_call", output_to_operand_aliasing={{0}: (7, {}), {1}: (8, {}), {2}: (9, {}), {3}: (10, {})} | custom-call | flops 1 | bytes 1 | tf_op jit(solution)/shard_map/pallas_call | solution.py:103
  48.6 3.8 %collective-permute-done.5.refs_3_ = bf16[64,6144]{1,0:T(8,128)(2,1)S(1)} collective-permute-done((bf16[64,6144]{1,0:T(8,128)(2,1)S(1)}, bf16[64,6144]{1,0:T(8,128)(2,1)S(1)}, u32[]{:S(2)}, u32[]{:S(2)}) %collective-permute-start.5) | collective-permute-done | bytes 786464 | tf_op jit(solution)/shard_map/ppermute | solution.py:17
  52.4 2.1 %collective-permute-done.6.refs_4_ = bf16[64,6144]{1,0:T(8,128)(2,1)S(1)} collective-permute-done((bf16[64,6144]{1,0:T(8,128)(2,1)S(1)}, bf16[64,6144]{1,0:T(8,128)(2,1)S(1)}, u32[]{:S(2)}, u32[]{:S(2)}) %collective-permute-start.6) | collective-permute-done | bytes 786464 | tf_op jit(solution)/shard_map/ppermute | solution.py:17
  54.6 0.5 collective-permute-start.14
  55.1 1.7 %collective-permute-start.11 = (bf16[32,6144]{1,0:T(8,128)(2,1)S(1)}, bf16[32,6144]{1,0:T(8,128)(2,1)S(1)}, u32[]{:S(2)}, u32[]{:S(2)}) collective-permute-start(bf16[32,6144]{1,0:T(8,128)(2,1)S(1)} %slice.22), channel_id=1, source_target_pairs={{0,64},{64,128},{128,192},{192,0},{1,65},{65,129},{129,193},{193,1... | collective-permute-start | bytes 1179656 | tf_op jit(solution)/shard_map/ppermute | solution.py:17
  56.9 0.3 collective-permute-start.12
  57.2 1.6 %collective-permute-start.20 = (s16[128,1664]{1,0:T(8,128)(2,1)S(1)}, s16[128,1664]{1,0:T(8,128)(2,1)S(1)}, u32[]{:S(2)}, u32[]{:S(2)}) collective-permute-start(s16[128,1664]{1,0:T(8,128)(2,1)S(1)} %get-tuple-element.73), channel_id=1, source_target_pairs={{0,16},{8,24},{16,0},{24,8},{1,17},{9,25},{17,1},{25,9},{2,18},{10... | collective-permute-start | bytes 1277960 | tf_op jit(solution)/shard_map/ppermute | solution.py:17
  58.8 9.5 %shard_map.40 = (s16[128,1664]{1,0:T(8,128)(2,1)S(1)}, s16[128,1664]{1,0:T(8,128)(2,1)S(1)}, s16[128,1664]{1,0:T(8,128)(2,1)S(1)}, s16[128,1664]{1,0:T(8,128)(2,1)S(1)}) custom-call(s32[4]{0:T(128)S(1)} %pad_add_fusion.refs_0_.pos_ref, s32[12,24]{1,0:T(8,128)S(1)} %bitcast.16, ...), custom_call_target="tpu_custom_call", output_to_operand_aliasing={{0}: (7, {}), {1}: (8, {}), {2}: (9, {}), {3}: (10, {})} | custom-call | flops 1 | bytes 1 | tf_op jit(solution)/shard_map/pallas_call | solution.py:103
  68.4 0.5 collective-permute-start.16
  68.9 0.7 collective-permute-start.21
  69.6 2.6 %collective-permute-start.22 = (s16[128,1664]{1,0:T(8,128)(2,1)S(1)}, s16[128,1664]{1,0:T(8,128)(2,1)S(1)}, u32[]{:S(2)}, u32[]{:S(2)}) collective-permute-start(s16[128,1664]{1,0:T(8,128)(2,1)S(1)} %get-tuple-element.74), channel_id=1, source_target_pairs={{0,24},{8,0},{16,8},{24,16},{1,25},{9,1},{17,9},{25,17},{2,26},{10... | collective-permute-start | bytes 1277960 | tf_op jit(solution)/shard_map/ppermute | solution.py:17
  72.1 7.0 %shard_map.41 = (s16[128,1664]{1,0:T(8,128)(2,1)S(1)}, s16[128,1664]{1,0:T(8,128)(2,1)S(1)}, s16[128,1664]{1,0:T(8,128)(2,1)S(1)}, s16[128,1664]{1,0:T(8,128)(2,1)S(1)}) custom-call(s32[4]{0:T(128)S(1)} %pad_add_fusion.refs_0_.pos_ref, s32[12,24]{1,0:T(8,128)S(1)} %bitcast.17, ...), custom_call_target="tpu_custom_call", output_to_operand_aliasing={{0}: (7, {}), {1}: (8, {}), {2}: (9, {}), {3}: (10, {})} | custom-call | flops 1 | bytes 1 | tf_op jit(solution)/shard_map/pallas_call | solution.py:103
  79.1 0.9 collective-permute-start.17
  80.0 3.2 %collective-permute-start.19 = (s16[128,1664]{1,0:T(8,128)(2,1)S(1)}, s16[128,1664]{1,0:T(8,128)(2,1)S(1)}, u32[]{:S(2)}, u32[]{:S(2)}) collective-permute-start(s16[128,1664]{1,0:T(8,128)(2,1)S(1)} %get-tuple-element.96), channel_id=1, source_target_pairs={{0,24},{8,0},{16,8},{24,16},{1,25},{9,1},{17,9},{25,17},{2,26},{10... | collective-permute-start | bytes 1277960 | tf_op jit(solution)/shard_map/ppermute | solution.py:17
  83.2 8.1 %collective-permute-done.22.refs_3_ = s16[128,1664]{1,0:T(8,128)(2,1)S(1)} collective-permute-done((s16[128,1664]{1,0:T(8,128)(2,1)S(1)}, s16[128,1664]{1,0:T(8,128)(2,1)S(1)}, u32[]{:S(2)}, u32[]{:S(2)}) %collective-permute-start.22) | collective-permute-done | bytes 426016 | tf_op jit(solution)/shard_map/ppermute | solution.py:17
  91.3 1.9 %shard_map.42.refs_4_ = s16[128,1664]{1,0:T(8,128)(2,1)S(1)} custom-call(s16[128,1664]{1,0:T(8,128)(2,1)S(1)} %get-tuple-element.97.refs_0_, s16[128,1664]{1,0:T(8,128)(2,1)S(1)} %collective-permute-done.20.refs_1_, s16[128,1664]{1,0:T(8,128)(2,1)S(1)} %collective-permute-done.21.refs_2_, s16[128,1664]{1,0:T(8,128)(2,1)S(1)} %collective-permute-done.22.refs_3_), custom_call_target="tpu_custom_call" | custom-call | tf_op jit(solution)/shard_map/pallas_call | solution.py:162
  93.2 0.3 collective-permute-done.17.refs_1_
  93.5 7.6 %collective-permute-done.18.refs_2_ = s16[128,1664]{1,0:T(8,128)(2,1)S(1)} collective-permute-done((s16[128,1664]{1,0:T(8,128)(2,1)S(1)}, s16[128,1664]{1,0:T(8,128)(2,1)S(1)}, u32[]{:S(2)}, u32[]{:S(2)}) %collective-permute-start.18) | collective-permute-done | bytes 426016 | tf_op jit(solution)/shard_map/ppermute | solution.py:17
  101.1 2.5 %shard_map.43 = (s16[32,1664]{1,0:T(8,128)(2,1)S(1)}, s16[32,1664]{1,0:T(8,128)(2,1)S(1)}, s16[32,1664]{1,0:T(8,128)(2,1)S(1)}, s16[32,1664]{1,0:T(8,128)(2,1)S(...) custom-call(s32[4]{0:T(128)S(1)} %pad_add_fusion.refs_0_.pos_ref, ...), custom_call_target="tpu_custom_call" | custom-call | tf_op jit(solution)/shard_map/pallas_call | solution.py:188
  103.7 7.0 %collective-permute-start.23 = (s16[32,1664]{1,0:T(8,128)(2,1)S(1)}, s16[32,1664]{1,0:T(8,128)(2,1)S(1)}, u32[]{:S(2)}, u32[]{:S(2)}) collective-permute-start(s16[32,1664]{1,0:T(8,128)(2,1)S(1)} %get-tuple-element.102), channel_id=1, source_target_pairs={{0,4},{1,5},{2,6},{3,7},{4,0},{5,1},{6,2},{7,3},{8,12},{9,13},{10,... | collective-permute-start | bytes 319496 | tf_op jit(solution)/shard_map/ppermute | solution.py:17
  110.7 1.9 %collective-permute-start.24 = (s16[32,1664]{1,0:T(8,128)(2,1)S(1)}, s16[32,1664]{1,0:T(8,128)(2,1)S(1)}, u32[]{:S(2)}, u32[]{:S(2)}) collective-permute-start(s16[32,1664]{1,0:T(8,128)(2,1)S(1)} %get-tuple-element.103), channel_id=1, source_target_pairs={{0,3},{1,4},{2,5},{3,6},{4,7},{5,0},{6,1},{7,2},{8,11},{9,12},{10,... | collective-permute-start | bytes 319496 | tf_op jit(solution)/shard_map/ppermute | solution.py:17
  112.7 3.1 %collective-permute-start.25 = (s16[32,1664]{1,0:T(8,128)(2,1)S(1)}, s16[32,1664]{1,0:T(8,128)(2,1)S(1)}, u32[]{:S(2)}, u32[]{:S(2)}) collective-permute-start(s16[32,1664]{1,0:T(8,128)(2,1)S(1)} %get-tuple-element.104), channel_id=1, source_target_pairs={{0,5},{1,6},{2,7},{3,0},{4,1},{5,2},{6,3},{7,4},{8,13},{9,14},{10,... | collective-permute-start | bytes 319496 | tf_op jit(solution)/shard_map/ppermute | solution.py:17
  115.7 1.5 %collective-permute-start.26 = (s16[32,1664]{1,0:T(8,128)(2,1)S(1)}, s16[32,1664]{1,0:T(8,128)(2,1)S(1)}, u32[]{:S(2)}, u32[]{:S(2)}) collective-permute-start(s16[32,1664]{1,0:T(8,128)(2,1)S(1)} %get-tuple-element.105), channel_id=1, source_target_pairs={{0,2},{1,3},{2,4},{3,5},{4,6},{5,7},{6,0},{7,1},{8,10},{9,11},{10,... | collective-permute-start | bytes 319496 | tf_op jit(solution)/shard_map/ppermute | solution.py:17
  117.3 2.6 %collective-permute-start.27 = (s16[32,1664]{1,0:T(8,128)(2,1)S(1)}, s16[32,1664]{1,0:T(8,128)(2,1)S(1)}, u32[]{:S(2)}, u32[]{:S(2)}) collective-permute-start(s16[32,1664]{1,0:T(8,128)(2,1)S(1)} %get-tuple-element.106), channel_id=1, source_target_pairs={{0,6},{1,7},{2,0},{3,1},{4,2},{5,3},{6,4},{7,5},{8,14},{9,15},{10,... | collective-permute-start | bytes 319496 | tf_op jit(solution)/shard_map/ppermute | solution.py:17
  119.9 1.0 collective-permute-start.28
  120.9 4.0 %collective-permute-done.24.refs_2_ = s16[32,1664]{1,0:T(8,128)(2,1)S(1)} collective-permute-done((s16[32,1664]{1,0:T(8,128)(2,1)S(1)}, s16[32,1664]{1,0:T(8,128)(2,1)S(1)}, u32[]{:S(2)}, u32[]{:S(2)}) %collective-permute-start.24) | collective-permute-done | bytes 106528 | tf_op jit(solution)/shard_map/ppermute | solution.py:17
  125.0 1.1 collective-permute-done.26.refs_4_
  126.0 2.7 %collective-permute-done.27.refs_5_ = s16[32,1664]{1,0:T(8,128)(2,1)S(1)} collective-permute-done((s16[32,1664]{1,0:T(8,128)(2,1)S(1)}, s16[32,1664]{1,0:T(8,128)(2,1)S(1)}, u32[]{:S(2)}, u32[]{:S(2)}) %collective-permute-start.27) | collective-permute-done | bytes 106528 | tf_op jit(solution)/shard_map/ppermute | solution.py:17
  128.7 1.2 collective-permute-done.28.refs_6_
  129.9 0.8 collective-permute-done.29.refs_7_
  130.6 1.4 %shard_map.44 = f32[32,1536]{1,0:T(8,128)} custom-call(s16[32,1664]{1,0:T(8,128)(2,1)S(1)} %get-tuple-element.101.refs_0_, s16[32,1664]{1,0:T(8,128)(2,1)S(1)} %collective-permute-done.23.refs_1_, s16[32,1664]{1,0:T(8,128)(2,1)S(1)} %collective-permute-done.24.refs_2_, s16[32,1664]{1,0:T(8,128)(2,1)S(1)} %collective-permute-done.25.refs_3_, ...), custom_call_target="tpu_custom_call" | custom-call | tf_op jit(solution)/shard_map/pallas_call | solution.py:221
  (36 shorter events, 0.6 us)
Async XLA Ops:
  0.0 4.5 %copy-start.2 = (bf16[128,6144]{1,0:T(8,128)(2,1)S(1)}, bf16[128,6144]{1,0:T(8,128)(2,1)}, u32[]{:S(2)}) copy-start(bf16[128,6144]{1,0:T(8,128)(2,1)} %refs_3_.1) | copy-start | bytes 4718596
  0.0 4.4 %copy-start.3 = (s32[12,1,24]{2,1,0:T(1,128)S(1)}, s32[12,1,24]{2,1,0:T(1,128)}, u32[]{:S(2)}) copy-start(s32[12,1,24]{2,1,0:T(1,128)} %param.5) | copy-start | bytes 3460
  0.0 4.5 %collective-permute-start = (bf16[128,6144]{1,0:T(8,128)(2,1)}, bf16[128,6144]{1,0:T(8,128)(2,1)}, u32[]{:S(2)}, u32[]{:S(2)}) collective-permute-start(bf16[128,6144]{1,0:T(8,128)(2,1)} %refs_3_.1), channel_id=1, source_target_pairs={{0,32},{32,0},{1,33},{33,1},{2,34},{34,2},{3,35},{35,3},{4,36},{36... | collective-permute-start | bytes 4718600 | tf_op jit(solution)/shard_map/ppermute | solution.py:17
  2.2 20.5 %collective-permute-start.1 = (bf16[64,6144]{1,0:T(8,128)(2,1)}, bf16[64,6144]{1,0:T(8,128)(2,1)S(1)}, u32[]{:S(2)}, u32[]{:S(2)}) collective-permute-start(bf16[64,6144]{1,0:T(8,128)(2,1)} %slice.19), channel_id=1, source_target_pairs={{0,64},{64,128},{128,192},{192,0},{1,65},{65,129},{129,193},{193,1... | collective-permute-start | bytes 2359304 | tf_op jit(solution)/shard_map/ppermute | solution.py:17
  3.8 19.7 %collective-permute-start.2 = (bf16[64,6144]{1,0:T(8,128)(2,1)}, bf16[64,6144]{1,0:T(8,128)(2,1)S(1)}, u32[]{:S(2)}, u32[]{:S(2)}) collective-permute-start(bf16[64,6144]{1,0:T(8,128)(2,1)} %slice.19), channel_id=1, source_target_pairs={{0,192},{64,0},{128,64},{192,128},{1,193},{65,1},{129,65},{193,129... | collective-permute-start | bytes 2359304 | tf_op jit(solution)/shard_map/ppermute | solution.py:17
  4.5 3.7 %copy-start = (bf16[12,1,24,128,128]{4,3,2,1,0:T(8,128)(2,1)S(1)}, bf16[12,1,24,128,128]{4,3,2,1,0:T(8,128)(2,1)}, u32[]{:S(2)}) copy-start(bf16[12,1,24,128,128]{4,3,2,1,0:T(8,128)(2,1)} %param.4) | copy-start | bytes 28311556
  8.2 21.6 %copy-start.1 = (bf16[12,1,24,128,128]{4,3,2,1,0:T(8,128)(2,1)S(1)}, bf16[12,1,24,128,128]{4,3,2,1,0:T(8,128)(2,1)}, u32[]{:S(2)}) copy-start(bf16[12,1,24,128,128]{4,3,2,1,0:T(8,128)(2,1)} %param.4) | copy-start | bytes 28311556
  23.5 2.9 %collective-permute-start.3 = (bf16[64,6144]{1,0:T(8,128)(2,1)S(1)}, bf16[64,6144]{1,0:T(8,128)(2,1)S(1)}, u32[]{:S(2)}, u32[]{:S(2)}) collective-permute-start(bf16[64,6144]{1,0:T(8,128)(2,1)S(1)} %collective-permute-done.1.refs_3_), channel_id=1, source_target_pairs={{0,32},{32,0},{1,33},{33,1},{2,34},{34,2},{3,35},{35,3},{4,36},{36... | collective-permute-start | bytes 2359304 | tf_op jit(solution)/shard_map/ppermute | solution.py:17
  23.5 3.4 %collective-permute-start.4 = (bf16[64,6144]{1,0:T(8,128)(2,1)S(1)}, bf16[64,6144]{1,0:T(8,128)(2,1)S(1)}, u32[]{:S(2)}, u32[]{:S(2)}) collective-permute-start(bf16[64,6144]{1,0:T(8,128)(2,1)S(1)} %collective-permute-done.2.refs_4_), channel_id=1, source_target_pairs={{0,32},{32,0},{1,33},{33,1},{2,34},{34,2},{3,35},{35,3},{4,36},{36... | collective-permute-start | bytes 2359304 | tf_op jit(solution)/shard_map/ppermute | solution.py:17
  24.1 15.2 %collective-permute-start.7 = (bf16[32,6144]{1,0:T(8,128)(2,1)S(1)}, bf16[32,6144]{1,0:T(8,128)(2,1)S(1)}, u32[]{:S(2)}, u32[]{:S(2)}) collective-permute-start(bf16[32,6144]{1,0:T(8,128)(2,1)S(1)} %slice.20), channel_id=1, source_target_pairs={{0,64},{64,128},{128,192},{192,0},{1,65},{65,129},{129,193},{193,1... | collective-permute-start | bytes 1179656 | tf_op jit(solution)/shard_map/ppermute | solution.py:17
  25.7 13.6 %collective-permute-start.8 = (bf16[32,6144]{1,0:T(8,128)(2,1)S(1)}, bf16[32,6144]{1,0:T(8,128)(2,1)S(1)}, u32[]{:S(2)}, u32[]{:S(2)}) collective-permute-start(bf16[32,6144]{1,0:T(8,128)(2,1)S(1)} %slice.21), channel_id=1, source_target_pairs={{0,192},{64,0},{128,64},{192,128},{1,193},{65,1},{129,65},{193,129... | collective-permute-start | bytes 1179656 | tf_op jit(solution)/shard_map/ppermute | solution.py:17
  26.9 25.5 %collective-permute-start.5 = (bf16[64,6144]{1,0:T(8,128)(2,1)S(1)}, bf16[64,6144]{1,0:T(8,128)(2,1)S(1)}, u32[]{:S(2)}, u32[]{:S(2)}) collective-permute-start(bf16[64,6144]{1,0:T(8,128)(2,1)S(1)} %slice.18), channel_id=1, source_target_pairs={{0,64},{64,128},{128,192},{192,0},{1,65},{65,129},{129,193},{193,1... | collective-permute-start | bytes 2359304 | tf_op jit(solution)/shard_map/ppermute | solution.py:17
  28.8 25.7 %collective-permute-start.6 = (bf16[64,6144]{1,0:T(8,128)(2,1)S(1)}, bf16[64,6144]{1,0:T(8,128)(2,1)S(1)}, u32[]{:S(2)}, u32[]{:S(2)}) collective-permute-start(bf16[64,6144]{1,0:T(8,128)(2,1)S(1)} %slice.18), channel_id=1, source_target_pairs={{0,192},{64,0},{128,64},{192,128},{1,193},{65,1},{129,65},{193,129... | collective-permute-start | bytes 2359304 | tf_op jit(solution)/shard_map/ppermute | solution.py:17
  39.3 1.8 %collective-permute-start.10 = (bf16[32,6144]{1,0:T(8,128)(2,1)S(1)}, bf16[32,6144]{1,0:T(8,128)(2,1)S(1)}, u32[]{:S(2)}, u32[]{:S(2)}) collective-permute-start(bf16[32,6144]{1,0:T(8,128)(2,1)S(1)} %collective-permute-done.8.refs_4_), channel_id=1, source_target_pairs={{0,32},{32,0},{1,33},{33,1},{2,34},{34,2},{3,35},{35,3},{4,36},{36... | collective-permute-start | bytes 1179656 | tf_op jit(solution)/shard_map/ppermute | solution.py:17
  39.4 2.3 %collective-permute-start.9 = (bf16[32,6144]{1,0:T(8,128)(2,1)S(1)}, bf16[32,6144]{1,0:T(8,128)(2,1)S(1)}, u32[]{:S(2)}, u32[]{:S(2)}) collective-permute-start(bf16[32,6144]{1,0:T(8,128)(2,1)S(1)} %collective-permute-done.7.refs_3_), channel_id=1, source_target_pairs={{0,32},{32,0},{1,33},{33,1},{2,34},{34,2},{3,35},{35,3},{4,36},{36... | collective-permute-start | bytes 1179656 | tf_op jit(solution)/shard_map/ppermute | solution.py:17
  54.5 4.2 %collective-permute-start.13 = (bf16[64,6144]{1,0:T(8,128)(2,1)S(1)}, bf16[64,6144]{1,0:T(8,128)(2,1)S(1)}, u32[]{:S(2)}, u32[]{:S(2)}) collective-permute-start(bf16[64,6144]{1,0:T(8,128)(2,1)S(1)} %collective-permute-done.5.refs_3_), channel_id=1, source_target_pairs={{0,32},{32,0},{1,33},{33,1},{2,34},{34,2},{3,35},{35,3},{4,36},{36... | collective-permute-start | bytes 2359304 | tf_op jit(solution)/shard_map/ppermute | solution.py:17
  54.6 4.1 %collective-permute-start.14 = (bf16[64,6144]{1,0:T(8,128)(2,1)S(1)}, bf16[64,6144]{1,0:T(8,128)(2,1)S(1)}, u32[]{:S(2)}, u32[]{:S(2)}) collective-permute-start(bf16[64,6144]{1,0:T(8,128)(2,1)S(1)} %collective-permute-done.6.refs_4_), channel_id=1, source_target_pairs={{0,32},{32,0},{1,33},{33,1},{2,34},{34,2},{3,35},{35,3},{4,36},{36... | collective-permute-start | bytes 2359304 | tf_op jit(solution)/shard_map/ppermute | solution.py:17
  55.1 13.1 %collective-permute-start.11 = (bf16[32,6144]{1,0:T(8,128)(2,1)S(1)}, bf16[32,6144]{1,0:T(8,128)(2,1)S(1)}, u32[]{:S(2)}, u32[]{:S(2)}) collective-permute-start(bf16[32,6144]{1,0:T(8,128)(2,1)S(1)} %slice.22), channel_id=1, source_target_pairs={{0,64},{64,128},{128,192},{192,0},{1,65},{65,129},{129,193},{193,1... | collective-permute-start | bytes 1179656 | tf_op jit(solution)/shard_map/ppermute | solution.py:17
  56.9 11.4 %collective-permute-start.12 = (bf16[32,6144]{1,0:T(8,128)(2,1)S(1)}, bf16[32,6144]{1,0:T(8,128)(2,1)S(1)}, u32[]{:S(2)}, u32[]{:S(2)}) collective-permute-start(bf16[32,6144]{1,0:T(8,128)(2,1)S(1)} %slice.23), channel_id=1, source_target_pairs={{0,192},{64,0},{128,64},{192,128},{1,193},{65,1},{129,65},{193,129... | collective-permute-start | bytes 1179656 | tf_op jit(solution)/shard_map/ppermute | solution.py:17
  57.2 22.9 %collective-permute-start.20 = (s16[128,1664]{1,0:T(8,128)(2,1)S(1)}, s16[128,1664]{1,0:T(8,128)(2,1)S(1)}, u32[]{:S(2)}, u32[]{:S(2)}) collective-permute-start(s16[128,1664]{1,0:T(8,128)(2,1)S(1)} %get-tuple-element.73), channel_id=1, source_target_pairs={{0,16},{8,24},{16,0},{24,8},{1,17},{9,25},{17,1},{25,9},{2,18},{10... | collective-permute-start | bytes 1277960 | tf_op jit(solution)/shard_map/ppermute | solution.py:17
  68.3 3.8 %collective-permute-start.15 = (bf16[32,6144]{1,0:T(8,128)(2,1)S(1)}, bf16[32,6144]{1,0:T(8,128)(2,1)S(1)}, u32[]{:S(2)}, u32[]{:S(2)}) collective-permute-start(bf16[32,6144]{1,0:T(8,128)(2,1)S(1)} %collective-permute-done.11.refs_3_), channel_id=1, source_target_pairs={{0,32},{32,0},{1,33},{33,1},{2,34},{34,2},{3,35},{35,3},{4,36},{36... | collective-permute-start | bytes 1179656 | tf_op jit(solution)/shard_map/ppermute | solution.py:17
  68.4 3.7 %collective-permute-start.16 = (bf16[32,6144]{1,0:T(8,128)(2,1)S(1)}, bf16[32,6144]{1,0:T(8,128)(2,1)S(1)}, u32[]{:S(2)}, u32[]{:S(2)}) collective-permute-start(bf16[32,6144]{1,0:T(8,128)(2,1)S(1)} %collective-permute-done.12.refs_4_), channel_id=1, source_target_pairs={{0,32},{32,0},{1,33},{33,1},{2,34},{34,2},{3,35},{35,3},{4,36},{36... | collective-permute-start | bytes 1179656 | tf_op jit(solution)/shard_map/ppermute | solution.py:17
  68.9 14.3 %collective-permute-start.21 = (s16[128,1664]{1,0:T(8,128)(2,1)S(1)}, s16[128,1664]{1,0:T(8,128)(2,1)S(1)}, u32[]{:S(2)}, u32[]{:S(2)}) collective-permute-start(s16[128,1664]{1,0:T(8,128)(2,1)S(1)} %get-tuple-element.72), channel_id=1, source_target_pairs={{0,8},{8,16},{16,24},{24,0},{1,9},{9,17},{17,25},{25,1},{2,10},{10... | collective-permute-start | bytes 1277960 | tf_op jit(solution)/shard_map/ppermute | solution.py:17
  69.6 21.7 %collective-permute-start.22 = (s16[128,1664]{1,0:T(8,128)(2,1)S(1)}, s16[128,1664]{1,0:T(8,128)(2,1)S(1)}, u32[]{:S(2)}, u32[]{:S(2)}) collective-permute-start(s16[128,1664]{1,0:T(8,128)(2,1)S(1)} %get-tuple-element.74), channel_id=1, source_target_pairs={{0,24},{8,0},{16,8},{24,16},{1,25},{9,1},{17,9},{25,17},{2,26},{10... | collective-permute-start | bytes 1277960 | tf_op jit(solution)/shard_map/ppermute | solution.py:17
  79.1 14.4 %collective-permute-start.17 = (s16[128,1664]{1,0:T(8,128)(2,1)S(1)}, s16[128,1664]{1,0:T(8,128)(2,1)S(1)}, u32[]{:S(2)}, u32[]{:S(2)}) collective-permute-start(s16[128,1664]{1,0:T(8,128)(2,1)S(1)} %get-tuple-element.94), channel_id=1, source_target_pairs={{0,16},{8,24},{16,0},{24,8},{1,17},{9,25},{17,1},{25,9},{2,18},{10... | collective-permute-start | bytes 1277960 | tf_op jit(solution)/shard_map/ppermute | solution.py:17
  80.0 21.1 %collective-permute-start.18 = (s16[128,1664]{1,0:T(8,128)(2,1)S(1)}, s16[128,1664]{1,0:T(8,128)(2,1)S(1)}, u32[]{:S(2)}, u32[]{:S(2)}) collective-permute-start(s16[128,1664]{1,0:T(8,128)(2,1)S(1)} %get-tuple-element.95), channel_id=1, source_target_pairs={{0,8},{8,16},{16,24},{24,0},{1,9},{9,17},{17,25},{25,1},{2,10},{10... | collective-permute-start | bytes 1277960 | tf_op jit(solution)/shard_map/ppermute | solution.py:17
  80.0 21.1 %collective-permute-start.19 = (s16[128,1664]{1,0:T(8,128)(2,1)S(1)}, s16[128,1664]{1,0:T(8,128)(2,1)S(1)}, u32[]{:S(2)}, u32[]{:S(2)}) collective-permute-start(s16[128,1664]{1,0:T(8,128)(2,1)S(1)} %get-tuple-element.96), channel_id=1, source_target_pairs={{0,24},{8,0},{16,8},{24,16},{1,25},{9,1},{17,9},{25,17},{2,26},{10... | collective-permute-start | bytes 1277960 | tf_op jit(solution)/shard_map/ppermute | solution.py:17
  103.7 16.2 %collective-permute-start.23 = (s16[32,1664]{1,0:T(8,128)(2,1)S(1)}, s16[32,1664]{1,0:T(8,128)(2,1)S(1)}, u32[]{:S(2)}, u32[]{:S(2)}) collective-permute-start(s16[32,1664]{1,0:T(8,128)(2,1)S(1)} %get-tuple-element.102), channel_id=1, source_target_pairs={{0,4},{1,5},{2,6},{3,7},{4,0},{5,1},{6,2},{7,3},{8,12},{9,13},{10,... | collective-permute-start | bytes 319496 | tf_op jit(solution)/shard_map/ppermute | solution.py:17
  110.7 14.2 %collective-permute-start.24 = (s16[32,1664]{1,0:T(8,128)(2,1)S(1)}, s16[32,1664]{1,0:T(8,128)(2,1)S(1)}, u32[]{:S(2)}, u32[]{:S(2)}) collective-permute-start(s16[32,1664]{1,0:T(8,128)(2,1)S(1)} %get-tuple-element.103), channel_id=1, source_target_pairs={{0,3},{1,4},{2,5},{3,6},{4,7},{5,0},{6,1},{7,2},{8,11},{9,12},{10,... | collective-permute-start | bytes 319496 | tf_op jit(solution)/shard_map/ppermute | solution.py:17
  112.7 12.3 %collective-permute-start.25 = (s16[32,1664]{1,0:T(8,128)(2,1)S(1)}, s16[32,1664]{1,0:T(8,128)(2,1)S(1)}, u32[]{:S(2)}, u32[]{:S(2)}) collective-permute-start(s16[32,1664]{1,0:T(8,128)(2,1)S(1)} %get-tuple-element.104), channel_id=1, source_target_pairs={{0,5},{1,6},{2,7},{3,0},{4,1},{5,2},{6,3},{7,4},{8,13},{9,14},{10,... | collective-permute-start | bytes 319496 | tf_op jit(solution)/shard_map/ppermute | solution.py:17
  115.7 10.3 %collective-permute-start.26 = (s16[32,1664]{1,0:T(8,128)(2,1)S(1)}, s16[32,1664]{1,0:T(8,128)(2,1)S(1)}, u32[]{:S(2)}, u32[]{:S(2)}) collective-permute-start(s16[32,1664]{1,0:T(8,128)(2,1)S(1)} %get-tuple-element.105), channel_id=1, source_target_pairs={{0,2},{1,3},{2,4},{3,5},{4,6},{5,7},{6,0},{7,1},{8,10},{9,11},{10,... | collective-permute-start | bytes 319496 | tf_op jit(solution)/shard_map/ppermute | solution.py:17
  117.3 11.4 %collective-permute-start.27 = (s16[32,1664]{1,0:T(8,128)(2,1)S(1)}, s16[32,1664]{1,0:T(8,128)(2,1)S(1)}, u32[]{:S(2)}, u32[]{:S(2)}) collective-permute-start(s16[32,1664]{1,0:T(8,128)(2,1)S(1)} %get-tuple-element.106), channel_id=1, source_target_pairs={{0,6},{1,7},{2,0},{3,1},{4,2},{5,3},{6,4},{7,5},{8,14},{9,15},{10,... | collective-permute-start | bytes 319496 | tf_op jit(solution)/shard_map/ppermute | solution.py:17
  119.9 10.0 %collective-permute-start.28 = (s16[32,1664]{1,0:T(8,128)(2,1)S(1)}, s16[32,1664]{1,0:T(8,128)(2,1)S(1)}, u32[]{:S(2)}, u32[]{:S(2)}) collective-permute-start(s16[32,1664]{1,0:T(8,128)(2,1)S(1)} %get-tuple-element.107), channel_id=1, source_target_pairs={{0,1},{1,2},{2,3},{3,4},{4,5},{5,6},{6,7},{7,0},{8,9},{9,10},{10,1... | collective-permute-start | bytes 319496 | tf_op jit(solution)/shard_map/ppermute | solution.py:17
  125.0 5.7 %collective-permute-start.29 = (s16[32,1664]{1,0:T(8,128)(2,1)S(1)}, s16[32,1664]{1,0:T(8,128)(2,1)S(1)}, u32[]{:S(2)}, u32[]{:S(2)}) collective-permute-start(s16[32,1664]{1,0:T(8,128)(2,1)S(1)} %get-tuple-element.108), channel_id=1, source_target_pairs={{0,7},{1,0},{2,1},{3,2},{4,3},{5,4},{6,5},{7,6},{8,15},{9,8},{10,9... | collective-permute-start | bytes 319496 | tf_op jit(solution)/shard_map/ppermute | solution.py:17

commit v7 on v6

--- a/solution.py
+++ b/solution.py
@@ -11,10 +11,17 @@
 QW = 4
 CHUNKS = (2, 2)
 LEVELS = 32767.0
+FAR_Z = (4, 3, 5)
+NEAR_Z = (2, 6, 1, 7)
 
 
 def shift(value, axis, size, step):
     return lax.ppermute(value, axis, [(i, (i + step) % size) for i in range(size)])
+
+
+def shift_to(value, axis, size, step, wanted):
+    pairs = [(i, (i + step) % size) for i in range(size)]
+    return lax.ppermute(value, axis, [p for p in pairs if wanted(p[1])])
 
 
 def encode(total):
@@ -153,20 +160,28 @@
     return [pltpu.VMEM((4, rows, TILE), jnp.float32), pltpu.VMEM((rows, TILE), jnp.float32)]
 
 
-def add_first(parts):
+def add_first(pos, parts):
+    rows, wide = parts[0].shape
     vmem = pl.BlockSpec(memory_space=pltpu.VMEM)
-
-    def body(*refs):
-        add_and_encode(refs[:4], refs[5], refs[6], refs[4])
+    n_far, groups = len(FAR_Z), CHUNKS[0]
+
+    def body(pos_ref, *refs):
+        res, outs, (scale, codes) = refs[4], refs[5 : 5 + n_far], refs[5 + n_far :]
+        add_and_encode(refs[:4], scale, codes, res)
+        for out, s in zip(outs, FAR_Z):
+            z = (pos_ref[3] + s) % NZ
+            row = pl.multiple_of((z // QW * groups + jnp.minimum(z % QW, groups - 1)) * ROWS, ROWS)
+            out[...] = res[pl.ds(row, ROWS), :]
 
     return pl.pallas_call(
         body,
-        out_shape=jax.ShapeDtypeStruct(parts[0].shape, jnp.int16),
-        in_specs=[vmem] * 4,
-        out_specs=vmem,
-        scratch_shapes=add_scratch(*parts[0].shape),
+        out_shape=[jax.ShapeDtypeStruct((rows, wide), jnp.int16)]
+        + [jax.ShapeDtypeStruct((ROWS, wide), jnp.int16)] * n_far,
+        in_specs=[pl.BlockSpec(memory_space=pltpu.SMEM)] + [vmem] * 4,
+        out_specs=[vmem] * (1 + n_far),
+        scratch_shapes=add_scratch(rows, wide),
         compiler_params=pltpu.CompilerParams(vmem_limit_bytes=10 << 20),
-    )(*parts)
+    )(pos, *parts)
 
 
 def add_second(pos, parts, done):
@@ -196,20 +211,21 @@
     )(pos, *parts, done)
 
 
-def add_last(eight):
-    rows, wide = eight[0].shape
+def add_last(arrived):
+    rows, wide = arrived[0].shape
+    n = len(arrived)
     n_tiles = wide // TILE - 1
 
     def body(*refs):
-        out, scale = refs[NZ:]
+        out, scale = refs[n:]
         lane = lax.broadcasted_iota(jnp.int32, (rows, TILE), 1)
-        for i in range(NZ):
+        for i in range(n):
             scale[i] = scales(refs[i][:, n_tiles * TILE :])
 
         def one_tile(t, carry):
             column = pl.ds(pl.multiple_of(t * TILE, TILE), TILE)
             total = None
-            for i in range(NZ):
+            for i in range(n):
                 factor = jnp.sum(jnp.where(lane == t, scale[i], 0.0), axis=1, keepdims=True)
                 part = refs[i][:, column].astype(jnp.int32).astype(jnp.float32) * factor
                 total = part if total is None else total + part
@@ -221,9 +237,9 @@
     return pl.pallas_call(
         body,
         out_shape=jax.ShapeDtypeStruct((rows, n_tiles * TILE), jnp.float32),
-        scratch_shapes=[pltpu.VMEM((NZ, rows, TILE), jnp.float32)],
+        scratch_shapes=[pltpu.VMEM((n, rows, TILE), jnp.float32)],
         compiler_params=pltpu.CompilerParams(vmem_limit_bytes=8 << 20),
-    )(*eight)
+    )(*arrived)
 
 
 def after(values, *others):
@@ -295,8 +311,14 @@
     coded_2 = contract(pos, cd_tiles, integrals, blocks, heights[1:], coded_2)
     met_2 = along_x(coded_2)
 
-    sums = add_second(pos, met_2, add_first(after(met_1, coded_2)))
-    return add_last([sums[0]] + [shift(sums[s], "z", NZ, s) for s in (4, 3, 5, 2, 6, 1, 7)])
+    done = add_first(pos, after(met_1, coded_2))
+    early = [
+        shift_to(part, "z", NZ, s, lambda z: z % QW < CHUNKS[0]) for part, s in zip(done[1:], FAR_Z)
+    ]
+    sums = add_second(pos, met_2, done[0])
+    late = [shift_to(sums[s], "z", NZ, s, lambda z: z % QW >= CHUNKS[0]) for s in FAR_Z]
+    late += [shift(sums[s], "z", NZ, s) for s in NEAR_Z]
+    return add_last([sums[0]] + early + late)
 
 
 def solution(mesh):

time: 134 us -> 137 us (1.022)
  starting transfers between devices: 37.8 us -> 53.3 us
  waiting for transfers between devices: 38.2 us -> 24.1 us
    ppermute x0 -> x6, starting transfers between devices: none -> 20.6 us  [shift_to(): return lax.ppermute(value, axis, [p for p in pairs if wanted(p[1])])]
    ppermute x30 -> x27, waiting for transfers between devices: 38.2 us -> 24.1 us  [shift(): lax.ppermute(value, axis, [(i, (i + step) % size) for i in range(size)])]
    ppermute x30 -> x27, starting transfers between devices: 37.8 us -> 32.7 us  [shift(): lax.ppermute(value, axis, [(i, (i + step) % size) for i in range(size)])]
  transfers between devices with their start and end apart: 30 -> 33, of which waited for: 15 -> 11; matrix products, arithmetic and copies ran while one was open for 2% -> 2% of each run, Pallas kernels for 35% -> 36%
where the time goes in v7:
time: 137 us; the launch traced here: 134 us
  starting transfers between devices  53.3 us (39%)
  Pallas kernels  50.5 us (37%)
  waiting for transfers between devices  24.1 us (18%)
  local copies, waits for them, and re-layouts  6.04 us (4%)
    pallas_call x5, Pallas kernels, contract(): pl.pallas_call(body, out_shape=[jax.ShapeDtypeStruct((NC * h, width + TIL...  43.9 us
    ppermute x27, starting transfers between devices, shift(): lax.ppermute(value, axis, [(i, (i + step) % size) for i in range(size)])  32.7 us
    ppermute x27, waiting for transfers between devices, shift(): lax.ppermute(value, axis, [(i, (i + step) % size) for i in range(size)])  24.1 us
    ppermute x6, starting transfers between devices, shift_to(): return lax.ppermute(value, axis, [p for p in pairs if wanted(p[1])])  20.6 us
    unnamed x9, local copies, waits for them, and re-layouts  3.69 us
  transfers between devices with their start and end apart: 33, of which 11 were waited for; matrix products, arithmetic and copies ran while one was open for 2% of the time, Pallas kernels for 36%

profile of v7, /device:TPU:8, one launch (start us, length us, event | category | flops | bytes accessed | tf_op | source)
XLA Modules:
  0.0 134.3 jit_solution(1972614459609734688)
XLA Ops:
  0.0 2.2 %slice.19 = bf16[64,6144]{1,0:T(8,128)(2,1)} slice(bf16[128,6144]{1,0:T(8,128)(2,1)} %refs_3_.1), slice={[0:64], [0:6144]} | slice | bytes 1572864 | tf_op jit(solution)/shard_map/slice | solution.py:274
  2.2 1.6 %collective-permute-start.1 = (bf16[64,6144]{1,0:T(8,128)(2,1)}, bf16[64,6144]{1,0:T(8,128)(2,1)S(1)}, u32[]{:S(2)}, u32[]{:S(2)}) collective-permute-start(bf16[64,6144]{1,0:T(8,128)(2,1)} %slice.19), channel_id=1, source_target_pairs={{0,64},{64,128},{128,192},{192,0},{1,65},{65,129},{129,193},{193,1... | collective-permute-start | bytes 2359304 | tf_op jit(solution)/shard_map/ppermute | solution.py:19
  3.8 0.6 collective-permute-start.2
  4.5 3.7 %copy-done = bf16[12,1,24,128,128]{4,3,2,1,0:T(8,128)(2,1)S(1)} copy-done((bf16[12,1,24,128,128]{4,3,2,1,0:T(8,128)(2,1)S(1)}, bf16[12,1,24,128,128]{4,3,2,1,0:T(8,128)(2,1)}, u32[]{:S(2)}) %copy-start) | copy-done | bytes 9437208
  8.2 11.0 %shard_map.37 = (s16[128,1664]{1,0:T(8,128)(2,1)S(1)}, s16[128,1664]{1,0:T(8,128)(2,1)S(1)}, s16[128,1664]{1,0:T(8,128)(2,1)S(1)}, s16[128,1664]{1,0:T(8,128)(2,...) custom-call(s32[4]{0:T(128)S(1)} %pad_add_fusion.refs_0_.pos_ref, ...), custom_call_target="tpu_custom_call" | custom-call | flops 1 | bytes 1 | tf_op jit(solution)/shard_map/pallas_call | solution.py:110
  19.2 3.5 %collective-permute-done.1.refs_3_ = bf16[64,6144]{1,0:T(8,128)(2,1)S(1)} collective-permute-done((bf16[64,6144]{1,0:T(8,128)(2,1)}, bf16[64,6144]{1,0:T(8,128)(2,1)S(1)}, u32[]{:S(2)}, u32[]{:S(2)}) %collective-permute-start.1) | collective-permute-done | bytes 786464 | tf_op jit(solution)/shard_map/ppermute | solution.py:19
  22.7 0.9 collective-permute-done.2.refs_4_
  23.5 0.5 collective-permute-start.4
  24.1 1.6 %collective-permute-start.7 = (bf16[32,6144]{1,0:T(8,128)(2,1)S(1)}, bf16[32,6144]{1,0:T(8,128)(2,1)S(1)}, u32[]{:S(2)}, u32[]{:S(2)}) collective-permute-start(bf16[32,6144]{1,0:T(8,128)(2,1)S(1)} %slice.20), channel_id=1, source_target_pairs={{0,64},{64,128},{128,192},{192,0},{1,65},{65,129},{129,193},{193,1... | collective-permute-start | bytes 1179656 | tf_op jit(solution)/shard_map/ppermute | solution.py:19
  25.7 0.7 collective-permute-start.8
  26.5 0.5 collective-permute-done.4.refs_6_
  26.9 1.9 %collective-permute-start.5 = (bf16[64,6144]{1,0:T(8,128)(2,1)S(1)}, bf16[64,6144]{1,0:T(8,128)(2,1)S(1)}, u32[]{:S(2)}, u32[]{:S(2)}) collective-permute-start(bf16[64,6144]{1,0:T(8,128)(2,1)S(1)} %slice.18), channel_id=1, source_target_pairs={{0,64},{64,128},{128,192},{192,0},{1,65},{65,129},{129,193},{193,1... | collective-permute-start | bytes 2359304 | tf_op jit(solution)/shard_map/ppermute | solution.py:19
  28.8 1.0 collective-permute-start.6
  29.8 9.5 %shard_map.38 = (s16[128,1664]{1,0:T(8,128)(2,1)S(1)}, s16[128,1664]{1,0:T(8,128)(2,1)S(1)}, s16[128,1664]{1,0:T(8,128)(2,1)S(1)}, s16[128,1664]{1,0:T(8,128)(2,1)S(1)}) custom-call(s32[4]{0:T(128)S(1)} %pad_add_fusion.refs_0_.pos_ref, s32[12,24]{1,0:T(8,128)S(1)} %bitcast.14, ...), custom_call_target="tpu_custom_call", output_to_operand_aliasing={{0}: (7, {}), {1}: (8, {}), {2}: (9, {}), {3}: (10, {})} | custom-call | flops 1 | bytes 1 | tf_op jit(solution)/shard_map/pallas_call | solution.py:110
  39.3 0.1 collective-permute-start.10
  39.4 0.5 collective-permute-start.9
  39.9 1.2 collective-permute-done.10.refs_6_
  41.1 0.6 collective-permute-done.9.refs_5_
  41.7 7.0 %shard_map.39 = (s16[128,1664]{1,0:T(8,128)(2,1)S(1)}, s16[128,1664]{1,0:T(8,128)(2,1)S(1)}, s16[128,1664]{1,0:T(8,128)(2,1)S(1)}, s16[128,1664]{1,0:T(8,128)(2,1)S(1)}) custom-call(s32[4]{0:T(128)S(1)} %pad_add_fusion.refs_0_.pos_ref, s32[12,24]{1,0:T(8,128)S(1)} %bitcast.15, ...), custom_call_target="tpu_custom_call", output_to_operand_aliasing={{0}: (7, {}), {1}: (8, {}), {2}: (9, {}), {3}: (10, {})} | custom-call | flops 1 | bytes 1 | tf_op jit(solution)/shard_map/pallas_call | solution.py:110
  48.7 3.8 %collective-permute-done.5.refs_3_ = bf16[64,6144]{1,0:T(8,128)(2,1)S(1)} collective-permute-done((bf16[64,6144]{1,0:T(8,128)(2,1)S(1)}, bf16[64,6144]{1,0:T(8,128)(2,1)S(1)}, u32[]{:S(2)}, u32[]{:S(2)}) %collective-permute-start.5) | collective-permute-done | bytes 786464 | tf_op jit(solution)/shard_map/ppermute | solution.py:19
  52.4 2.1 %collective-permute-done.6.refs_4_ = bf16[64,6144]{1,0:T(8,128)(2,1)S(1)} collective-permute-done((bf16[64,6144]{1,0:T(8,128)(2,1)S(1)}, bf16[64,6144]{1,0:T(8,128)(2,1)S(1)}, u32[]{:S(2)}, u32[]{:S(2)}) %collective-permute-start.6) | collective-permute-done | bytes 786464 | tf_op jit(solution)/shard_map/ppermute | solution.py:19
  54.7 0.5 collective-permute-start.14
  55.2 1.7 %collective-permute-start.11 = (bf16[32,6144]{1,0:T(8,128)(2,1)S(1)}, bf16[32,6144]{1,0:T(8,128)(2,1)S(1)}, u32[]{:S(2)}, u32[]{:S(2)}) collective-permute-start(bf16[32,6144]{1,0:T(8,128)(2,1)S(1)} %slice.22), channel_id=1, source_target_pairs={{0,64},{64,128},{128,192},{192,0},{1,65},{65,129},{129,193},{193,1... | collective-permute-start | bytes 1179656 | tf_op jit(solution)/shard_map/ppermute | solution.py:19
  56.9 0.3 collective-permute-start.12
  57.2 1.6 %collective-permute-start.20 = (s16[128,1664]{1,0:T(8,128)(2,1)S(1)}, s16[128,1664]{1,0:T(8,128)(2,1)S(1)}, u32[]{:S(2)}, u32[]{:S(2)}) collective-permute-start(s16[128,1664]{1,0:T(8,128)(2,1)S(1)} %get-tuple-element.77), channel_id=1, source_target_pairs={{0,16},{8,24},{16,0},{24,8},{1,17},{9,25},{17,1},{25,9},{2,18},{10... | collective-permute-start | bytes 1277960 | tf_op jit(solution)/shard_map/ppermute | solution.py:19
  58.8 9.5 %shard_map.40 = (s16[128,1664]{1,0:T(8,128)(2,1)S(1)}, s16[128,1664]{1,0:T(8,128)(2,1)S(1)}, s16[128,1664]{1,0:T(8,128)(2,1)S(1)}, s16[128,1664]{1,0:T(8,128)(2,1)S(1)}) custom-call(s32[4]{0:T(128)S(1)} %pad_add_fusion.refs_0_.pos_ref, s32[12,24]{1,0:T(8,128)S(1)} %bitcast.16, ...), custom_call_target="tpu_custom_call", output_to_operand_aliasing={{0}: (7, {}), {1}: (8, {}), {2}: (9, {}), {3}: (10, {})} | custom-call | flops 1 | bytes 1 | tf_op jit(solution)/shard_map/pallas_call | solution.py:110
  68.3 0.1 collective-permute-start.15
  68.4 0.5 collective-permute-start.16
  68.9 0.6 collective-permute-start.21
  69.6 2.6 %collective-permute-start.22 = (s16[128,1664]{1,0:T(8,128)(2,1)S(1)}, s16[128,1664]{1,0:T(8,128)(2,1)S(1)}, u32[]{:S(2)}, u32[]{:S(2)}) collective-permute-start(s16[128,1664]{1,0:T(8,128)(2,1)S(1)} %get-tuple-element.78), channel_id=1, source_target_pairs={{0,24},{8,0},{16,8},{24,16},{1,25},{9,1},{17,9},{25,17},{2,26},{10... | collective-permute-start | bytes 1277960 | tf_op jit(solution)/shard_map/ppermute | solution.py:19
  72.2 7.0 %shard_map.41 = (s16[128,1664]{1,0:T(8,128)(2,1)S(1)}, s16[128,1664]{1,0:T(8,128)(2,1)S(1)}, s16[128,1664]{1,0:T(8,128)(2,1)S(1)}, s16[128,1664]{1,0:T(8,128)(2,1)S(1)}) custom-call(s32[4]{0:T(128)S(1)} %pad_add_fusion.refs_0_.pos_ref, s32[12,24]{1,0:T(8,128)S(1)} %bitcast.17, ...), custom_call_target="tpu_custom_call", output_to_operand_aliasing={{0}: (7, {}), {1}: (8, {}), {2}: (9, {}), {3}: (10, {})} | custom-call | flops 1 | bytes 1 | tf_op jit(solution)/shard_map/pallas_call | solution.py:110
  79.1 0.8 collective-permute-start.17
  80.1 3.1 %collective-permute-start.19 = (s16[128,1664]{1,0:T(8,128)(2,1)S(1)}, s16[128,1664]{1,0:T(8,128)(2,1)S(1)}, u32[]{:S(2)}, u32[]{:S(2)}) collective-permute-start(s16[128,1664]{1,0:T(8,128)(2,1)S(1)} %get-tuple-element.100), channel_id=1, source_target_pairs={{0,24},{8,0},{16,8},{24,16},{1,25},{9,1},{17,9},{25,17},{2,26},{10... | collective-permute-start | bytes 1277960 | tf_op jit(solution)/shard_map/ppermute | solution.py:19
  83.2 8.1 %collective-permute-done.22.refs_3_ = s16[128,1664]{1,0:T(8,128)(2,1)S(1)} collective-permute-done((s16[128,1664]{1,0:T(8,128)(2,1)S(1)}, s16[128,1664]{1,0:T(8,128)(2,1)S(1)}, u32[]{:S(2)}, u32[]{:S(2)}) %collective-permute-start.22) | collective-permute-done | bytes 426016 | tf_op jit(solution)/shard_map/ppermute | solution.py:19
  91.4 2.5 %shard_map.42 = (s16[128,1664]{1,0:T(8,128)(2,1)S(1)}, s16[32,1664]{1,0:T(8,128)(2,1)S(1)}, s16[32,1664]{1,0:T(8,128)(2,1)S(1)}, s16[32,1664]{1,0:T(8,128)(2,1)S(1)}) custom-call(s32[4]{0:T(128)S(1)} %pad_add_fusion.refs_0_.pos_ref, s16[128,1664]{1,0:T(8,128)(2,1)S(1)} %get-tuple-element.101.refs_0_, s16[128,1664]{1,0:T(8,128)(2,1)S(1)} %collective-permute-done.20.refs_1_, ...), custom_call_target="tpu_custom_call" | custom-call | tf_op jit(solution)/shard_map/pallas_call | solution.py:176
  93.8 9.1 %collective-permute-start.23 = (s16[32,1664]{1,0:T(8,128)(2,1)S(1)}, s16[32,1664]{1,0:T(8,128)(2,1)S(1)}, u32[]{:S(2)}, u32[]{:S(2)}) collective-permute-start(s16[32,1664]{1,0:T(8,128)(2,1)S(1)} %get-tuple-element.107), channel_id=1, source_target_pairs={{0,4},{1,5},{4,0},{5,1},{8,12},{9,13},{12,8},{13,9},{16,20},{17,21... | collective-permute-start | bytes 319496 | tf_op jit(solution)/shard_map/ppermute | solution.py:24
  102.9 1.3 collective-permute-start.24
  104.2 7.6 %collective-permute-start.25 = (s16[32,1664]{1,0:T(8,128)(2,1)S(1)}, s16[32,1664]{1,0:T(8,128)(2,1)S(1)}, u32[]{:S(2)}, u32[]{:S(2)}) collective-permute-start(s16[32,1664]{1,0:T(8,128)(2,1)S(1)} %get-tuple-element.109), channel_id=1, source_target_pairs={{0,5},{3,0},{4,1},{7,4},{8,13},{11,8},{12,9},{15,12},{16,21},{19,1... | collective-permute-start | bytes 319496 | tf_op jit(solution)/shard_map/ppermute | solution.py:24
  111.8 2.6 %shard_map.43 = (s16[32,1664]{1,0:T(8,128)(2,1)S(1)}, s16[32,1664]{1,0:T(8,128)(2,1)S(1)}, s16[32,1664]{1,0:T(8,128)(2,1)S(1)}, s16[32,1664]{1,0:T(8,128)(2,1)S(...) custom-call(s32[4]{0:T(128)S(1)} %pad_add_fusion.refs_0_.pos_ref, ...), custom_call_target="tpu_custom_call" | custom-call | tf_op jit(solution)/shard_map/pallas_call | solution.py:203
  114.4 0.7 collective-permute-start.26
  115.0 1.4 %collective-permute-start.27 = (s16[32,1664]{1,0:T(8,128)(2,1)S(1)}, s16[32,1664]{1,0:T(8,128)(2,1)S(1)}, u32[]{:S(2)}, u32[]{:S(2)}) collective-permute-start(s16[32,1664]{1,0:T(8,128)(2,1)S(1)} %get-tuple-element.111), channel_id=1, source_target_pairs={{0,3},{3,6},{4,7},{7,2},{8,11},{11,14},{12,15},{15,10},{16,19},{19... | collective-permute-start | bytes 319496 | tf_op jit(solution)/shard_map/ppermute | solution.py:24
  116.5 0.7 collective-permute-start.28
  117.1 8.8 %collective-permute-start.29 = (s16[32,1664]{1,0:T(8,128)(2,1)S(1)}, s16[32,1664]{1,0:T(8,128)(2,1)S(1)}, u32[]{:S(2)}, u32[]{:S(2)}) collective-permute-start(s16[32,1664]{1,0:T(8,128)(2,1)S(1)} %get-tuple-element.113), channel_id=1, source_target_pairs={{0,2},{1,3},{2,4},{3,5},{4,6},{5,7},{6,0},{7,1},{8,10},{9,11},{10,... | collective-permute-start | bytes 319496 | tf_op jit(solution)/shard_map/ppermute | solution.py:19
  126.1 3.2 %collective-permute-start.32 = (s16[32,1664]{1,0:T(8,128)(2,1)S(1)}, s16[32,1664]{1,0:T(8,128)(2,1)S(1)}, u32[]{:S(2)}, u32[]{:S(2)}) collective-permute-start(s16[32,1664]{1,0:T(8,128)(2,1)S(1)} %get-tuple-element.116), channel_id=1, source_target_pairs={{0,7},{1,0},{2,1},{3,2},{4,3},{5,4},{6,5},{7,6},{8,15},{9,8},{10,9... | collective-permute-start | bytes 319496 | tf_op jit(solution)/shard_map/ppermute | solution.py:19
  129.3 2.4 %collective-permute-done.30.refs_8_ = s16[32,1664]{1,0:T(8,128)(2,1)S(1)} collective-permute-done((s16[32,1664]{1,0:T(8,128)(2,1)S(1)}, s16[32,1664]{1,0:T(8,128)(2,1)S(1)}, u32[]{:S(2)}, u32[]{:S(2)}) %collective-permute-start.30) | collective-permute-done | bytes 106528 | tf_op jit(solution)/shard_map/ppermute | solution.py:19
  131.7 0.3 collective-permute-done.31.refs_9_
  132.0 0.8 collective-permute-done.32.refs_10_
  132.8 1.5 %shard_map.44 = f32[32,1536]{1,0:T(8,128)} custom-call(s16[32,1664]{1,0:T(8,128)(2,1)S(1)} %get-tuple-element.106.refs_0_, s16[32,1664]{1,0:T(8,128)(2,1)S(1)} %collective-permute-done.23.refs_1_, s16[32,1664]{1,0:T(8,128)(2,1)S(1)} %collective-permute-done.24.refs_2_, s16[32,1664]{1,0:T(8,128)(2,1)S(1)} %collective-permute-done.25.refs_3_, ...), custom_call_target="tpu_custom_call" | custom-call | tf_op jit(solution)/shard_map/pallas_call | solution.py:237
  (42 shorter events, 0.6 us)
Async XLA Ops:
  0.0 4.5 %copy-start.2 = (bf16[128,6144]{1,0:T(8,128)(2,1)S(1)}, bf16[128,6144]{1,0:T(8,128)(2,1)}, u32[]{:S(2)}) copy-start(bf16[128,6144]{1,0:T(8,128)(2,1)} %refs_3_.1) | copy-start | bytes 4718596
  0.0 4.4 %copy-start.3 = (s32[12,1,24]{2,1,0:T(1,128)S(1)}, s32[12,1,24]{2,1,0:T(1,128)}, u32[]{:S(2)}) copy-start(s32[12,1,24]{2,1,0:T(1,128)} %param.5) | copy-start | bytes 3460
  0.0 4.5 %collective-permute-start = (bf16[128,6144]{1,0:T(8,128)(2,1)}, bf16[128,6144]{1,0:T(8,128)(2,1)}, u32[]{:S(2)}, u32[]{:S(2)}) collective-permute-start(bf16[128,6144]{1,0:T(8,128)(2,1)} %refs_3_.1), channel_id=1, source_target_pairs={{0,32},{32,0},{1,33},{33,1},{2,34},{34,2},{3,35},{35,3},{4,36},{36... | collective-permute-start | bytes 4718600 | tf_op jit(solution)/shard_map/ppermute | solution.py:19
  2.2 20.5 %collective-permute-start.1 = (bf16[64,6144]{1,0:T(8,128)(2,1)}, bf16[64,6144]{1,0:T(8,128)(2,1)S(1)}, u32[]{:S(2)}, u32[]{:S(2)}) collective-permute-start(bf16[64,6144]{1,0:T(8,128)(2,1)} %slice.19), channel_id=1, source_target_pairs={{0,64},{64,128},{128,192},{192,0},{1,65},{65,129},{129,193},{193,1... | collective-permute-start | bytes 2359304 | tf_op jit(solution)/shard_map/ppermute | solution.py:19
  3.8 19.7 %collective-permute-start.2 = (bf16[64,6144]{1,0:T(8,128)(2,1)}, bf16[64,6144]{1,0:T(8,128)(2,1)S(1)}, u32[]{:S(2)}, u32[]{:S(2)}) collective-permute-start(bf16[64,6144]{1,0:T(8,128)(2,1)} %slice.19), channel_id=1, source_target_pairs={{0,192},{64,0},{128,64},{192,128},{1,193},{65,1},{129,65},{193,129... | collective-permute-start | bytes 2359304 | tf_op jit(solution)/shard_map/ppermute | solution.py:19
  4.5 3.7 %copy-start = (bf16[12,1,24,128,128]{4,3,2,1,0:T(8,128)(2,1)S(1)}, bf16[12,1,24,128,128]{4,3,2,1,0:T(8,128)(2,1)}, u32[]{:S(2)}) copy-start(bf16[12,1,24,128,128]{4,3,2,1,0:T(8,128)(2,1)} %param.4) | copy-start | bytes 28311556
  8.2 21.6 %copy-start.1 = (bf16[12,1,24,128,128]{4,3,2,1,0:T(8,128)(2,1)S(1)}, bf16[12,1,24,128,128]{4,3,2,1,0:T(8,128)(2,1)}, u32[]{:S(2)}) copy-start(bf16[12,1,24,128,128]{4,3,2,1,0:T(8,128)(2,1)} %param.4) | copy-start | bytes 28311556
  23.5 2.9 %collective-permute-start.3 = (bf16[64,6144]{1,0:T(8,128)(2,1)S(1)}, bf16[64,6144]{1,0:T(8,128)(2,1)S(1)}, u32[]{:S(2)}, u32[]{:S(2)}) collective-permute-start(bf16[64,6144]{1,0:T(8,128)(2,1)S(1)} %collective-permute-done.1.refs_3_), channel_id=1, source_target_pairs={{0,32},{32,0},{1,33},{33,1},{2,34},{34,2},{3,35},{35,3},{4,36},{36... | collective-permute-start | bytes 2359304 | tf_op jit(solution)/shard_map/ppermute | solution.py:19
  23.5 3.4 %collective-permute-start.4 = (bf16[64,6144]{1,0:T(8,128)(2,1)S(1)}, bf16[64,6144]{1,0:T(8,128)(2,1)S(1)}, u32[]{:S(2)}, u32[]{:S(2)}) collective-permute-start(bf16[64,6144]{1,0:T(8,128)(2,1)S(1)} %collective-permute-done.2.refs_4_), channel_id=1, source_target_pairs={{0,32},{32,0},{1,33},{33,1},{2,34},{34,2},{3,35},{35,3},{4,36},{36... | collective-permute-start | bytes 2359304 | tf_op jit(solution)/shard_map/ppermute | solution.py:19
  24.1 15.2 %collective-permute-start.7 = (bf16[32,6144]{1,0:T(8,128)(2,1)S(1)}, bf16[32,6144]{1,0:T(8,128)(2,1)S(1)}, u32[]{:S(2)}, u32[]{:S(2)}) collective-permute-start(bf16[32,6144]{1,0:T(8,128)(2,1)S(1)} %slice.20), channel_id=1, source_target_pairs={{0,64},{64,128},{128,192},{192,0},{1,65},{65,129},{129,193},{193,1... | collective-permute-start | bytes 1179656 | tf_op jit(solution)/shard_map/ppermute | solution.py:19
  25.7 13.6 %collective-permute-start.8 = (bf16[32,6144]{1,0:T(8,128)(2,1)S(1)}, bf16[32,6144]{1,0:T(8,128)(2,1)S(1)}, u32[]{:S(2)}, u32[]{:S(2)}) collective-permute-start(bf16[32,6144]{1,0:T(8,128)(2,1)S(1)} %slice.21), channel_id=1, source_target_pairs={{0,192},{64,0},{128,64},{192,128},{1,193},{65,1},{129,65},{193,129... | collective-permute-start | bytes 1179656 | tf_op jit(solution)/shard_map/ppermute | solution.py:19
  26.9 25.5 %collective-permute-start.5 = (bf16[64,6144]{1,0:T(8,128)(2,1)S(1)}, bf16[64,6144]{1,0:T(8,128)(2,1)S(1)}, u32[]{:S(2)}, u32[]{:S(2)}) collective-permute-start(bf16[64,6144]{1,0:T(8,128)(2,1)S(1)} %slice.18), channel_id=1, source_target_pairs={{0,64},{64,128},{128,192},{192,0},{1,65},{65,129},{129,193},{193,1... | collective-permute-start | bytes 2359304 | tf_op jit(solution)/shard_map/ppermute | solution.py:19
  28.8 25.7 %collective-permute-start.6 = (bf16[64,6144]{1,0:T(8,128)(2,1)S(1)}, bf16[64,6144]{1,0:T(8,128)(2,1)S(1)}, u32[]{:S(2)}, u32[]{:S(2)}) collective-permute-start(bf16[64,6144]{1,0:T(8,128)(2,1)S(1)} %slice.18), channel_id=1, source_target_pairs={{0,192},{64,0},{128,64},{192,128},{1,193},{65,1},{129,65},{193,129... | collective-permute-start | bytes 2359304 | tf_op jit(solution)/shard_map/ppermute | solution.py:19
  39.3 1.8 %collective-permute-start.10 = (bf16[32,6144]{1,0:T(8,128)(2,1)S(1)}, bf16[32,6144]{1,0:T(8,128)(2,1)S(1)}, u32[]{:S(2)}, u32[]{:S(2)}) collective-permute-start(bf16[32,6144]{1,0:T(8,128)(2,1)S(1)} %collective-permute-done.8.refs_4_), channel_id=1, source_target_pairs={{0,32},{32,0},{1,33},{33,1},{2,34},{34,2},{3,35},{35,3},{4,36},{36... | collective-permute-start | bytes 1179656 | tf_op jit(solution)/shard_map/ppermute | solution.py:19
  39.4 2.3 %collective-permute-start.9 = (bf16[32,6144]{1,0:T(8,128)(2,1)S(1)}, bf16[32,6144]{1,0:T(8,128)(2,1)S(1)}, u32[]{:S(2)}, u32[]{:S(2)}) collective-permute-start(bf16[32,6144]{1,0:T(8,128)(2,1)S(1)} %collective-permute-done.7.refs_3_), channel_id=1, source_target_pairs={{0,32},{32,0},{1,33},{33,1},{2,34},{34,2},{3,35},{35,3},{4,36},{36... | collective-permute-start | bytes 1179656 | tf_op jit(solution)/shard_map/ppermute | solution.py:19
  54.6 4.2 %collective-permute-start.13 = (bf16[64,6144]{1,0:T(8,128)(2,1)S(1)}, bf16[64,6144]{1,0:T(8,128)(2,1)S(1)}, u32[]{:S(2)}, u32[]{:S(2)}) collective-permute-start(bf16[64,6144]{1,0:T(8,128)(2,1)S(1)} %collective-permute-done.5.refs_3_), channel_id=1, source_target_pairs={{0,32},{32,0},{1,33},{33,1},{2,34},{34,2},{3,35},{35,3},{4,36},{36... | collective-permute-start | bytes 2359304 | tf_op jit(solution)/shard_map/ppermute | solution.py:19
  54.7 4.1 %collective-permute-start.14 = (bf16[64,6144]{1,0:T(8,128)(2,1)S(1)}, bf16[64,6144]{1,0:T(8,128)(2,1)S(1)}, u32[]{:S(2)}, u32[]{:S(2)}) collective-permute-start(bf16[64,6144]{1,0:T(8,128)(2,1)S(1)} %collective-permute-done.6.refs_4_), channel_id=1, source_target_pairs={{0,32},{32,0},{1,33},{33,1},{2,34},{34,2},{3,35},{35,3},{4,36},{36... | collective-permute-start | bytes 2359304 | tf_op jit(solution)/shard_map/ppermute | solution.py:19
  55.2 13.2 %collective-permute-start.11 = (bf16[32,6144]{1,0:T(8,128)(2,1)S(1)}, bf16[32,6144]{1,0:T(8,128)(2,1)S(1)}, u32[]{:S(2)}, u32[]{:S(2)}) collective-permute-start(bf16[32,6144]{1,0:T(8,128)(2,1)S(1)} %slice.22), channel_id=1, source_target_pairs={{0,64},{64,128},{128,192},{192,0},{1,65},{65,129},{129,193},{193,1... | collective-permute-start | bytes 1179656 | tf_op jit(solution)/shard_map/ppermute | solution.py:19
  56.9 11.4 %collective-permute-start.12 = (bf16[32,6144]{1,0:T(8,128)(2,1)S(1)}, bf16[32,6144]{1,0:T(8,128)(2,1)S(1)}, u32[]{:S(2)}, u32[]{:S(2)}) collective-permute-start(bf16[32,6144]{1,0:T(8,128)(2,1)S(1)} %slice.23), channel_id=1, source_target_pairs={{0,192},{64,0},{128,64},{192,128},{1,193},{65,1},{129,65},{193,129... | collective-permute-start | bytes 1179656 | tf_op jit(solution)/shard_map/ppermute | solution.py:19
  57.2 22.9 %collective-permute-start.20 = (s16[128,1664]{1,0:T(8,128)(2,1)S(1)}, s16[128,1664]{1,0:T(8,128)(2,1)S(1)}, u32[]{:S(2)}, u32[]{:S(2)}) collective-permute-start(s16[128,1664]{1,0:T(8,128)(2,1)S(1)} %get-tuple-element.77), channel_id=1, source_target_pairs={{0,16},{8,24},{16,0},{24,8},{1,17},{9,25},{17,1},{25,9},{2,18},{10... | collective-permute-start | bytes 1277960 | tf_op jit(solution)/shard_map/ppermute | solution.py:19
  68.3 3.8 %collective-permute-start.15 = (bf16[32,6144]{1,0:T(8,128)(2,1)S(1)}, bf16[32,6144]{1,0:T(8,128)(2,1)S(1)}, u32[]{:S(2)}, u32[]{:S(2)}) collective-permute-start(bf16[32,6144]{1,0:T(8,128)(2,1)S(1)} %collective-permute-done.11.refs_3_), channel_id=1, source_target_pairs={{0,32},{32,0},{1,33},{33,1},{2,34},{34,2},{3,35},{35,3},{4,36},{36... | collective-permute-start | bytes 1179656 | tf_op jit(solution)/shard_map/ppermute | solution.py:19
  68.4 3.7 %collective-permute-start.16 = (bf16[32,6144]{1,0:T(8,128)(2,1)S(1)}, bf16[32,6144]{1,0:T(8,128)(2,1)S(1)}, u32[]{:S(2)}, u32[]{:S(2)}) collective-permute-start(bf16[32,6144]{1,0:T(8,128)(2,1)S(1)} %collective-permute-done.12.refs_4_), channel_id=1, source_target_pairs={{0,32},{32,0},{1,33},{33,1},{2,34},{34,2},{3,35},{35,3},{4,36},{36... | collective-permute-start | bytes 1179656 | tf_op jit(solution)/shard_map/ppermute | solution.py:19
  68.9 14.3 %collective-permute-start.21 = (s16[128,1664]{1,0:T(8,128)(2,1)S(1)}, s16[128,1664]{1,0:T(8,128)(2,1)S(1)}, u32[]{:S(2)}, u32[]{:S(2)}) collective-permute-start(s16[128,1664]{1,0:T(8,128)(2,1)S(1)} %get-tuple-element.76), channel_id=1, source_target_pairs={{0,8},{8,16},{16,24},{24,0},{1,9},{9,17},{17,25},{25,1},{2,10},{10... | collective-permute-start | bytes 1277960 | tf_op jit(solution)/shard_map/ppermute | solution.py:19
  69.6 21.8 %collective-permute-start.22 = (s16[128,1664]{1,0:T(8,128)(2,1)S(1)}, s16[128,1664]{1,0:T(8,128)(2,1)S(1)}, u32[]{:S(2)}, u32[]{:S(2)}) collective-permute-start(s16[128,1664]{1,0:T(8,128)(2,1)S(1)} %get-tuple-element.78), channel_id=1, source_target_pairs={{0,24},{8,0},{16,8},{24,16},{1,25},{9,1},{17,9},{25,17},{2,26},{10... | collective-permute-start | bytes 1277960 | tf_op jit(solution)/shard_map/ppermute | solution.py:19
  79.1 25.1 %collective-permute-start.17 = (s16[128,1664]{1,0:T(8,128)(2,1)S(1)}, s16[128,1664]{1,0:T(8,128)(2,1)S(1)}, u32[]{:S(2)}, u32[]{:S(2)}) collective-permute-start(s16[128,1664]{1,0:T(8,128)(2,1)S(1)} %get-tuple-element.98), channel_id=1, source_target_pairs={{0,16},{8,24},{16,0},{24,8},{1,17},{9,25},{17,1},{25,9},{2,18},{10... | collective-permute-start | bytes 1277960 | tf_op jit(solution)/shard_map/ppermute | solution.py:19
  80.0 31.8 %collective-permute-start.18 = (s16[128,1664]{1,0:T(8,128)(2,1)S(1)}, s16[128,1664]{1,0:T(8,128)(2,1)S(1)}, u32[]{:S(2)}, u32[]{:S(2)}) collective-permute-start(s16[128,1664]{1,0:T(8,128)(2,1)S(1)} %get-tuple-element.99), channel_id=1, source_target_pairs={{0,8},{8,16},{16,24},{24,0},{1,9},{9,17},{17,25},{25,1},{2,10},{10... | collective-permute-start | bytes 1277960 | tf_op jit(solution)/shard_map/ppermute | solution.py:19
  80.1 31.7 %collective-permute-start.19 = (s16[128,1664]{1,0:T(8,128)(2,1)S(1)}, s16[128,1664]{1,0:T(8,128)(2,1)S(1)}, u32[]{:S(2)}, u32[]{:S(2)}) collective-permute-start(s16[128,1664]{1,0:T(8,128)(2,1)S(1)} %get-tuple-element.100), channel_id=1, source_target_pairs={{0,24},{8,0},{16,8},{24,16},{1,25},{9,1},{17,9},{25,17},{2,26},{10... | collective-permute-start | bytes 1277960 | tf_op jit(solution)/shard_map/ppermute | solution.py:19
  93.8 22.6 %collective-permute-start.23 = (s16[32,1664]{1,0:T(8,128)(2,1)S(1)}, s16[32,1664]{1,0:T(8,128)(2,1)S(1)}, u32[]{:S(2)}, u32[]{:S(2)}) collective-permute-start(s16[32,1664]{1,0:T(8,128)(2,1)S(1)} %get-tuple-element.107), channel_id=1, source_target_pairs={{0,4},{1,5},{4,0},{5,1},{8,12},{9,13},{12,8},{13,9},{16,20},{17,21... | collective-permute-start | bytes 319496 | tf_op jit(solution)/shard_map/ppermute | solution.py:24
  102.9 14.2 %collective-permute-start.24 = (s16[32,1664]{1,0:T(8,128)(2,1)S(1)}, s16[32,1664]{1,0:T(8,128)(2,1)S(1)}, u32[]{:S(2)}, u32[]{:S(2)}) collective-permute-start(s16[32,1664]{1,0:T(8,128)(2,1)S(1)} %get-tuple-element.108), channel_id=1, source_target_pairs={{1,4},{2,5},{5,0},{6,1},{9,12},{10,13},{13,8},{14,9},{17,20},{18,2... | collective-permute-start | bytes 319496 | tf_op jit(solution)/shard_map/ppermute | solution.py:24
  104.2 21.8 %collective-permute-start.25 = (s16[32,1664]{1,0:T(8,128)(2,1)S(1)}, s16[32,1664]{1,0:T(8,128)(2,1)S(1)}, u32[]{:S(2)}, u32[]{:S(2)}) collective-permute-start(s16[32,1664]{1,0:T(8,128)(2,1)S(1)} %get-tuple-element.109), channel_id=1, source_target_pairs={{0,5},{3,0},{4,1},{7,4},{8,13},{11,8},{12,9},{15,12},{16,21},{19,1... | collective-permute-start | bytes 319496 | tf_op jit(solution)/shard_map/ppermute | solution.py:24
  114.4 11.6 %collective-permute-start.26 = (s16[32,1664]{1,0:T(8,128)(2,1)S(1)}, s16[32,1664]{1,0:T(8,128)(2,1)S(1)}, u32[]{:S(2)}, u32[]{:S(2)}) collective-permute-start(s16[32,1664]{1,0:T(8,128)(2,1)S(1)} %get-tuple-element.110), channel_id=1, source_target_pairs={{2,6},{3,7},{6,2},{7,3},{10,14},{11,15},{14,10},{15,11},{18,22},{1... | collective-permute-start | bytes 319496 | tf_op jit(solution)/shard_map/ppermute | solution.py:24
  115.0 11.0 %collective-permute-start.27 = (s16[32,1664]{1,0:T(8,128)(2,1)S(1)}, s16[32,1664]{1,0:T(8,128)(2,1)S(1)}, u32[]{:S(2)}, u32[]{:S(2)}) collective-permute-start(s16[32,1664]{1,0:T(8,128)(2,1)S(1)} %get-tuple-element.111), channel_id=1, source_target_pairs={{0,3},{3,6},{4,7},{7,2},{8,11},{11,14},{12,15},{15,10},{16,19},{19... | collective-permute-start | bytes 319496 | tf_op jit(solution)/shard_map/ppermute | solution.py:24
  116.5 12.9 %collective-permute-start.28 = (s16[32,1664]{1,0:T(8,128)(2,1)S(1)}, s16[32,1664]{1,0:T(8,128)(2,1)S(1)}, u32[]{:S(2)}, u32[]{:S(2)}) collective-permute-start(s16[32,1664]{1,0:T(8,128)(2,1)S(1)} %get-tuple-element.112), channel_id=1, source_target_pairs={{1,6},{2,7},{5,2},{6,3},{9,14},{10,15},{13,10},{14,11},{17,22},{18... | collective-permute-start | bytes 319496 | tf_op jit(solution)/shard_map/ppermute | solution.py:24
  117.1 12.2 %collective-permute-start.29 = (s16[32,1664]{1,0:T(8,128)(2,1)S(1)}, s16[32,1664]{1,0:T(8,128)(2,1)S(1)}, u32[]{:S(2)}, u32[]{:S(2)}) collective-permute-start(s16[32,1664]{1,0:T(8,128)(2,1)S(1)} %get-tuple-element.113), channel_id=1, source_target_pairs={{0,2},{1,3},{2,4},{3,5},{4,6},{5,7},{6,0},{7,1},{8,10},{9,11},{10,... | collective-permute-start | bytes 319496 | tf_op jit(solution)/shard_map/ppermute | solution.py:19
  126.0 5.7 %collective-permute-start.30 = (s16[32,1664]{1,0:T(8,128)(2,1)S(1)}, s16[32,1664]{1,0:T(8,128)(2,1)S(1)}, u32[]{:S(2)}, u32[]{:S(2)}) collective-permute-start(s16[32,1664]{1,0:T(8,128)(2,1)S(1)} %get-tuple-element.114), channel_id=1, source_target_pairs={{0,6},{1,7},{2,0},{3,1},{4,2},{5,3},{6,4},{7,5},{8,14},{9,15},{10,... | collective-permute-start | bytes 319496 | tf_op jit(solution)/shard_map/ppermute | solution.py:19
  126.0 6.0 %collective-permute-start.31 = (s16[32,1664]{1,0:T(8,128)(2,1)S(1)}, s16[32,1664]{1,0:T(8,128)(2,1)S(1)}, u32[]{:S(2)}, u32[]{:S(2)}) collective-permute-start(s16[32,1664]{1,0:T(8,128)(2,1)S(1)} %get-tuple-element.115), channel_id=1, source_target_pairs={{0,1},{1,2},{2,3},{3,4},{4,5},{5,6},{6,7},{7,0},{8,9},{9,10},{10,1... | collective-permute-start | bytes 319496 | tf_op jit(solution)/shard_map/ppermute | solution.py:19
  126.1 6.7 %collective-permute-start.32 = (s16[32,1664]{1,0:T(8,128)(2,1)S(1)}, s16[32,1664]{1,0:T(8,128)(2,1)S(1)}, u32[]{:S(2)}, u32[]{:S(2)}) collective-permute-start(s16[32,1664]{1,0:T(8,128)(2,1)S(1)} %get-tuple-element.116), channel_id=1, source_target_pairs={{0,7},{1,0},{2,1},{3,2},{4,3},{5,4},{6,5},{7,6},{8,15},{9,8},{10,9... | collective-permute-start | bytes 319496 | tf_op jit(solution)/shard_map/ppermute | solution.py:19

commit v8 on v6

--- a/solution.py
+++ b/solution.py
@@ -296,7 +296,7 @@
     met_2 = along_x(coded_2)
 
     sums = add_second(pos, met_2, add_first(after(met_1, coded_2)))
-    return add_last([sums[0]] + [shift(sums[s], "z", NZ, s) for s in (4, 3, 5, 2, 6, 1, 7)])
+    return add_last([sums[0]] + [shift(sums[s], "z", NZ, s) for s in (4, 1, 3, 5, 2, 6, 7)])
 
 
 def solution(mesh):

time: 134 us -> 134 us (level)
  no operation moved by 1% of the time
where the time goes in v8:
time: 134 us; the launch traced here: 132 us
  Pallas kernels  49.7 us (37%)
  starting transfers between devices  38.4 us (29%)
  waiting for transfers between devices  37.3 us (28%)
  local copies, waits for them, and re-layouts  6.03 us (4%)
    pallas_call x5, Pallas kernels, contract(): pl.pallas_call(body, out_shape=[jax.ShapeDtypeStruct((NC * h, width + TIL...  43.9 us
    ppermute x30, starting transfers between devices, shift(): lax.ppermute(value, axis, [(i, (i + step) % size) for i in range(size)])  38.4 us
    ppermute x30, waiting for transfers between devices, shift(): lax.ppermute(value, axis, [(i, (i + step) % size) for i in range(size)])  37.3 us
    unnamed x9, local copies, waits for them, and re-layouts  3.69 us
  transfers between devices with their start and end apart: 30, of which 15 were waited for; matrix products, arithmetic and copies ran while one was open for 2% of the time, Pallas kernels for 35%

profile of v8, /device:TPU:8, one launch (start us, length us, event | category | flops | bytes accessed | tf_op | source)
XLA Modules:
  0.0 131.8 jit_solution(15386780628560064500)
XLA Ops:
  0.0 2.2 %slice.19 = bf16[64,6144]{1,0:T(8,128)(2,1)} slice(bf16[128,6144]{1,0:T(8,128)(2,1)} %refs_3_.1), slice={[0:64], [0:6144]} | slice | bytes 1572864 | tf_op jit(solution)/shard_map/slice | solution.py:258
  2.2 1.6 %collective-permute-start.1 = (bf16[64,6144]{1,0:T(8,128)(2,1)}, bf16[64,6144]{1,0:T(8,128)(2,1)S(1)}, u32[]{:S(2)}, u32[]{:S(2)}) collective-permute-start(bf16[64,6144]{1,0:T(8,128)(2,1)} %slice.19), channel_id=1, source_target_pairs={{0,64},{64,128},{128,192},{192,0},{1,65},{65,129},{129,193},{193,1... | collective-permute-start | bytes 2359304 | tf_op jit(solution)/shard_map/ppermute | solution.py:17
  3.8 0.6 collective-permute-start.2
  4.5 3.7 %copy-done = bf16[12,1,24,128,128]{4,3,2,1,0:T(8,128)(2,1)S(1)} copy-done((bf16[12,1,24,128,128]{4,3,2,1,0:T(8,128)(2,1)S(1)}, bf16[12,1,24,128,128]{4,3,2,1,0:T(8,128)(2,1)}, u32[]{:S(2)}) %copy-start) | copy-done | bytes 9437208
  8.2 11.0 %shard_map.37 = (s16[128,1664]{1,0:T(8,128)(2,1)S(1)}, s16[128,1664]{1,0:T(8,128)(2,1)S(1)}, s16[128,1664]{1,0:T(8,128)(2,1)S(1)}, s16[128,1664]{1,0:T(8,128)(2,...) custom-call(s32[4]{0:T(128)S(1)} %pad_add_fusion.refs_0_.pos_ref, ...), custom_call_target="tpu_custom_call" | custom-call | flops 1 | bytes 1 | tf_op jit(solution)/shard_map/pallas_call | solution.py:103
  19.2 3.5 %collective-permute-done.1.refs_3_ = bf16[64,6144]{1,0:T(8,128)(2,1)S(1)} collective-permute-done((bf16[64,6144]{1,0:T(8,128)(2,1)}, bf16[64,6144]{1,0:T(8,128)(2,1)S(1)}, u32[]{:S(2)}, u32[]{:S(2)}) %collective-permute-start.1) | collective-permute-done | bytes 786464 | tf_op jit(solution)/shard_map/ppermute | solution.py:17
  22.7 0.9 collective-permute-done.2.refs_4_
  23.5 0.5 collective-permute-start.4
  24.1 1.6 %collective-permute-start.7 = (bf16[32,6144]{1,0:T(8,128)(2,1)S(1)}, bf16[32,6144]{1,0:T(8,128)(2,1)S(1)}, u32[]{:S(2)}, u32[]{:S(2)}) collective-permute-start(bf16[32,6144]{1,0:T(8,128)(2,1)S(1)} %slice.20), channel_id=1, source_target_pairs={{0,64},{64,128},{128,192},{192,0},{1,65},{65,129},{129,193},{193,1... | collective-permute-start | bytes 1179656 | tf_op jit(solution)/shard_map/ppermute | solution.py:17
  25.7 0.7 collective-permute-start.8
  26.4 0.5 collective-permute-done.4.refs_6_
  26.9 1.9 %collective-permute-start.5 = (bf16[64,6144]{1,0:T(8,128)(2,1)S(1)}, bf16[64,6144]{1,0:T(8,128)(2,1)S(1)}, u32[]{:S(2)}, u32[]{:S(2)}) collective-permute-start(bf16[64,6144]{1,0:T(8,128)(2,1)S(1)} %slice.18), channel_id=1, source_target_pairs={{0,64},{64,128},{128,192},{192,0},{1,65},{65,129},{129,193},{193,1... | collective-permute-start | bytes 2359304 | tf_op jit(solution)/shard_map/ppermute | solution.py:17
  28.8 1.0 collective-permute-start.6
  29.8 9.5 %shard_map.38 = (s16[128,1664]{1,0:T(8,128)(2,1)S(1)}, s16[128,1664]{1,0:T(8,128)(2,1)S(1)}, s16[128,1664]{1,0:T(8,128)(2,1)S(1)}, s16[128,1664]{1,0:T(8,128)(2,1)S(1)}) custom-call(s32[4]{0:T(128)S(1)} %pad_add_fusion.refs_0_.pos_ref, s32[12,24]{1,0:T(8,128)S(1)} %bitcast.14, ...), custom_call_target="tpu_custom_call", output_to_operand_aliasing={{0}: (7, {}), {1}: (8, {}), {2}: (9, {}), {3}: (10, {})} | custom-call | flops 1 | bytes 1 | tf_op jit(solution)/shard_map/pallas_call | solution.py:103
  39.4 0.5 collective-permute-start.9
  39.9 1.2 collective-permute-done.10.refs_6_
  41.1 0.6 collective-permute-done.9.refs_5_
  41.7 6.9 %shard_map.39 = (s16[128,1664]{1,0:T(8,128)(2,1)S(1)}, s16[128,1664]{1,0:T(8,128)(2,1)S(1)}, s16[128,1664]{1,0:T(8,128)(2,1)S(1)}, s16[128,1664]{1,0:T(8,128)(2,1)S(1)}) custom-call(s32[4]{0:T(128)S(1)} %pad_add_fusion.refs_0_.pos_ref, s32[12,24]{1,0:T(8,128)S(1)} %bitcast.15, ...), custom_call_target="tpu_custom_call", output_to_operand_aliasing={{0}: (7, {}), {1}: (8, {}), {2}: (9, {}), {3}: (10, {})} | custom-call | flops 1 | bytes 1 | tf_op jit(solution)/shard_map/pallas_call | solution.py:103
  48.6 3.8 %collective-permute-done.5.refs_3_ = bf16[64,6144]{1,0:T(8,128)(2,1)S(1)} collective-permute-done((bf16[64,6144]{1,0:T(8,128)(2,1)S(1)}, bf16[64,6144]{1,0:T(8,128)(2,1)S(1)}, u32[]{:S(2)}, u32[]{:S(2)}) %collective-permute-start.5) | collective-permute-done | bytes 786464 | tf_op jit(solution)/shard_map/ppermute | solution.py:17
  52.4 2.1 %collective-permute-done.6.refs_4_ = bf16[64,6144]{1,0:T(8,128)(2,1)S(1)} collective-permute-done((bf16[64,6144]{1,0:T(8,128)(2,1)S(1)}, bf16[64,6144]{1,0:T(8,128)(2,1)S(1)}, u32[]{:S(2)}, u32[]{:S(2)}) %collective-permute-start.6) | collective-permute-done | bytes 786464 | tf_op jit(solution)/shard_map/ppermute | solution.py:17
  54.6 0.5 collective-permute-start.14
  55.1 1.7 %collective-permute-start.11 = (bf16[32,6144]{1,0:T(8,128)(2,1)S(1)}, bf16[32,6144]{1,0:T(8,128)(2,1)S(1)}, u32[]{:S(2)}, u32[]{:S(2)}) collective-permute-start(bf16[32,6144]{1,0:T(8,128)(2,1)S(1)} %slice.22), channel_id=1, source_target_pairs={{0,64},{64,128},{128,192},{192,0},{1,65},{65,129},{129,193},{193,1... | collective-permute-start | bytes 1179656 | tf_op jit(solution)/shard_map/ppermute | solution.py:17
  56.9 0.3 collective-permute-start.12
  57.2 1.6 %collective-permute-start.20 = (s16[128,1664]{1,0:T(8,128)(2,1)S(1)}, s16[128,1664]{1,0:T(8,128)(2,1)S(1)}, u32[]{:S(2)}, u32[]{:S(2)}) collective-permute-start(s16[128,1664]{1,0:T(8,128)(2,1)S(1)} %get-tuple-element.73), channel_id=1, source_target_pairs={{0,16},{8,24},{16,0},{24,8},{1,17},{9,25},{17,1},{25,9},{2,18},{10... | collective-permute-start | bytes 1277960 | tf_op jit(solution)/shard_map/ppermute | solution.py:17
  58.8 9.5 %shard_map.40 = (s16[128,1664]{1,0:T(8,128)(2,1)S(1)}, s16[128,1664]{1,0:T(8,128)(2,1)S(1)}, s16[128,1664]{1,0:T(8,128)(2,1)S(1)}, s16[128,1664]{1,0:T(8,128)(2,1)S(1)}) custom-call(s32[4]{0:T(128)S(1)} %pad_add_fusion.refs_0_.pos_ref, s32[12,24]{1,0:T(8,128)S(1)} %bitcast.16, ...), custom_call_target="tpu_custom_call", output_to_operand_aliasing={{0}: (7, {}), {1}: (8, {}), {2}: (9, {}), {3}: (10, {})} | custom-call | flops 1 | bytes 1 | tf_op jit(solution)/shard_map/pallas_call | solution.py:103
  68.4 0.5 collective-permute-start.16
  68.9 0.6 collective-permute-start.21
  69.5 2.6 %collective-permute-start.22 = (s16[128,1664]{1,0:T(8,128)(2,1)S(1)}, s16[128,1664]{1,0:T(8,128)(2,1)S(1)}, u32[]{:S(2)}, u32[]{:S(2)}) collective-permute-start(s16[128,1664]{1,0:T(8,128)(2,1)S(1)} %get-tuple-element.74), channel_id=1, source_target_pairs={{0,24},{8,0},{16,8},{24,16},{1,25},{9,1},{17,9},{25,17},{2,26},{10... | collective-permute-start | bytes 1277960 | tf_op jit(solution)/shard_map/ppermute | solution.py:17
  72.2 6.9 %shard_map.41 = (s16[128,1664]{1,0:T(8,128)(2,1)S(1)}, s16[128,1664]{1,0:T(8,128)(2,1)S(1)}, s16[128,1664]{1,0:T(8,128)(2,1)S(1)}, s16[128,1664]{1,0:T(8,128)(2,1)S(1)}) custom-call(s32[4]{0:T(128)S(1)} %pad_add_fusion.refs_0_.pos_ref, s32[12,24]{1,0:T(8,128)S(1)} %bitcast.17, ...), custom_call_target="tpu_custom_call", output_to_operand_aliasing={{0}: (7, {}), {1}: (8, {}), {2}: (9, {}), {3}: (10, {})} | custom-call | flops 1 | bytes 1 | tf_op jit(solution)/shard_map/pallas_call | solution.py:103
  79.1 0.8 collective-permute-start.17
  80.1 3.0 %collective-permute-start.19 = (s16[128,1664]{1,0:T(8,128)(2,1)S(1)}, s16[128,1664]{1,0:T(8,128)(2,1)S(1)}, u32[]{:S(2)}, u32[]{:S(2)}) collective-permute-start(s16[128,1664]{1,0:T(8,128)(2,1)S(1)} %get-tuple-element.96), channel_id=1, source_target_pairs={{0,24},{8,0},{16,8},{24,16},{1,25},{9,1},{17,9},{25,17},{2,26},{10... | collective-permute-start | bytes 1277960 | tf_op jit(solution)/shard_map/ppermute | solution.py:17
  83.1 8.2 %collective-permute-done.22.refs_3_ = s16[128,1664]{1,0:T(8,128)(2,1)S(1)} collective-permute-done((s16[128,1664]{1,0:T(8,128)(2,1)S(1)}, s16[128,1664]{1,0:T(8,128)(2,1)S(1)}, u32[]{:S(2)}, u32[]{:S(2)}) %collective-permute-start.22) | collective-permute-done | bytes 426016 | tf_op jit(solution)/shard_map/ppermute | solution.py:17
  91.4 1.9 %shard_map.42.refs_4_ = s16[128,1664]{1,0:T(8,128)(2,1)S(1)} custom-call(s16[128,1664]{1,0:T(8,128)(2,1)S(1)} %get-tuple-element.97.refs_0_, s16[128,1664]{1,0:T(8,128)(2,1)S(1)} %collective-permute-done.20.refs_1_, s16[128,1664]{1,0:T(8,128)(2,1)S(1)} %collective-permute-done.21.refs_2_, s16[128,1664]{1,0:T(8,128)(2,1)S(1)} %collective-permute-done.22.refs_3_), custom_call_target="tpu_custom_call" | custom-call | tf_op jit(solution)/shard_map/pallas_call | solution.py:162
  93.5 7.7 %collective-permute-done.18.refs_2_ = s16[128,1664]{1,0:T(8,128)(2,1)S(1)} collective-permute-done((s16[128,1664]{1,0:T(8,128)(2,1)S(1)}, s16[128,1664]{1,0:T(8,128)(2,1)S(1)}, u32[]{:S(2)}, u32[]{:S(2)}) %collective-permute-start.18) | collective-permute-done | bytes 426016 | tf_op jit(solution)/shard_map/ppermute | solution.py:17
  101.2 2.5 %shard_map.43 = (s16[32,1664]{1,0:T(8,128)(2,1)S(1)}, s16[32,1664]{1,0:T(8,128)(2,1)S(1)}, s16[32,1664]{1,0:T(8,128)(2,1)S(1)}, s16[32,1664]{1,0:T(8,128)(2,1)S(...) custom-call(s32[4]{0:T(128)S(1)} %pad_add_fusion.refs_0_.pos_ref, ...), custom_call_target="tpu_custom_call" | custom-call | tf_op jit(solution)/shard_map/pallas_call | solution.py:188
  103.7 7.0 %collective-permute-start.23 = (s16[32,1664]{1,0:T(8,128)(2,1)S(1)}, s16[32,1664]{1,0:T(8,128)(2,1)S(1)}, u32[]{:S(2)}, u32[]{:S(2)}) collective-permute-start(s16[32,1664]{1,0:T(8,128)(2,1)S(1)} %get-tuple-element.102), channel_id=1, source_target_pairs={{0,4},{1,5},{2,6},{3,7},{4,0},{5,1},{6,2},{7,3},{8,12},{9,13},{10,... | collective-permute-start | bytes 319496 | tf_op jit(solution)/shard_map/ppermute | solution.py:17
  110.7 1.1 collective-permute-start.24
  111.8 0.9 collective-permute-start.25
  112.7 4.1 %collective-permute-start.26 = (s16[32,1664]{1,0:T(8,128)(2,1)S(1)}, s16[32,1664]{1,0:T(8,128)(2,1)S(1)}, u32[]{:S(2)}, u32[]{:S(2)}) collective-permute-start(s16[32,1664]{1,0:T(8,128)(2,1)S(1)} %get-tuple-element.105), channel_id=1, source_target_pairs={{0,5},{1,6},{2,7},{3,0},{4,1},{5,2},{6,3},{7,4},{8,13},{9,14},{10,... | collective-permute-start | bytes 319496 | tf_op jit(solution)/shard_map/ppermute | solution.py:17
  116.8 1.4 %collective-permute-start.27 = (s16[32,1664]{1,0:T(8,128)(2,1)S(1)}, s16[32,1664]{1,0:T(8,128)(2,1)S(1)}, u32[]{:S(2)}, u32[]{:S(2)}) collective-permute-start(s16[32,1664]{1,0:T(8,128)(2,1)S(1)} %get-tuple-element.106), channel_id=1, source_target_pairs={{0,2},{1,3},{2,4},{3,5},{4,6},{5,7},{6,0},{7,1},{8,10},{9,11},{10,... | collective-permute-start | bytes 319496 | tf_op jit(solution)/shard_map/ppermute | solution.py:17
  118.3 3.2 %collective-permute-start.28 = (s16[32,1664]{1,0:T(8,128)(2,1)S(1)}, s16[32,1664]{1,0:T(8,128)(2,1)S(1)}, u32[]{:S(2)}, u32[]{:S(2)}) collective-permute-start(s16[32,1664]{1,0:T(8,128)(2,1)S(1)} %get-tuple-element.107), channel_id=1, source_target_pairs={{0,6},{1,7},{2,0},{3,1},{4,2},{5,3},{6,4},{7,5},{8,14},{9,15},{10,... | collective-permute-start | bytes 319496 | tf_op jit(solution)/shard_map/ppermute | solution.py:17
  121.4 0.8 collective-permute-done.24.refs_2_
  122.3 0.3 collective-permute-start.29
  122.5 3.7 %collective-permute-done.25.refs_3_ = s16[32,1664]{1,0:T(8,128)(2,1)S(1)} collective-permute-done((s16[32,1664]{1,0:T(8,128)(2,1)S(1)}, s16[32,1664]{1,0:T(8,128)(2,1)S(1)}, u32[]{:S(2)}, u32[]{:S(2)}) %collective-permute-start.25) | collective-permute-done | bytes 106528 | tf_op jit(solution)/shard_map/ppermute | solution.py:17
  126.3 1.8 %collective-permute-done.27.refs_5_ = s16[32,1664]{1,0:T(8,128)(2,1)S(1)} collective-permute-done((s16[32,1664]{1,0:T(8,128)(2,1)S(1)}, s16[32,1664]{1,0:T(8,128)(2,1)S(1)}, u32[]{:S(2)}, u32[]{:S(2)}) %collective-permute-start.27) | collective-permute-done | bytes 106528 | tf_op jit(solution)/shard_map/ppermute | solution.py:17
  128.0 1.1 collective-permute-done.28.refs_6_
  129.1 1.3 collective-permute-done.29.refs_7_
  130.4 1.4 %shard_map.44 = f32[32,1536]{1,0:T(8,128)} custom-call(s16[32,1664]{1,0:T(8,128)(2,1)S(1)} %get-tuple-element.101.refs_0_, s16[32,1664]{1,0:T(8,128)(2,1)S(1)} %collective-permute-done.23.refs_1_, s16[32,1664]{1,0:T(8,128)(2,1)S(1)} %collective-permute-done.24.refs_2_, s16[32,1664]{1,0:T(8,128)(2,1)S(1)} %collective-permute-done.25.refs_3_, ...), custom_call_target="tpu_custom_call" | custom-call | tf_op jit(solution)/shard_map/pallas_call | solution.py:221
  (36 shorter events, 1.0 us)
Async XLA Ops:
  0.0 4.5 %copy-start.2 = (bf16[128,6144]{1,0:T(8,128)(2,1)S(1)}, bf16[128,6144]{1,0:T(8,128)(2,1)}, u32[]{:S(2)}) copy-start(bf16[128,6144]{1,0:T(8,128)(2,1)} %refs_3_.1) | copy-start | bytes 4718596
  0.0 4.4 %copy-start.3 = (s32[12,1,24]{2,1,0:T(1,128)S(1)}, s32[12,1,24]{2,1,0:T(1,128)}, u32[]{:S(2)}) copy-start(s32[12,1,24]{2,1,0:T(1,128)} %param.5) | copy-start | bytes 3460
  0.0 4.5 %collective-permute-start = (bf16[128,6144]{1,0:T(8,128)(2,1)}, bf16[128,6144]{1,0:T(8,128)(2,1)}, u32[]{:S(2)}, u32[]{:S(2)}) collective-permute-start(bf16[128,6144]{1,0:T(8,128)(2,1)} %refs_3_.1), channel_id=1, source_target_pairs={{0,32},{32,0},{1,33},{33,1},{2,34},{34,2},{3,35},{35,3},{4,36},{36... | collective-permute-start | bytes 4718600 | tf_op jit(solution)/shard_map/ppermute | solution.py:17
  2.2 20.5 %collective-permute-start.1 = (bf16[64,6144]{1,0:T(8,128)(2,1)}, bf16[64,6144]{1,0:T(8,128)(2,1)S(1)}, u32[]{:S(2)}, u32[]{:S(2)}) collective-permute-start(bf16[64,6144]{1,0:T(8,128)(2,1)} %slice.19), channel_id=1, source_target_pairs={{0,64},{64,128},{128,192},{192,0},{1,65},{65,129},{129,193},{193,1... | collective-permute-start | bytes 2359304 | tf_op jit(solution)/shard_map/ppermute | solution.py:17
  3.8 19.7 %collective-permute-start.2 = (bf16[64,6144]{1,0:T(8,128)(2,1)}, bf16[64,6144]{1,0:T(8,128)(2,1)S(1)}, u32[]{:S(2)}, u32[]{:S(2)}) collective-permute-start(bf16[64,6144]{1,0:T(8,128)(2,1)} %slice.19), channel_id=1, source_target_pairs={{0,192},{64,0},{128,64},{192,128},{1,193},{65,1},{129,65},{193,129... | collective-permute-start | bytes 2359304 | tf_op jit(solution)/shard_map/ppermute | solution.py:17
  4.5 3.7 %copy-start = (bf16[12,1,24,128,128]{4,3,2,1,0:T(8,128)(2,1)S(1)}, bf16[12,1,24,128,128]{4,3,2,1,0:T(8,128)(2,1)}, u32[]{:S(2)}) copy-start(bf16[12,1,24,128,128]{4,3,2,1,0:T(8,128)(2,1)} %param.4) | copy-start | bytes 28311556
  8.2 21.6 %copy-start.1 = (bf16[12,1,24,128,128]{4,3,2,1,0:T(8,128)(2,1)S(1)}, bf16[12,1,24,128,128]{4,3,2,1,0:T(8,128)(2,1)}, u32[]{:S(2)}) copy-start(bf16[12,1,24,128,128]{4,3,2,1,0:T(8,128)(2,1)} %param.4) | copy-start | bytes 28311556
  23.5 2.9 %collective-permute-start.3 = (bf16[64,6144]{1,0:T(8,128)(2,1)S(1)}, bf16[64,6144]{1,0:T(8,128)(2,1)S(1)}, u32[]{:S(2)}, u32[]{:S(2)}) collective-permute-start(bf16[64,6144]{1,0:T(8,128)(2,1)S(1)} %collective-permute-done.1.refs_3_), channel_id=1, source_target_pairs={{0,32},{32,0},{1,33},{33,1},{2,34},{34,2},{3,35},{35,3},{4,36},{36... | collective-permute-start | bytes 2359304 | tf_op jit(solution)/shard_map/ppermute | solution.py:17
  23.5 3.4 %collective-permute-start.4 = (bf16[64,6144]{1,0:T(8,128)(2,1)S(1)}, bf16[64,6144]{1,0:T(8,128)(2,1)S(1)}, u32[]{:S(2)}, u32[]{:S(2)}) collective-permute-start(bf16[64,6144]{1,0:T(8,128)(2,1)S(1)} %collective-permute-done.2.refs_4_), channel_id=1, source_target_pairs={{0,32},{32,0},{1,33},{33,1},{2,34},{34,2},{3,35},{35,3},{4,36},{36... | collective-permute-start | bytes 2359304 | tf_op jit(solution)/shard_map/ppermute | solution.py:17
  24.1 15.2 %collective-permute-start.7 = (bf16[32,6144]{1,0:T(8,128)(2,1)S(1)}, bf16[32,6144]{1,0:T(8,128)(2,1)S(1)}, u32[]{:S(2)}, u32[]{:S(2)}) collective-permute-start(bf16[32,6144]{1,0:T(8,128)(2,1)S(1)} %slice.20), channel_id=1, source_target_pairs={{0,64},{64,128},{128,192},{192,0},{1,65},{65,129},{129,193},{193,1... | collective-permute-start | bytes 1179656 | tf_op jit(solution)/shard_map/ppermute | solution.py:17
  25.7 13.6 %collective-permute-start.8 = (bf16[32,6144]{1,0:T(8,128)(2,1)S(1)}, bf16[32,6144]{1,0:T(8,128)(2,1)S(1)}, u32[]{:S(2)}, u32[]{:S(2)}) collective-permute-start(bf16[32,6144]{1,0:T(8,128)(2,1)S(1)} %slice.21), channel_id=1, source_target_pairs={{0,192},{64,0},{128,64},{192,128},{1,193},{65,1},{129,65},{193,129... | collective-permute-start | bytes 1179656 | tf_op jit(solution)/shard_map/ppermute | solution.py:17
  26.9 25.5 %collective-permute-start.5 = (bf16[64,6144]{1,0:T(8,128)(2,1)S(1)}, bf16[64,6144]{1,0:T(8,128)(2,1)S(1)}, u32[]{:S(2)}, u32[]{:S(2)}) collective-permute-start(bf16[64,6144]{1,0:T(8,128)(2,1)S(1)} %slice.18), channel_id=1, source_target_pairs={{0,64},{64,128},{128,192},{192,0},{1,65},{65,129},{129,193},{193,1... | collective-permute-start | bytes 2359304 | tf_op jit(solution)/shard_map/ppermute | solution.py:17
  28.8 25.7 %collective-permute-start.6 = (bf16[64,6144]{1,0:T(8,128)(2,1)S(1)}, bf16[64,6144]{1,0:T(8,128)(2,1)S(1)}, u32[]{:S(2)}, u32[]{:S(2)}) collective-permute-start(bf16[64,6144]{1,0:T(8,128)(2,1)S(1)} %slice.18), channel_id=1, source_target_pairs={{0,192},{64,0},{128,64},{192,128},{1,193},{65,1},{129,65},{193,129... | collective-permute-start | bytes 2359304 | tf_op jit(solution)/shard_map/ppermute | solution.py:17
  39.3 1.8 %collective-permute-start.10 = (bf16[32,6144]{1,0:T(8,128)(2,1)S(1)}, bf16[32,6144]{1,0:T(8,128)(2,1)S(1)}, u32[]{:S(2)}, u32[]{:S(2)}) collective-permute-start(bf16[32,6144]{1,0:T(8,128)(2,1)S(1)} %collective-permute-done.8.refs_4_), channel_id=1, source_target_pairs={{0,32},{32,0},{1,33},{33,1},{2,34},{34,2},{3,35},{35,3},{4,36},{36... | collective-permute-start | bytes 1179656 | tf_op jit(solution)/shard_map/ppermute | solution.py:17
  39.4 2.3 %collective-permute-start.9 = (bf16[32,6144]{1,0:T(8,128)(2,1)S(1)}, bf16[32,6144]{1,0:T(8,128)(2,1)S(1)}, u32[]{:S(2)}, u32[]{:S(2)}) collective-permute-start(bf16[32,6144]{1,0:T(8,128)(2,1)S(1)} %collective-permute-done.7.refs_3_), channel_id=1, source_target_pairs={{0,32},{32,0},{1,33},{33,1},{2,34},{34,2},{3,35},{35,3},{4,36},{36... | collective-permute-start | bytes 1179656 | tf_op jit(solution)/shard_map/ppermute | solution.py:17
  54.5 4.2 %collective-permute-start.13 = (bf16[64,6144]{1,0:T(8,128)(2,1)S(1)}, bf16[64,6144]{1,0:T(8,128)(2,1)S(1)}, u32[]{:S(2)}, u32[]{:S(2)}) collective-permute-start(bf16[64,6144]{1,0:T(8,128)(2,1)S(1)} %collective-permute-done.5.refs_3_), channel_id=1, source_target_pairs={{0,32},{32,0},{1,33},{33,1},{2,34},{34,2},{3,35},{35,3},{4,36},{36... | collective-permute-start | bytes 2359304 | tf_op jit(solution)/shard_map/ppermute | solution.py:17
  54.6 4.1 %collective-permute-start.14 = (bf16[64,6144]{1,0:T(8,128)(2,1)S(1)}, bf16[64,6144]{1,0:T(8,128)(2,1)S(1)}, u32[]{:S(2)}, u32[]{:S(2)}) collective-permute-start(bf16[64,6144]{1,0:T(8,128)(2,1)S(1)} %collective-permute-done.6.refs_4_), channel_id=1, source_target_pairs={{0,32},{32,0},{1,33},{33,1},{2,34},{34,2},{3,35},{35,3},{4,36},{36... | collective-permute-start | bytes 2359304 | tf_op jit(solution)/shard_map/ppermute | solution.py:17
  55.1 13.2 %collective-permute-start.11 = (bf16[32,6144]{1,0:T(8,128)(2,1)S(1)}, bf16[32,6144]{1,0:T(8,128)(2,1)S(1)}, u32[]{:S(2)}, u32[]{:S(2)}) collective-permute-start(bf16[32,6144]{1,0:T(8,128)(2,1)S(1)} %slice.22), channel_id=1, source_target_pairs={{0,64},{64,128},{128,192},{192,0},{1,65},{65,129},{129,193},{193,1... | collective-permute-start | bytes 1179656 | tf_op jit(solution)/shard_map/ppermute | solution.py:17
  56.9 11.4 %collective-permute-start.12 = (bf16[32,6144]{1,0:T(8,128)(2,1)S(1)}, bf16[32,6144]{1,0:T(8,128)(2,1)S(1)}, u32[]{:S(2)}, u32[]{:S(2)}) collective-permute-start(bf16[32,6144]{1,0:T(8,128)(2,1)S(1)} %slice.23), channel_id=1, source_target_pairs={{0,192},{64,0},{128,64},{192,128},{1,193},{65,1},{129,65},{193,129... | collective-permute-start | bytes 1179656 | tf_op jit(solution)/shard_map/ppermute | solution.py:17
  57.2 22.9 %collective-permute-start.20 = (s16[128,1664]{1,0:T(8,128)(2,1)S(1)}, s16[128,1664]{1,0:T(8,128)(2,1)S(1)}, u32[]{:S(2)}, u32[]{:S(2)}) collective-permute-start(s16[128,1664]{1,0:T(8,128)(2,1)S(1)} %get-tuple-element.73), channel_id=1, source_target_pairs={{0,16},{8,24},{16,0},{24,8},{1,17},{9,25},{17,1},{25,9},{2,18},{10... | collective-permute-start | bytes 1277960 | tf_op jit(solution)/shard_map/ppermute | solution.py:17
  68.3 3.8 %collective-permute-start.15 = (bf16[32,6144]{1,0:T(8,128)(2,1)S(1)}, bf16[32,6144]{1,0:T(8,128)(2,1)S(1)}, u32[]{:S(2)}, u32[]{:S(2)}) collective-permute-start(bf16[32,6144]{1,0:T(8,128)(2,1)S(1)} %collective-permute-done.11.refs_3_), channel_id=1, source_target_pairs={{0,32},{32,0},{1,33},{33,1},{2,34},{34,2},{3,35},{35,3},{4,36},{36... | collective-permute-start | bytes 1179656 | tf_op jit(solution)/shard_map/ppermute | solution.py:17
  68.4 3.7 %collective-permute-start.16 = (bf16[32,6144]{1,0:T(8,128)(2,1)S(1)}, bf16[32,6144]{1,0:T(8,128)(2,1)S(1)}, u32[]{:S(2)}, u32[]{:S(2)}) collective-permute-start(bf16[32,6144]{1,0:T(8,128)(2,1)S(1)} %collective-permute-done.12.refs_4_), channel_id=1, source_target_pairs={{0,32},{32,0},{1,33},{33,1},{2,34},{34,2},{3,35},{35,3},{4,36},{36... | collective-permute-start | bytes 1179656 | tf_op jit(solution)/shard_map/ppermute | solution.py:17
  68.9 14.2 %collective-permute-start.21 = (s16[128,1664]{1,0:T(8,128)(2,1)S(1)}, s16[128,1664]{1,0:T(8,128)(2,1)S(1)}, u32[]{:S(2)}, u32[]{:S(2)}) collective-permute-start(s16[128,1664]{1,0:T(8,128)(2,1)S(1)} %get-tuple-element.72), channel_id=1, source_target_pairs={{0,8},{8,16},{16,24},{24,0},{1,9},{9,17},{17,25},{25,1},{2,10},{10... | collective-permute-start | bytes 1277960 | tf_op jit(solution)/shard_map/ppermute | solution.py:17
  69.5 21.8 %collective-permute-start.22 = (s16[128,1664]{1,0:T(8,128)(2,1)S(1)}, s16[128,1664]{1,0:T(8,128)(2,1)S(1)}, u32[]{:S(2)}, u32[]{:S(2)}) collective-permute-start(s16[128,1664]{1,0:T(8,128)(2,1)S(1)} %get-tuple-element.74), channel_id=1, source_target_pairs={{0,24},{8,0},{16,8},{24,16},{1,25},{9,1},{17,9},{25,17},{2,26},{10... | collective-permute-start | bytes 1277960 | tf_op jit(solution)/shard_map/ppermute | solution.py:17
  79.1 14.4 %collective-permute-start.17 = (s16[128,1664]{1,0:T(8,128)(2,1)S(1)}, s16[128,1664]{1,0:T(8,128)(2,1)S(1)}, u32[]{:S(2)}, u32[]{:S(2)}) collective-permute-start(s16[128,1664]{1,0:T(8,128)(2,1)S(1)} %get-tuple-element.94), channel_id=1, source_target_pairs={{0,16},{8,24},{16,0},{24,8},{1,17},{9,25},{17,1},{25,9},{2,18},{10... | collective-permute-start | bytes 1277960 | tf_op jit(solution)/shard_map/ppermute | solution.py:17
  79.9 21.2 %collective-permute-start.18 = (s16[128,1664]{1,0:T(8,128)(2,1)S(1)}, s16[128,1664]{1,0:T(8,128)(2,1)S(1)}, u32[]{:S(2)}, u32[]{:S(2)}) collective-permute-start(s16[128,1664]{1,0:T(8,128)(2,1)S(1)} %get-tuple-element.95), channel_id=1, source_target_pairs={{0,8},{8,16},{16,24},{24,0},{1,9},{9,17},{17,25},{25,1},{2,10},{10... | collective-permute-start | bytes 1277960 | tf_op jit(solution)/shard_map/ppermute | solution.py:17
  80.1 21.1 %collective-permute-start.19 = (s16[128,1664]{1,0:T(8,128)(2,1)S(1)}, s16[128,1664]{1,0:T(8,128)(2,1)S(1)}, u32[]{:S(2)}, u32[]{:S(2)}) collective-permute-start(s16[128,1664]{1,0:T(8,128)(2,1)S(1)} %get-tuple-element.96), channel_id=1, source_target_pairs={{0,24},{8,0},{16,8},{24,16},{1,25},{9,1},{17,9},{25,17},{2,26},{10... | collective-permute-start | bytes 1277960 | tf_op jit(solution)/shard_map/ppermute | solution.py:17
  103.7 14.6 %collective-permute-start.23 = (s16[32,1664]{1,0:T(8,128)(2,1)S(1)}, s16[32,1664]{1,0:T(8,128)(2,1)S(1)}, u32[]{:S(2)}, u32[]{:S(2)}) collective-permute-start(s16[32,1664]{1,0:T(8,128)(2,1)S(1)} %get-tuple-element.102), channel_id=1, source_target_pairs={{0,4},{1,5},{2,6},{3,7},{4,0},{5,1},{6,2},{7,3},{8,12},{9,13},{10,... | collective-permute-start | bytes 319496 | tf_op jit(solution)/shard_map/ppermute | solution.py:17
  110.7 11.6 %collective-permute-start.24 = (s16[32,1664]{1,0:T(8,128)(2,1)S(1)}, s16[32,1664]{1,0:T(8,128)(2,1)S(1)}, u32[]{:S(2)}, u32[]{:S(2)}) collective-permute-start(s16[32,1664]{1,0:T(8,128)(2,1)S(1)} %get-tuple-element.103), channel_id=1, source_target_pairs={{0,1},{1,2},{2,3},{3,4},{4,5},{5,6},{6,7},{7,0},{8,9},{9,10},{10,1... | collective-permute-start | bytes 319496 | tf_op jit(solution)/shard_map/ppermute | solution.py:17
  111.8 14.5 %collective-permute-start.25 = (s16[32,1664]{1,0:T(8,128)(2,1)S(1)}, s16[32,1664]{1,0:T(8,128)(2,1)S(1)}, u32[]{:S(2)}, u32[]{:S(2)}) collective-permute-start(s16[32,1664]{1,0:T(8,128)(2,1)S(1)} %get-tuple-element.104), channel_id=1, source_target_pairs={{0,3},{1,4},{2,5},{3,6},{4,7},{5,0},{6,1},{7,2},{8,11},{9,12},{10,... | collective-permute-start | bytes 319496 | tf_op jit(solution)/shard_map/ppermute | solution.py:17
  112.7 13.6 %collective-permute-start.26 = (s16[32,1664]{1,0:T(8,128)(2,1)S(1)}, s16[32,1664]{1,0:T(8,128)(2,1)S(1)}, u32[]{:S(2)}, u32[]{:S(2)}) collective-permute-start(s16[32,1664]{1,0:T(8,128)(2,1)S(1)} %get-tuple-element.105), channel_id=1, source_target_pairs={{0,5},{1,6},{2,7},{3,0},{4,1},{5,2},{6,3},{7,4},{8,13},{9,14},{10,... | collective-permute-start | bytes 319496 | tf_op jit(solution)/shard_map/ppermute | solution.py:17
  116.8 11.2 %collective-permute-start.27 = (s16[32,1664]{1,0:T(8,128)(2,1)S(1)}, s16[32,1664]{1,0:T(8,128)(2,1)S(1)}, u32[]{:S(2)}, u32[]{:S(2)}) collective-permute-start(s16[32,1664]{1,0:T(8,128)(2,1)S(1)} %get-tuple-element.106), channel_id=1, source_target_pairs={{0,2},{1,3},{2,4},{3,5},{4,6},{5,7},{6,0},{7,1},{8,10},{9,11},{10,... | collective-permute-start | bytes 319496 | tf_op jit(solution)/shard_map/ppermute | solution.py:17
  118.3 10.8 %collective-permute-start.28 = (s16[32,1664]{1,0:T(8,128)(2,1)S(1)}, s16[32,1664]{1,0:T(8,128)(2,1)S(1)}, u32[]{:S(2)}, u32[]{:S(2)}) collective-permute-start(s16[32,1664]{1,0:T(8,128)(2,1)S(1)} %get-tuple-element.107), channel_id=1, source_target_pairs={{0,6},{1,7},{2,0},{3,1},{4,2},{5,3},{6,4},{7,5},{8,14},{9,15},{10,... | collective-permute-start | bytes 319496 | tf_op jit(solution)/shard_map/ppermute | solution.py:17
  122.3 8.1 %collective-permute-start.29 = (s16[32,1664]{1,0:T(8,128)(2,1)S(1)}, s16[32,1664]{1,0:T(8,128)(2,1)S(1)}, u32[]{:S(2)}, u32[]{:S(2)}) collective-permute-start(s16[32,1664]{1,0:T(8,128)(2,1)S(1)} %get-tuple-element.108), channel_id=1, source_target_pairs={{0,7},{1,0},{2,1},{3,2},{4,3},{5,4},{6,5},{7,6},{8,15},{9,8},{10,9... | collective-permute-start | bytes 319496 | tf_op jit(solution)/shard_map/ppermute | solution.py:17
